TPU v7x, 256 devices: a whole 4x4x8 slice. The times are simulated.
256 devices in a mesh: dp: 128 (over y, z, x), blk: 2 (over core).
Axes of the slice: x: 4, y: 4, z: 8, core: 2. Of those that a mesh axis runs over, the one named last changes fastest.
Arguments:
- vectors: float32 [131072, 96], P('dp'), may hold values from -16 to 16
- codes: int32 [131072, 8], P('dp'), may hold values from 0 to 255, as said below
- weights: bfloat16 [131072], P('dp'), may hold values from 0.25 to 4
- ridge: float32 [1], replicated, may hold values from 0.1 to 0.5
Outputs:
- codebooks: float32 [8, 256, 96], replicated
- residual: float32 [131072, 96], P('dp')
- distortion: float32 [], replicated
Inputs may be any that keep to these rules, and one draw needn't show every extreme that they name: `codes`: 8 codebook indices per vector.
All inputs are finite; a program needn't handle non-finite values.
Results may differ from a plain program's by a relative error of at most 0.0003.
Values sent between devices are 32-bit elements; how exact they have to be, the bound alone decides.
No kernel may reach another device: no remote copies, remote signals or barrier semaphores. Data moves between devices by JAX's collectives and lax.ppermute only.
A program may use at most 128 MiB of HBM per device.

v0:
```python
import jax
import jax.numpy as jnp
from jax import lax
from jax.sharding import Mesh
from jax.sharding import PartitionSpec as P

K = 256
M = 8
ITERS = 8
DP = ("dp_0", "dp_1", "dp_2")


HIGH = lax.Precision.HIGHEST


def in_one(arrays, axis):
    ends = [0]
    for a in arrays:
        ends.append(ends[-1] + a.size)
    running = lax.psum(jnp.concatenate([a.ravel() for a in arrays]), axis)
    return tuple((running[b:e].reshape(a.shape) for a, b, e in zip(arrays, ends, ends[1:])))


def partner_2(array, axis, bit):
    return lax.ppermute(array, axis, [(i, i ^ 1 << bit) for i in range(lax.axis_size(axis))])


def sent_together(arrays, axis, dim, along):
    columns = [a.reshape(*a.shape[:along], -1) for a in arrays]
    both = jnp.concatenate(columns, axis=along)
    filled, at, gathered = (lax.all_gather(both, axis, axis=dim, tiled=True), 0, [])
    for a, column in zip(arrays, columns):
        slab = filled[..., at : at + column.shape[along]]
        gathered.append(slab.reshape(*slab.shape[:along], *a.shape[along:]))
        at += column.shape[along]
    return tuple(gathered)


def by_axis(array, axes):
    for axis in axes:
        array = lax.psum(array, axis)
    return array


def pair_books(half):
    local = jnp.array([0, 0, 0, 1, 1, 1, 2, 2, 2, 3, 3, 3], jnp.int32)
    spread = jnp.array([1, 2, 3, 1, 2, 3, 1, 2, 3, 1, 2, 3], jnp.int32)
    near_first = local + 4 * half
    near_second = (near_first + spread) % 8
    far_first = jnp.array([0, 1], jnp.int32) + 2 * half
    firsts = jnp.concatenate([near_first, far_first])
    seconds = jnp.concatenate([near_second, far_first + 4])
    return (firsts, seconds)


def body(vectors, codes, weights, ridge):
    rows = vectors.shape[0]
    width = vectors.shape[1]
    half = lax.axis_index("blk")
    firsts, seconds = pair_books(half)
    npairs = firsts.shape[0]
    levels = lax.iota(jnp.int32, K)
    step_rows = min(512, rows)

    def accumulate(turn, carry):
        joint, right_part, count_part = carry
        start = turn * step_rows
        block_codes = lax.dynamic_slice_in_dim(codes, start, step_rows, 0)
        block_vectors = lax.dynamic_slice_in_dim(vectors, start, step_rows, 0)
        block_mass = lax.dynamic_slice_in_dim(weights, start, step_rows, 0)
        hot = (block_codes.T[:, :, None] == levels[None, None, :]).astype(jnp.bfloat16)
        first_hot = jnp.take(hot, firsts, axis=0) * block_mass[None, :, None]
        second_hot = jnp.take(hot, seconds, axis=0)
        joint = joint + jnp.einsum(
            "krc,kre->kce", first_hot, second_hot, preferred_element_type=jnp.float32
        )
        owned = lax.dynamic_slice_in_dim(hot, 4 * half, 4, 0).astype(jnp.float32)
        owned = owned * block_mass.astype(jnp.float32)[None, :, None]
        right_part = right_part + jnp.einsum("mrk,rd->mkd", owned, block_vectors, precision=HIGH)
        count_part = count_part + jnp.sum(owned, axis=1)
        return (joint, right_part, count_part)

    start_carry = (
        jnp.zeros((npairs, K, K), jnp.float32),
        jnp.zeros((4, K, width), jnp.float32),
        jnp.zeros((4, K), jnp.float32),
    )
    joint, right_part, count_part = lax.fori_loop(0, rows // step_rows, accumulate, start_carry)
    books = lax.iota(jnp.int32, M)
    pick_first = (firsts[:, None] == books[None, :]).astype(jnp.float32)
    pick_second = (seconds[:, None] == books[None, :]).astype(jnp.float32)
    joint, right_part, count_part = in_one((joint, right_part, count_part), DP)
    right_all, count_all = sent_together((right_part, count_part), "blk", 0, 2)
    total_mass = jnp.sum(count_all[0])
    lam = ridge[0] * total_mass / K
    precond = (count_all + lam)[:, :, None]
    solution = jnp.zeros((M, K, width), jnp.float32)
    remain = right_all
    scaled = remain / precond
    direction = scaled
    inner = jnp.sum(remain * scaled, axis=(0, 1))
    for step in range(ITERS):
        at_second = jnp.einsum("km,mcd->kcd", pick_second, direction, precision=HIGH)
        at_first = jnp.einsum("km,mcd->kcd", pick_first, direction, precision=HIGH)
        forward = jnp.einsum("kce,ked->kcd", joint, at_second, precision=HIGH)
        backward = jnp.einsum("kce,kcd->ked", joint, at_first, precision=HIGH)
        part = jnp.einsum("km,kcd->mcd", pick_first, forward, precision=HIGH)
        part = part + jnp.einsum("km,ked->med", pick_second, backward, precision=HIGH)
        partner = partner_2(part, "blk", 0)
        image = part + partner + precond * direction
        alpha = inner / jnp.sum(direction * image, axis=(0, 1))
        solution = solution + alpha * direction
        remain = remain - alpha * image
        scaled = remain / precond
        fresh = jnp.sum(remain * scaled, axis=(0, 1))
        direction = scaled + fresh / inner * direction
        inner = fresh
    recon = jnp.zeros_like(vectors)
    for book in range(M):
        recon = recon + jnp.take(solution[book], codes[:, book], axis=0)
    residual = vectors - recon
    mass = weights.astype(jnp.float32)
    total = by_axis(jnp.sum(mass[:, None] * residual * residual), DP)
    distortion = total / (total_mass * width)
    return (solution, residual, distortion)


def solution(mesh):
    finer = Mesh(mesh.devices.reshape(4, 8, 4, mesh.shape["blk"]), ("dp_0", "dp_1", "dp_2", "blk"))
    placed = (P(DP, None), P(DP, None), P(DP), P())
    return jax.shard_map(
        body, mesh=finer, in_specs=placed, out_specs=(P(), P(DP, None), P()), check_vma=False
    )
```

profile of v0, /device:TPU:2, one launch (start us, length us, event | category | flops | bytes accessed | tf_op | source)
XLA Modules:
  0.0 532.6 jit_solution(17953652379254644061)
XLA Ops:
  8.1 34.0 %while.20 = (s32[]{:T(128)}, f32[14,256,256]{2,1,0:T(8,128)}, f32[4,256,96]{1,2,0:T(8,128)S(1)}, f32[4,256]{1,0:T(4,128)S(1)}, s32[1024,8]{0,1:T(8,128)}, /*inde...) while((s32[]{:T(128)}, f32[14,256,256]{2,1,0:T(8,128)}, ...), condition=%wide.region_2.4_spmd.clone, body=%wide.region_0.3_spmd.clone.sunk | while | flops 1555762944 | bytes 36194140 | solution.py:88
  17.7 6.8 %select_add_fusion.11 = f32[14,256,256]{2,1,0:T(8,128)} fusion(f32[14,256,256]{2,1,0:T(8,128)} %get-tuple-element.474, pred[]{:T(512)S(6)} %compare.4, bf16[14,512,256]{2,1,0:T(8,128)(2,1)} %gather_fusion, pred[14]{0:T(512)(128)(4,1)S(1)} %get-tuple-element.454, bf16[14,512,256]{2,1,0:T(8,128)(2,1)} %gather_fusion.1, ...), kind=kOutput, calls=%fused_computation.16.clone.1 | convolution fusion | flops 946864128 | bytes 14681117 | tf_op jit(solution)/shard_map/while/body/eval_jaxpr/krc,kre->kce/dot_general | solution.py:74
  34.2 7.9 %select_add_fusion.11 = f32[14,256,256]{2,1,0:T(8,128)} fusion(f32[14,256,256]{2,1,0:T(8,128)} %get-tuple-element.474, pred[]{:T(512)S(6)} %compare.4, bf16[14,512,256]{2,1,0:T(8,128)(2,1)} %gather_fusion, pred[14]{0:T(512)(128)(4,1)S(1)} %get-tuple-element.454, bf16[14,512,256]{2,1,0:T(8,128)(2,1)} %gather_fusion.1, ...), kind=kOutput, calls=%fused_computation.16.clone.1 | convolution fusion | flops 946864128 | bytes 14681117 | tf_op jit(solution)/shard_map/while/body/eval_jaxpr/krc,kre->kce/dot_general | solution.py:74
  42.1 5.7 %copy.142 = f32[448,2,8,128]{3,1,2,0:T(2,128)} copy(f32[448,2,8,128]{3,2,1,0:T(8,128)} %bitcast.134) | data formatting | bytes 7340032
  48.3 4.2 pad_maximum_fusion
  53.2 237.3 %all-reduce.2.cloned.1.call-done = f32[1016832]{0:T(1024)} async-done(((f32[1016832]{0:T(1024)}), f32[1016832]{0:T(1024)}) %all-reduce.2.cloned.1.call-update) | async-done | bytes 4067344 | tf_op jit(solution)/shard_map/psum | solution.py:20
  302.0 5.2 reshape.128
  307.2 5.3 fusion.80
  313.9 4.4 fusion.82
  331.6 4.4 fusion.78
  348.7 4.4 fusion.74
  366.0 4.4 fusion.70
  383.1 4.4 fusion.66
  404.8 4.4 fusion.62
  421.9 4.4 fusion.58
  439.0 4.4 fusion.54
  460.3 4.0 gather_fusion.6
  468.3 4.0 gather_fusion.8
  472.3 4.0 gather_fusion.9
  476.3 4.0 gather_fusion.2
  480.3 4.3 fusion.108
  484.6 9.7 %psum.29 = f32[]{:T(128)} all-reduce(f32[]{:T(128)} %get-tuple-element.338), channel_id=1, replica_groups=mesh['dp_0'=4,'dp_1'=8,'dp_2'=4,'blk'=2] {'dp_0'}, use_global_device_ids=true, to_apply=%region_22.25 | all-reduce | flops 1 | bytes 8 | tf_op jit(solution)/shard_map/psum | solution.py:41
  495.0 16.2 %psum.30 = f32[]{:T(128)} all-reduce(f32[]{:T(128)} %psum.29), channel_id=1, replica_groups=mesh['dp_0'=4,'dp_1'=8,'dp_2'=4,'blk'=2] {'dp_1'}, use_global_device_ids=true, to_apply=%region_23.26 | all-reduce | flops 1 | bytes 8 | tf_op jit(solution)/shard_map/psum | solution.py:41
  512.4 10.2 %psum.31 = f32[]{:T(128)} all-reduce(f32[]{:T(128)} %psum.30), channel_id=1, replica_groups=mesh['dp_0'=4,'dp_1'=8,'dp_2'=4,'blk'=2] {'dp_2'}, use_global_device_ids=true, to_apply=%region_24.27 | all-reduce | flops 1 | bytes 8 | tf_op jit(solution)/shard_map/psum | solution.py:41
  (224 shorter events, 149.4 us)
Async XLA Ops:
  7.2 283.3 %all-reduce.2.cloned.1.call-start = ((), (), s32[]{:S(2)}) async-start(), calls=%async_computation | async-start | bytes 8134656 | tf_op jit(solution)/shard_map/psum | solution.py:20
  295.7 29.2 %copy-start.2 = (f32[8,256,96]{1,2,0:T(8,128)}, f32[8,256,96]{1,2,0:T(8,128)S(1)}, u32[]{:S(2)}) copy-start(f32[8,256,96]{1,2,0:T(8,128)S(1)} %slice.124) | copy-start | bytes 2359300
  296.4 3.5 copy-start.10
  307.2 6.7 %copy-start = (f32[14,256,256]{2,1,0:T(8,128)S(1)}, f32[14,256,256]{2,1,0:T(8,128)}, u32[]{:S(2)}) copy-start(f32[14,256,256]{2,1,0:T(8,128)} %reshape.128) | copy-start | bytes 11010052
  319.7 2.8 collective-permute-start
  337.6 2.4 collective-permute-start.1
  354.9 2.4 collective-permute-start.2
  372.0 2.4 collective-permute-start.3
  387.4 2.9 copy-start.13
  387.5 3.5 copy-start.9
  390.2 2.8 collective-permute-start.4
  392.0 3.3 copy-start.24
  392.0 3.3 copy-start.7
  410.8 2.4 collective-permute-start.5
  427.9 2.4 collective-permute-start.6
  445.1 3.2 copy-start.3
  445.1 3.2 copy-start.16
  445.1 3.2 copy-start.18
  445.1 3.2 copy-start.20
  445.1 3.2 copy-start.22
  445.1 2.4 collective-permute-start.7
  476.3 4.0 copy-start.11
  476.3 4.0 copy-start.14
  480.3 31.0 %copy-start.5 = (f32[8,256,96]{1,0,2:T(8,128)S(1)}, f32[8,256,96]{1,0,2:T(8,128)}, u32[]{:S(2)}) copy-start(f32[8,256,96]{1,0,2:T(8,128)} %copy-done.4) | copy-start | bytes 2359300
  (12 other events, 15.7 us)
Sparse Core Ops, SparseCore 0:
  52.7 237.7 all-reduce.1
where the time goes:
time: 541 us; the launch traced here: 533 us
  waiting for transfers between devices  252 us (47%)
  matrix products  121 us (22%)
  local copies, waits for them, and re-layouts  62.1 us (11%)
  blocking collectives  38.6 us (7%)
  other arithmetic  37.4 us (7%)
  between operations  19.2 us (4%)
    psum x1, waiting for transfers between devices, in_one(): running = lax.psum(jnp.concatenate([a.ravel() for a in arrays]), axis)  237 us
    psum x3, blocking collectives, by_axis(): array = lax.psum(array, axis)  36.2 us
    dot_general x8, matrix products, body(): forward = jnp.einsum('kce,ked->kcd', joint, at_second, precision=HIGH)  35.1 us
    gather x8, local copies, waits for them, and re-layouts, body(): recon = recon + jnp.take(solution[book], codes[:, book], axis=0)  28.4 us
    dot_general x8, matrix products, body(): backward = jnp.einsum('kce,kcd->ked', joint, at_first, precision=HIGH)  27.2 us
    dot_general x2, matrix products, accumulate(): jnp.einsum('krc,kre->kce', first_hot, second_hot, preferred_element_type=...  14.7 us
    ppermute x8, waiting for transfers between devices, partner_2(): lax.ppermute(array, axis, [(i, i ^ 1 << bit) for i in range(lax.axis_size...  14.2 us
    dot_general x8, matrix products, body(): part = jnp.einsum('km,kcd->mcd', pick_first, forward, precision=HIGH)  14.1 us
  transfers between devices with their start and end apart: 9, of which 8 were waited for; matrix products, arithmetic and copies ran while one was open for 1% of the time, Pallas kernels for 0%

commit v1 on v0

v1 whole, which is shorter than its diff:
```python
import functools

import jax
import jax.numpy as jnp
from jax import lax
from jax.experimental import pallas as pl
from jax.experimental.pallas import tpu as pltpu
from jax.sharding import Mesh
from jax.sharding import PartitionSpec as P

K = 256
M = 8
D = 96
ITERS = 8
NY, NZ, NX = 4, 8, 4
DP = ("y", "z", "x")
F32 = jnp.float32
BF16 = jnp.bfloat16
NT = (((1,), (1,)), ((), ()))
NN = (((1,), (0,)), ((), ()))


def dot(a, b, dims):
    return lax.dot_general(a, b, dims, preferred_element_type=F32)


def split3(a):
    hi = a.astype(BF16).astype(F32)
    rest = a - hi
    mid = rest.astype(BF16).astype(F32)
    return hi, mid, rest - mid


def params(**more):
    return pltpu.CompilerParams(vmem_limit_bytes=48 << 20, **more)


VMEM = pl.BlockSpec(memory_space=pltpu.VMEM)
SMEM = pl.BlockSpec(memory_space=pltpu.SMEM)
ANY = pl.BlockSpec(memory_space=pl.ANY)


def message_kernel(info, codes_ref, mass_ref, vectors_ref, out_ref):
    core = info[3]
    codes = codes_ref[...].astype(F32)
    mass = mass_ref[...]
    ones = jnp.ones_like(mass)
    for z in range(NZ):
        out_ref[z, 0:8, :] = codes
        out_ref[z, 8:9, :] = mass
        for j in range(6):
            out_ref[z, 9 + j : 10 + j, :] = vectors_ref[pl.ds(12 * z + 6 * core + j, 1), :]
        out_ref[z, 15:16, :] = ones


def joint_kernel(info, msg_ref, out_ref, hot, near, far, right):
    step = pl.program_id(0)
    z = info[1]
    core = info[3]
    rows = msg_ref.shape[2]

    @pl.when(step == 0)
    def _():
        near[...] = jnp.zeros_like(near)
        far[...] = jnp.zeros_like(far)
        right[...] = jnp.zeros_like(right)

    level = lax.broadcasted_iota(jnp.int32, (K, rows), 0).astype(F32).astype(BF16)
    for book in range(M):
        code = msg_ref[0, book : book + 1, :].astype(BF16)
        hot[book] = jnp.where(level == code, jnp.ones((), BF16), jnp.zeros((), BF16))
    mass = msg_ref[0, 8:9, :]
    weighted = msg_ref[0, 8:16, :] * mass
    hi, mid, lo = split3(weighted)
    sums = jnp.concatenate([hi, mid, lo, jnp.zeros_like(lo)], axis=0).astype(BF16)
    mass = mass.astype(BF16)
    base = pl.multiple_of(128 * core, 128)
    mine = hot[z, pl.ds(base, 128), :] * mass
    for s in range(M):
        book = (z + s) & 7
        second = hot[book]
        if 1 <= s <= 3:
            near[s - 1] += dot(mine, second, NT)
        right[book] += dot(sums, second, NT)
    low = z & 3
    side = pl.multiple_of(128 * (z >> 2), 128)
    first = hot[low, pl.ds(base, 128), :] * mass
    far[...] += dot(first, hot[low + 4, pl.ds(side, 128), :], NT)

    @pl.when(step == pl.num_programs(0) - 1)
    def _():
        for s in range(3):
            for h in range(2):
                t = 2 * s + h
                out_ref[2 * t] = near[s, 0:64, 128 * h : 128 * h + 128]
                out_ref[2 * t + 1] = near[s, 64:128, 128 * h : 128 * h + 128]
        out_ref[12] = far[0:64, :]
        out_ref[13] = far[64:128, :]
        for book in range(M):
            part = right[book]
            part = part[0:8] + part[8:16] + part[16:24]
            for h in range(2):
                i = 2 * book + h
                out_ref[14 + i // 8, 8 * (i % 8) : 8 * (i % 8) + 8, :] = part[:, 128 * h : 128 * h + 128]


def sum_kernel(in_ref, out_ref):
    total = in_ref[0]
    for i in range(1, in_ref.shape[0]):
        total = total + in_ref[i]
    for i in range(out_ref.shape[0]):
        out_ref[i] = total


def solve_kernel(places, info, ridge, *refs):
    n = len(places)
    pieces = refs[:n]
    out_ref, mass_ref = refs[n : n + 2]
    slab, high, low, wide, vec, sem = refs[n + 2 :]
    y, z, x, core = (info[i] for i in range(4))
    copies = []
    for piece, (other, parts) in zip(pieces, places):
        at_core = 1 - core if other else core
        for at, half, dy, dx, sub, size in parts:
            chunk = ((y + dy) & 3) * 4 + ((x + dx) & 3)
            row = pl.multiple_of(64 * chunk + 32 * half, 32)
            copies.append(
                pltpu.make_async_copy(
                    piece.at[pl.ds(at, size)],
                    slab.at[at_core, pl.ds(sub, size), pl.ds(row, 32), :],
                    sem,
                )
            )
    for copy in copies:
        copy.start()
    for copy in copies:
        copy.wait()

    def keep(block, r, c, tile):
        hi = tile.astype(BF16)
        high[block, r : r + 128, c : c + 128] = hi
        low[block, r : r + 128, c : c + 128] = (tile - hi.astype(F32)).astype(BF16)

    def build(p, _):
        for s in range(3):
            for h in range(2):
                for c in range(2):
                    keep(3 * p + s, 128 * c, 128 * h, slab[c, p, 128 * (2 * s + h) : 128 * (2 * s + h) + 128, :])
        return 0

    lax.fori_loop(0, M, build, 0)

    def build_far(p, _):
        for c in range(2):
            keep(24 + p, 128 * c, 0, slab[c, p, 768:896, :])
            keep(24 + p, 128 * c, 128, slab[c, p + 4, 768:896, :])
        return 0

    lax.fori_loop(0, 4, build_far, 0)

    group = 4 * y + x
    start, remain, direction, precond = 0, 1, 2, 3
    for i in range(16):
        tile = slab[group & 1, group >> 1, 896 + 8 * i : 904 + 8 * i, :]
        vec[remain, :, 128 * i : 128 * i + 128] = tile
    counts = vec[remain, 7:8, :]
    mass = jnp.sum(counts[:, 0:K], axis=1, keepdims=True)
    mass_ref[...] = jnp.broadcast_to(mass, mass_ref.shape)
    lam = ridge[0] * mass / K
    vec[precond] = jnp.broadcast_to(counts + lam, vec.shape[1:])
    vec[start] = jnp.zeros(vec.shape[1:], F32)
    scaled = vec[remain] / vec[precond]
    vec[direction] = scaled
    first_inner = jnp.sum(vec[remain] * scaled, axis=1, keepdims=True)

    def step(_, inner):
        d = vec[direction]
        hi, mid, lo = split3(d)
        wide[...] = jnp.concatenate([hi, mid, lo, jnp.zeros_like(lo)], axis=0).astype(BF16)
        image = []
        for m in range(M):
            total = jnp.zeros((32, K), F32)
            for s in range(1, M):
                q = (m + s) % M
                if s <= 3 or (s == 4 and m < 4):
                    block, dims = (3 * m + s - 1 if s <= 3 else 24 + m), NT
                else:
                    block, dims = (3 * q + 7 - s if s >= 5 else 24 + q), NN
                part = wide[:, K * q : K * q + K]
                total = total + dot(part, high[block], dims) + dot(part, low[block], dims)
            image.append(total[0:8] + total[8:16] + total[16:24])
        image = jnp.concatenate(image, axis=1) + vec[precond] * d
        alpha = inner / jnp.sum(d * image, axis=1, keepdims=True)
        vec[start] = vec[start] + alpha * d
        r = vec[remain] - alpha * image
        vec[remain] = r
        scaled = r / vec[precond]
        fresh = jnp.sum(r * scaled, axis=1, keepdims=True)
        vec[direction] = scaled + fresh / inner * d
        return fresh

    lax.fori_loop(0, ITERS, step, first_inner)
    for i in range(16):
        out_ref[6 * i : 6 * i + 6, :] = vec[start, 1:7, 128 * i : 128 * i + 128]


def residual_kernel(books_ref, codes_ref, mass_ref, vectors_ref, out_ref, table_ref, part_ref, left, hot):
    step = pl.program_id(0)

    @pl.when(step == 0)
    def _():
        for m in range(M):
            for h in range(2):
                for k in range(16):
                    i = 2 * m + h
                    table_ref[m, 6 * k : 6 * k + 6, 128 * h : 128 * h + 128] = books_ref[k, 6 * i : 6 * i + 6, :]
        for m in range(M):
            for t, piece in enumerate(split3(table_ref[m])):
                left[D * t : D * t + D, K * m : K * m + K] = piece.astype(BF16)
        part_ref[...] = jnp.zeros_like(part_ref)

    cols = codes_ref.shape[1]
    level = lax.broadcasted_iota(jnp.int32, (K, cols), 0).astype(F32).astype(BF16)
    for m in range(M):
        code = codes_ref[m : m + 1, :].astype(F32).astype(BF16)
        hot[K * m : K * m + K, :] = jnp.where(level == code, jnp.ones((), BF16), jnp.zeros((), BF16))
    recon = dot(left[...], hot[...], NN)
    recon = recon[0:D] + recon[D : 2 * D] + recon[2 * D : 3 * D]
    residual = vectors_ref[...] - recon
    out_ref[...] = residual
    total = jnp.sum(residual * residual, axis=0, keepdims=True) * mass_ref[...]
    part_ref[...] += jnp.broadcast_to(jnp.sum(total, axis=1, keepdims=True), part_ref.shape)


def shift(array, axis, by):
    size = lax.axis_size(axis)
    return lax.ppermute(array, axis, [(i, (i + by) % size) for i in range(size)])


def swap(array):
    return lax.ppermute(array, "c", [(0, 1), (1, 0)])


def ring(array, axis):
    up = shift(array, axis, 1)
    down = shift(array, axis, -1)
    half = array.shape[0] // 2
    return up, down, shift(up[:half], axis, 1), shift(down[half:], axis, -1)


def spread(array, axes):
    return lax.all_to_all(array, axes, 0, 0, tiled=True)


def body(vectors, codes, weights, ridge):
    rows = vectors.shape[0]
    vectors = vectors.T
    codes = codes.T
    mass = weights.astype(F32).reshape(1, rows)
    info = jnp.stack([lax.axis_index(a) for a in ("y", "z", "x", "c")]).astype(jnp.int32)
    message = pl.pallas_call(
        message_kernel,
        out_shape=jax.ShapeDtypeStruct((NZ, 16, rows), F32),
        in_specs=[SMEM, VMEM, VMEM, VMEM],
        out_specs=VMEM,
        compiler_params=params(),
        name="message",
    )(info, codes, mass, vectors)
    message = spread(message, "z")
    slab = pl.pallas_call(
        joint_kernel,
        grid=(NZ,),
        out_shape=jax.ShapeDtypeStruct((16, 64, 128), F32),
        in_specs=[SMEM, pl.BlockSpec((1, 16, rows), lambda i: (i, 0, 0))],
        out_specs=pl.BlockSpec((16, 64, 128), lambda i: (0, 0, 0)),
        scratch_shapes=[
            pltpu.VMEM((M, K, rows), BF16),
            pltpu.VMEM((3, 128, K), F32),
            pltpu.VMEM((128, 128), F32),
            pltpu.VMEM((M, 32, K), F32),
        ],
        compiler_params=params(dimension_semantics=("arbitrary",)),
        name="joint",
    )(info, message)
    slab = spread(slab, ("y", "x"))
    chunk = pl.pallas_call(
        sum_kernel,
        out_shape=jax.ShapeDtypeStruct((NZ, 64, 128), F32),
        in_specs=[VMEM],
        out_specs=VMEM,
        compiler_params=params(),
        name="chunk",
    )(slab)
    line = spread(chunk, "z")
    pieces = []
    for half, first, second in ((0, "y", "x"), (1, "x", "y")):
        own = line[:, 32 * half : 32 * half + 32]
        wide = jnp.concatenate([own, *ring(own, first)], axis=0)
        pieces.extend(zip(("own", "up", "down", "far0", "far1"), (half,) * 5, (wide, *ring(wide, second))))
    places, arrays = [], []
    for name, half, array in pieces:
        parts = []
        units = {"far0": (0, 1), "far1": (2, 3)}.get(name, (0, 1, 2, 3))
        outer = {"own": 0, "up": -1, "down": 1}.get(name, 2)
        for n, u in enumerate(units):
            inner = (0, -1, 1, 2)[u]
            dy, dx = (inner, outer) if half == 0 else (outer, inner)
            parts.append((8 * n, half, dy, dx, 0, 8))
        for other in (False, True):
            places.append((other, parts))
            arrays.append(swap(array) if other else array)
    columns, total_mass = pl.pallas_call(
        functools.partial(solve_kernel, places),
        out_shape=(jax.ShapeDtypeStruct((D, 128), F32), jax.ShapeDtypeStruct((8, 128), F32)),
        in_specs=[SMEM, SMEM] + [ANY] * len(arrays),
        out_specs=(VMEM, VMEM),
        scratch_shapes=[
            pltpu.VMEM((2, NZ, 1024, 128), F32),
            pltpu.VMEM((28, K, K), BF16),
            pltpu.VMEM((28, K, K), BF16),
            pltpu.VMEM((32, M * K), BF16),
            pltpu.VMEM((4, 8, M * K), F32),
            pltpu.SemaphoreType.DMA,
        ],
        compiler_params=params(),
        name="solve",
    )(info, ridge, *arrays)
    books = spread(jnp.broadcast_to(columns[None], (16, D, 128)), ("y", "x"))
    lanes = 256
    residual, table, part = pl.pallas_call(
        residual_kernel,
        grid=(rows // lanes,),
        out_shape=(
            jax.ShapeDtypeStruct((D, rows), F32),
            jax.ShapeDtypeStruct((M, D, K), F32),
            jax.ShapeDtypeStruct((8, 128), F32),
        ),
        in_specs=[
            pl.BlockSpec((16, D, 128), lambda i: (0, 0, 0)),
            pl.BlockSpec((M, lanes), lambda i: (0, i)),
            pl.BlockSpec((1, lanes), lambda i: (0, i)),
            pl.BlockSpec((D, lanes), lambda i: (0, i)),
        ],
        out_specs=(
            pl.BlockSpec((D, lanes), lambda i: (0, i)),
            pl.BlockSpec((M, D, K), lambda i: (0, 0, 0)),
            pl.BlockSpec((8, 128), lambda i: (0, 0)),
        ),
        scratch_shapes=[pltpu.VMEM((3 * D, M * K), BF16), pltpu.VMEM((M * K, lanes), BF16)],
        compiler_params=params(dimension_semantics=("arbitrary",)),
        name="residual",
    )(books, codes, mass, vectors)
    plane = spread(jnp.broadcast_to(part[:1], (16, 128)), ("y", "x"))
    plane = jnp.sum(plane, axis=0, keepdims=True)
    total = spread(jnp.broadcast_to(plane, (NZ, 128)), "z")
    total = jnp.sum(total[:, 0])
    distortion = total / (total_mass[0, 0] * D)
    return (table.transpose(0, 2, 1), residual.T, distortion)


def solution(mesh):
    finer = Mesh(mesh.devices.reshape(NY, NZ, NX, 2), ("y", "z", "x", "c"))
    placed = (P(DP, None), P(DP, None), P(DP), P())
    return jax.shard_map(
        body, mesh=finer, in_specs=placed, out_specs=(P(), P(DP, None), P()), check_vma=False
    )
```

time: 541 us -> 203 us (0.38); the launches traced: 533 us -> 203 us
  waiting for transfers between devices: 252 us -> 27.8 us
  matrix products: 121 us -> 0 us
  Pallas kernels: 0 us -> 58.2 us
  local copies, waits for them, and re-layouts: 62.1 us -> 3.99 us
  blocking collectives: 38.6 us -> 84.6 us
  other arithmetic: 37.4 us -> 1.38 us
  starting transfers between devices: 2.9 us -> 22.5 us
  between operations: 19.2 us -> 4.01 us
    psum x1 -> x0, waiting for transfers between devices: 237 us -> none  [in_one(): running = lax.psum(jnp.concatenate([a.ravel() for a in arrays]), axis)]
    dot_general x52 -> x0, matrix products: 121 us -> none  [the longest x8 35.1 us: body(): forward = jnp.einsum('kce,ked->kcd', joint, at_second, precision=HIGH)]
    all_to_all x0 -> x5, blocking collectives: none -> 84.6 us  [spread(): return lax.all_to_all(array, axes, 0, 0, tiled=True)]
    pallas_call x0 -> x5, Pallas kernels: none -> 58.2 us  [the longest x1 34.4 us: body(): pl.pallas_call(functools.partial(solve_kernel, places), out_shape=(jax.Sh...]
    gather x12 -> x0, local copies, waits for them, and re-layouts: 39 us -> none  [the longest x8 28.4 us: body(): recon = recon + jnp.take(solution[book], codes[:, book], axis=0)]
    psum x3 -> x0, blocking collectives: 36.2 us -> none  [by_axis(): array = lax.psum(array, axis)]
    reduce_sum x19 -> x2, other arithmetic: 24.7 us -> 0.62 us  [the longest x1 0.6 us: body(): total = jnp.sum(total[:, 0])]
    ppermute x8 -> x26, starting transfers between devices: 2.87 us -> 19.2 us  [the longest x16 17.9 us: shift(): lax.ppermute(array, axis, [(i, (i + by) % size) for i in range(size)])]
  transfers between devices with their start and end apart: 9 -> 27, of which waited for: 8 -> 11; matrix products, arithmetic and copies ran while one was open for 1% -> 0% of each run, Pallas kernels for 0% -> 0%
where the time goes in v1:
time: 203 us
  blocking collectives  84.6 us (42%)
  Pallas kernels  58.2 us (29%)
  waiting for transfers between devices  27.8 us (14%)
  starting transfers between devices  22.5 us (11%)
  between operations  4.01 us (2%)
  local copies, waits for them, and re-layouts  3.99 us (2%)
    all_to_all x5, blocking collectives, spread(): return lax.all_to_all(array, axes, 0, 0, tiled=True)  84.6 us
    pallas_call x1, Pallas kernels, body(): pl.pallas_call(functools.partial(solve_kernel, places), out_shape=(jax.Sh...  34.4 us
    pallas_call x1, Pallas kernels, body(): pl.pallas_call(joint_kernel, grid=(NZ,), out_shape=jax.ShapeDtypeStruct((...  19.9 us
    ppermute x16, waiting for transfers between devices, shift(): lax.ppermute(array, axis, [(i, (i + by) % size) for i in range(size)])  18.7 us
    ppermute x16, starting transfers between devices, shift(): lax.ppermute(array, axis, [(i, (i + by) % size) for i in range(size)])  17.9 us
    all_to_all x1, waiting for transfers between devices, spread(): return lax.all_to_all(array, axes, 0, 0, tiled=True)  6.42 us
  transfers between devices with their start and end apart: 27, of which 11 were waited for; matrix products, arithmetic and copies ran while one was open for 0% of the time, Pallas kernels for 0%

profile of v1, /device:TPU:2, one launch (start us, length us, event | category | flops | bytes accessed | tf_op | source)
XLA Modules:
  0.0 202.6 jit_solution(16241515042350542484)
XLA Ops:
  3.1 25.8 %all_to_all.35.msg_ref = f32[8,16,1024]{2,1,0:T(8,128)S(1)} all-to-all(f32[8,16,1024]{2,1,0:T(8,128)S(1)} %message.1), channel_id=1, replica_groups=mesh['y'=4,'z'=8,'x'=4,'c'=2] {'z'}, dimensions={0} | all-to-all | bytes 1048576 | tf_op jit(solution)/shard_map/all_to_all | solution.py:252
  28.8 19.9 %joint.1 = f32[16,64,128]{2,1,0:T(8,128)S(1)} custom-call(s32[4]{0:T(128)S(1)} %pad_add_fusion.info, f32[8,16,1024]{2,1,0:T(8,128)S(1)} %all_to_all.35.msg_ref), custom_call_target="tpu_custom_call" | custom-call | tf_op jit(solution)/shard_map/joint/pallas_call | solution.py:270
  48.7 16.0 %all_to_all.36.in_ref = f32[16,64,128]{2,1,0:T(8,128)S(1)} all-to-all(f32[16,64,128]{2,1,0:T(8,128)S(1)} %joint.1), channel_id=1, replica_groups=mesh['y'=4,'z'=8,'x'=4,'c'=2] {'y','x'}, dimensions={0} | all-to-all | bytes 1048576 | tf_op jit(solution)/shard_map/all_to_all | solution.py:252
  64.8 13.0 %all_to_all.37 = f32[8,64,128]{2,1,0:T(8,128)S(1)} all-to-all(f32[8,64,128]{2,1,0:T(8,128)S(1)} %chunk.1), channel_id=1, replica_groups=mesh['y'=4,'z'=8,'x'=4,'c'=2] {'z'}, dimensions={0} | all-to-all | bytes 524288 | tf_op jit(solution)/shard_map/all_to_all | solution.py:252
  77.8 1.5 collective-permute-start.14
  80.8 1.2 collective-permute-start
  81.9 1.5 collective-permute-done.14
  83.4 1.3 collective-permute-start.16
  85.6 2.1 %collective-permute-start.3 = (f32[4,32,128]{2,1,0:T(8,128)S(1)}, f32[4,32,128]{2,1,0:T(8,128)S(1)}, u32[]{:S(2)}, u32[]{:S(2)}) collective-permute-start(f32[4,32,128]{2,1,0:T(8,128)S(1)} %slice.57), channel_id=1, source_target_pairs={{0,192},{64,0},{128,64},{192,128},{1,193},{65,1},{129,65},{193,129... | collective-permute-start | bytes 196616 | tf_op jit(solution)/shard_map/ppermute | solution.py:237
  87.8 5.8 %collective-permute-done.2 = f32[4,32,128]{2,1,0:T(8,128)S(1)} collective-permute-done((f32[4,32,128]{2,1,0:T(8,128)S(1)}, f32[4,32,128]{2,1,0:T(8,128)S(1)}, u32[]{:S(2)}, u32[]{:S(2)}) %collective-permute-start.2) | collective-permute-done | bytes 65568 | tf_op jit(solution)/shard_map/ppermute | solution.py:237
  93.7 1.1 collective-permute-start.7
  95.9 2.0 collective-permute-start.18
  97.9 5.0 %collective-permute-done.7.refs_4_ = f32[32,32,128]{2,1,0:T(8,128)S(1)} collective-permute-done((f32[32,32,128]{2,1,0:T(8,128)S(1)}, f32[32,32,128]{2,1,0:T(8,128)S(1)}, u32[]{:S(2)}, u32[]{:S(2)}) %collective-permute-start.7) | collective-permute-done | bytes 524320 | tf_op jit(solution)/shard_map/ppermute | solution.py:237
  104.0 3.2 %collective-permute-start.11 = (f32[16,32,128]{2,1,0:T(8,128)S(1)}, f32[16,32,128]{2,1,0:T(8,128)S(1)}, u32[]{:S(2)}, u32[]{:S(2)}) collective-permute-start(f32[16,32,128]{2,1,0:T(8,128)S(1)} %slice.59), channel_id=1, source_target_pairs={{0,6},{2,0},{4,2},{6,4},{1,7},{3,1},{5,3},{7,5},{8,14},{10,8},{12,... | collective-permute-start | bytes 786440 | tf_op jit(solution)/shard_map/ppermute | solution.py:237
  107.7 1.9 collective-permute-start.22
  109.5 2.2 %collective-permute-done.11.refs_8_ = f32[16,32,128]{2,1,0:T(8,128)S(1)} collective-permute-done((f32[16,32,128]{2,1,0:T(8,128)S(1)}, f32[16,32,128]{2,1,0:T(8,128)S(1)}, u32[]{:S(2)}, u32[]{:S(2)}) %collective-permute-start.11) | collective-permute-done | bytes 262176 | tf_op jit(solution)/shard_map/ppermute | solution.py:237
  111.7 2.3 %collective-permute-done.9.refs_6_ = f32[16,32,128]{2,1,0:T(8,128)S(1)} collective-permute-done((f32[16,32,128]{2,1,0:T(8,128)S(1)}, f32[16,32,128]{2,1,0:T(8,128)S(1)}, u32[]{:S(2)}, u32[]{:S(2)}) %collective-permute-start.9) | collective-permute-done | bytes 262176 | tf_op jit(solution)/shard_map/ppermute | solution.py:237
  117.5 1.8 collective-permute-done.23.refs_17_
  121.0 34.4 %solve.1 = (f32[96,128]{1,0:T(8,128)S(1)}, f32[8,128]{1,0:T(8,128)S(1)}) custom-call(s32[4]{0:T(128)S(1)} %pad_add_fusion.info, f32[1]{0:T(128)S(6)} %copy.18.ridge, f32[32,32,128]{2,1,0:T(8,128)S(1)} %constant_dynamic-update-slice_fusion.refs_0_, f32[32,32,128]{2,1,0:T(8,128)S(1)} %collective-permute-done.4.refs_1_, ...), custom_call_target="tpu_custom_call" | custom-call | tf_op jit(solution)/shard_map/solve/pallas_call | solution.py:312
  155.5 19.4 %all_to_all.38.books_ref = f32[16,96,128]{2,1,0:T(8,128)S(1)} all-to-all(f32[16,96,128]{2,1,0:T(8,128)S(1)} %broadcast_in_dim.6), channel_id=1, replica_groups=mesh['y'=4,'z'=8,'x'=4,'c'=2] {'y','x'}, dimensions={0} | all-to-all | bytes 1572864 | tf_op jit(solution)/shard_map/all_to_all | solution.py:252
  174.9 3.3 %residual.1 = (f32[96,1024]{1,0:T(8,128)}, f32[8,96,256]{2,1,0:T(8,128)}, f32[8,128]{1,0:T(8,128)S(1)}) custom-call(f32[16,96,128]{2,1,0:T(8,128)S(1)} %all_to_all.38.books_ref, s32[8,1024]{1,0:T(8,128)S(1)} %bitcast.17, f32[1,1024]{1,0:T(1,128)S(1)} %bitcast.19, f32[96,1024]{1,0:T(8,128)S(1)} %bitcast.15), custom_call_target="tpu_custom_call" | custom-call | tf_op jit(solution)/shard_map/residual/pallas_call | solution.py:330
  178.2 10.5 %all_to_all.39 = f32[16,1,128]{2,1,0:T(1,128)S(1)} all-to-all(f32[16,1,128]{2,1,0:T(1,128)S(1)} %broadcast_in_dim.7), channel_id=1, replica_groups=mesh['y'=4,'z'=8,'x'=4,'c'=2] {'y','x'}, dimensions={0} | all-to-all | bytes 16384 | tf_op jit(solution)/shard_map/all_to_all | solution.py:252
  189.3 3.3 %all-to-all-start.5 = ((f32[8,1,128]{2,1,0:T(1,128)}), f32[8,1,128]{2,1,0:T(1,128)S(1)}, u32[]{:S(2)}, u32[]{:S(2)}) async-start(f32[8,1,128]{2,1,0:T(1,128)} %broadcast_in_dim.8), calls=%async_computation.5 | async-start | bytes 8192 | tf_op jit(solution)/shard_map/all_to_all | solution.py:252
  193.8 6.4 %all-to-all-done.5 = f32[8,1,128]{2,1,0:T(1,128)S(1)} async-done(((f32[8,1,128]{2,1,0:T(1,128)}), f32[8,1,128]{2,1,0:T(1,128)S(1)}, u32[]{:S(2)}, u32[]{:S(2)}) %all-to-all-start.5) | async-done | bytes 4128 | tf_op jit(solution)/shard_map/all_to_all | solution.py:252
  (82 shorter events, 13.7 us)
Async XLA Ops:
  77.8 5.6 %collective-permute-start.14 = (f32[8,32,128]{2,1,0:T(8,128)S(1)}, f32[8,32,128]{2,1,0:T(8,128)S(1)}, u32[]{:S(2)}, u32[]{:S(2)}) collective-permute-start(f32[8,32,128]{2,1,0:T(8,128)S(1)} %get-tuple-element.13), channel_id=1, source_target_pairs={{0,6},{2,0},{4,2},{6,4},{1,7},{3,1},{5,3},{7,5},{8,14},{10,8},{12,... | collective-permute-start | bytes 393224 | tf_op jit(solution)/shard_map/ppermute | solution.py:237
  79.3 5.6 %collective-permute-start.13 = (f32[8,32,128]{2,1,0:T(8,128)S(1)}, f32[8,32,128]{2,1,0:T(8,128)S(1)}, u32[]{:S(2)}, u32[]{:S(2)}) collective-permute-start(f32[8,32,128]{2,1,0:T(8,128)S(1)} %get-tuple-element.13), channel_id=1, source_target_pairs={{0,2},{2,4},{4,6},{6,0},{1,3},{3,5},{5,7},{7,1},{8,10},{10,12},{12... | collective-permute-start | bytes 393224 | tf_op jit(solution)/shard_map/ppermute | solution.py:237
  79.9 5.6 %collective-permute-start.1 = (f32[8,32,128]{2,1,0:T(8,128)S(1)}, f32[8,32,128]{2,1,0:T(8,128)S(1)}, u32[]{:S(2)}, u32[]{:S(2)}) collective-permute-start(f32[8,32,128]{2,1,0:T(8,128)S(1)} %get-tuple-element.16), channel_id=1, source_target_pairs={{0,192},{64,0},{128,64},{192,128},{1,193},{65,1},{129,65},{193,129... | collective-permute-start | bytes 393224 | tf_op jit(solution)/shard_map/ppermute | solution.py:237
  80.8 6.9 %collective-permute-start = (f32[8,32,128]{2,1,0:T(8,128)S(1)}, f32[8,32,128]{2,1,0:T(8,128)S(1)}, u32[]{:S(2)}, u32[]{:S(2)}) collective-permute-start(f32[8,32,128]{2,1,0:T(8,128)S(1)} %get-tuple-element.16), channel_id=1, source_target_pairs={{0,64},{64,128},{128,192},{192,0},{1,65},{65,129},{129,193},{193,1... | collective-permute-start | bytes 393224 | tf_op jit(solution)/shard_map/ppermute | solution.py:237
  83.4 12.3 %collective-permute-start.16 = (f32[4,32,128]{2,1,0:T(8,128)S(1)}, f32[4,32,128]{2,1,0:T(8,128)S(1)}, u32[]{:S(2)}, u32[]{:S(2)}) collective-permute-start(f32[4,32,128]{2,1,0:T(8,128)S(1)} %slice.62), channel_id=1, source_target_pairs={{0,6},{2,0},{4,2},{6,4},{1,7},{3,1},{5,3},{7,5},{8,14},{10,8},{12,... | collective-permute-start | bytes 196616 | tf_op jit(solution)/shard_map/ppermute | solution.py:237
  84.9 10.8 %collective-permute-start.15 = (f32[4,32,128]{2,1,0:T(8,128)S(1)}, f32[4,32,128]{2,1,0:T(8,128)S(1)}, u32[]{:S(2)}, u32[]{:S(2)}) collective-permute-start(f32[4,32,128]{2,1,0:T(8,128)S(1)} %slice.61), channel_id=1, source_target_pairs={{0,2},{2,4},{4,6},{6,0},{1,3},{3,5},{5,7},{7,1},{8,10},{10,12},{12... | collective-permute-start | bytes 196616 | tf_op jit(solution)/shard_map/ppermute | solution.py:237
  85.6 8.1 %collective-permute-start.3 = (f32[4,32,128]{2,1,0:T(8,128)S(1)}, f32[4,32,128]{2,1,0:T(8,128)S(1)}, u32[]{:S(2)}, u32[]{:S(2)}) collective-permute-start(f32[4,32,128]{2,1,0:T(8,128)S(1)} %slice.57), channel_id=1, source_target_pairs={{0,192},{64,0},{128,64},{192,128},{1,193},{65,1},{129,65},{193,129... | collective-permute-start | bytes 196616 | tf_op jit(solution)/shard_map/ppermute | solution.py:237
  87.7 6.0 %collective-permute-start.2 = (f32[4,32,128]{2,1,0:T(8,128)S(1)}, f32[4,32,128]{2,1,0:T(8,128)S(1)}, u32[]{:S(2)}, u32[]{:S(2)}) collective-permute-start(f32[4,32,128]{2,1,0:T(8,128)S(1)} %slice.56), channel_id=1, source_target_pairs={{0,64},{64,128},{128,192},{192,0},{1,65},{65,129},{129,193},{193,1... | collective-permute-start | bytes 196616 | tf_op jit(solution)/shard_map/ppermute | solution.py:237
  93.7 9.3 %collective-permute-start.7 = (f32[32,32,128]{2,1,0:T(8,128)S(1)}, f32[32,32,128]{2,1,0:T(8,128)S(1)}, u32[]{:S(2)}, u32[]{:S(2)}) collective-permute-start(f32[32,32,128]{2,1,0:T(8,128)S(1)} %constant_dynamic-update-slice_fusion.refs_0_), channel_id=1, source_target_pairs={{0,6},{2,0},{4,2},{6,4},{1,7},{3,1},{5,3},{7,5},{8,14},{10,8},{12,... | collective-permute-start | bytes 1572872 | tf_op jit(solution)/shard_map/ppermute | solution.py:237
  94.8 9.2 %collective-permute-start.5 = (f32[32,32,128]{2,1,0:T(8,128)S(1)}, f32[32,32,128]{2,1,0:T(8,128)S(1)}, u32[]{:S(2)}, u32[]{:S(2)}) collective-permute-start(f32[32,32,128]{2,1,0:T(8,128)S(1)} %constant_dynamic-update-slice_fusion.refs_0_), channel_id=1, source_target_pairs={{0,2},{2,4},{4,6},{6,0},{1,3},{3,5},{5,7},{7,1},{8,10},{10,12},{12... | collective-permute-start | bytes 1572872 | tf_op jit(solution)/shard_map/ppermute | solution.py:237
  95.8 11.4 %collective-permute-start.20 = (f32[32,32,128]{2,1,0:T(8,128)S(1)}, f32[32,32,128]{2,1,0:T(8,128)S(1)}, u32[]{:S(2)}, u32[]{:S(2)}) collective-permute-start(f32[32,32,128]{2,1,0:T(8,128)S(1)} %constant_dynamic-update-slice_fusion.5.refs_10_), channel_id=1, source_target_pairs={{0,192},{64,0},{128,64},{192,128},{1,193},{65,1},{129,65},{193,129... | collective-permute-start | bytes 1572872 | tf_op jit(solution)/shard_map/ppermute | solution.py:237
  95.9 11.4 %collective-permute-start.18 = (f32[32,32,128]{2,1,0:T(8,128)S(1)}, f32[32,32,128]{2,1,0:T(8,128)S(1)}, u32[]{:S(2)}, u32[]{:S(2)}) collective-permute-start(f32[32,32,128]{2,1,0:T(8,128)S(1)} %constant_dynamic-update-slice_fusion.5.refs_10_), channel_id=1, source_target_pairs={{0,64},{64,128},{128,192},{192,0},{1,65},{65,129},{129,193},{193,1... | collective-permute-start | bytes 1572872 | tf_op jit(solution)/shard_map/ppermute | solution.py:237
  97.9 9.8 %collective-permute-start.4 = (f32[32,32,128]{2,1,0:T(8,128)S(1)}, f32[32,32,128]{2,1,0:T(8,128)S(1)}, u32[]{:S(2)}, u32[]{:S(2)}) collective-permute-start(f32[32,32,128]{2,1,0:T(8,128)S(1)} %constant_dynamic-update-slice_fusion.refs_0_), channel_id=1, source_target_pairs={{0,1},{1,0},{2,3},{3,2},{4,5},{5,4},{6,7},{7,6},{8,9},{9,8},{10,11... | collective-permute-start | bytes 1572872 | tf_op jit(solution)/shard_map/ppermute | solution.py:241
  102.9 11.2 %collective-permute-start.17 = (f32[32,32,128]{2,1,0:T(8,128)S(1)}, f32[32,32,128]{2,1,0:T(8,128)S(1)}, u32[]{:S(2)}, u32[]{:S(2)}) collective-permute-start(f32[32,32,128]{2,1,0:T(8,128)S(1)} %constant_dynamic-update-slice_fusion.5.refs_10_), channel_id=1, source_target_pairs={{0,1},{1,0},{2,3},{3,2},{4,5},{5,4},{6,7},{7,6},{8,9},{9,8},{10,11... | collective-permute-start | bytes 1572872 | tf_op jit(solution)/shard_map/ppermute | solution.py:241
  104.0 7.8 %collective-permute-start.11 = (f32[16,32,128]{2,1,0:T(8,128)S(1)}, f32[16,32,128]{2,1,0:T(8,128)S(1)}, u32[]{:S(2)}, u32[]{:S(2)}) collective-permute-start(f32[16,32,128]{2,1,0:T(8,128)S(1)} %slice.59), channel_id=1, source_target_pairs={{0,6},{2,0},{4,2},{6,4},{1,7},{3,1},{5,3},{7,5},{8,14},{10,8},{12,... | collective-permute-start | bytes 786440 | tf_op jit(solution)/shard_map/ppermute | solution.py:237
  107.2 6.9 %collective-permute-start.9 = (f32[16,32,128]{2,1,0:T(8,128)S(1)}, f32[16,32,128]{2,1,0:T(8,128)S(1)}, u32[]{:S(2)}, u32[]{:S(2)}) collective-permute-start(f32[16,32,128]{2,1,0:T(8,128)S(1)} %slice.58), channel_id=1, source_target_pairs={{0,2},{2,4},{4,6},{6,0},{1,3},{3,5},{5,7},{7,1},{8,10},{10,12},{12... | collective-permute-start | bytes 786440 | tf_op jit(solution)/shard_map/ppermute | solution.py:237
  107.3 7.3 %collective-permute-start.24 = (f32[16,32,128]{2,1,0:T(8,128)S(1)}, f32[16,32,128]{2,1,0:T(8,128)S(1)}, u32[]{:S(2)}, u32[]{:S(2)}) collective-permute-start(f32[16,32,128]{2,1,0:T(8,128)S(1)} %slice.64), channel_id=1, source_target_pairs={{0,192},{64,0},{128,64},{192,128},{1,193},{65,1},{129,65},{193,129... | collective-permute-start | bytes 786440 | tf_op jit(solution)/shard_map/ppermute | solution.py:237
  107.7 7.7 %collective-permute-start.22 = (f32[16,32,128]{2,1,0:T(8,128)S(1)}, f32[16,32,128]{2,1,0:T(8,128)S(1)}, u32[]{:S(2)}, u32[]{:S(2)}) collective-permute-start(f32[16,32,128]{2,1,0:T(8,128)S(1)} %slice.63), channel_id=1, source_target_pairs={{0,64},{64,128},{128,192},{192,0},{1,65},{65,129},{129,193},{193,1... | collective-permute-start | bytes 786440 | tf_op jit(solution)/shard_map/ppermute | solution.py:237
  111.7 3.6 %collective-permute-start.12 = (f32[16,32,128]{2,1,0:T(8,128)S(1)}, f32[16,32,128]{2,1,0:T(8,128)S(1)}, u32[]{:S(2)}, u32[]{:S(2)}) collective-permute-start(f32[16,32,128]{2,1,0:T(8,128)S(1)} %collective-permute-done.11.refs_8_), channel_id=1, source_target_pairs={{0,1},{1,0},{2,3},{3,2},{4,5},{5,4},{6,7},{7,6},{8,9},{9,8},{10,11... | collective-permute-start | bytes 786440 | tf_op jit(solution)/shard_map/ppermute | solution.py:241
  114.1 5.3 %collective-permute-start.8 = (f32[32,32,128]{2,1,0:T(8,128)S(1)}, f32[32,32,128]{2,1,0:T(8,128)S(1)}, u32[]{:S(2)}, u32[]{:S(2)}) collective-permute-start(f32[32,32,128]{2,1,0:T(8,128)S(1)} %collective-permute-done.7.refs_4_), channel_id=1, source_target_pairs={{0,1},{1,0},{2,3},{3,2},{4,5},{5,4},{6,7},{7,6},{8,9},{9,8},{10,11... | collective-permute-start | bytes 1572872 | tf_op jit(solution)/shard_map/ppermute | solution.py:241
  115.3 4.0 %collective-permute-start.6 = (f32[32,32,128]{2,1,0:T(8,128)S(1)}, f32[32,32,128]{2,1,0:T(8,128)S(1)}, u32[]{:S(2)}, u32[]{:S(2)}) collective-permute-start(f32[32,32,128]{2,1,0:T(8,128)S(1)} %collective-permute-done.5.refs_2_), channel_id=1, source_target_pairs={{0,1},{1,0},{2,3},{3,2},{4,5},{5,4},{6,7},{7,6},{8,9},{9,8},{10,11... | collective-permute-start | bytes 1572872 | tf_op jit(solution)/shard_map/ppermute | solution.py:241
  115.3 4.0 %collective-permute-start.21 = (f32[32,32,128]{2,1,0:T(8,128)S(1)}, f32[32,32,128]{2,1,0:T(8,128)S(1)}, u32[]{:S(2)}, u32[]{:S(2)}) collective-permute-start(f32[32,32,128]{2,1,0:T(8,128)S(1)} %collective-permute-done.20.refs_14_), channel_id=1, source_target_pairs={{0,1},{1,0},{2,3},{3,2},{4,5},{5,4},{6,7},{7,6},{8,9},{9,8},{10,11... | collective-permute-start | bytes 1572872 | tf_op jit(solution)/shard_map/ppermute | solution.py:241
  115.9 3.5 %collective-permute-start.19 = (f32[32,32,128]{2,1,0:T(8,128)S(1)}, f32[32,32,128]{2,1,0:T(8,128)S(1)}, u32[]{:S(2)}, u32[]{:S(2)}) collective-permute-start(f32[32,32,128]{2,1,0:T(8,128)S(1)} %collective-permute-done.18.refs_12_), channel_id=1, source_target_pairs={{0,1},{1,0},{2,3},{3,2},{4,5},{5,4},{6,7},{7,6},{8,9},{9,8},{10,11... | collective-permute-start | bytes 1572872 | tf_op jit(solution)/shard_map/ppermute | solution.py:241
  189.3 10.9 %all-to-all-start.5 = ((f32[8,1,128]{2,1,0:T(1,128)}), f32[8,1,128]{2,1,0:T(1,128)S(1)}, u32[]{:S(2)}, u32[]{:S(2)}) async-start(f32[8,1,128]{2,1,0:T(1,128)} %broadcast_in_dim.8), calls=%async_computation.5 | async-start | bytes 8192 | tf_op jit(solution)/shard_map/all_to_all | solution.py:252
  (11 other events, 54.9 us)

commit v2 on v1

--- a/solution.py
+++ b/solution.py
@@ -53,7 +53,7 @@
         out_ref[z, 15:16, :] = ones
 
 
-def joint_kernel(info, msg_ref, out_ref, hot, near, far, right):
+def joint_kernel(info, msg_ref, out_ref, hot, near, far, right, square):
     step = pl.program_id(0)
     z = info[1]
     core = info[3]
@@ -64,6 +64,7 @@
         near[...] = jnp.zeros_like(near)
         far[...] = jnp.zeros_like(far)
         right[...] = jnp.zeros_like(right)
+        square[...] = jnp.zeros_like(square)
 
     level = lax.broadcasted_iota(jnp.int32, (K, rows), 0).astype(F32).astype(BF16)
     for book in range(M):
@@ -71,6 +72,8 @@
         hot[book] = jnp.where(level == code, jnp.ones((), BF16), jnp.zeros((), BF16))
     mass = msg_ref[0, 8:9, :]
     weighted = msg_ref[0, 8:16, :] * mass
+    squares = weighted * msg_ref[0, 8:16, :]
+    square[...] += sum(squares[:, 128 * i : 128 * i + 128] for i in range(rows // 128))
     hi, mid, lo = split3(weighted)
     sums = jnp.concatenate([hi, mid, lo, jnp.zeros_like(lo)], axis=0).astype(BF16)
     mass = mass.astype(BF16)
@@ -102,34 +105,35 @@
             for h in range(2):
                 i = 2 * book + h
                 out_ref[14 + i // 8, 8 * (i % 8) : 8 * (i % 8) + 8, :] = part[:, 128 * h : 128 * h + 128]
+        for j in range(6):
+            out_ref[14, 8 * j : 8 * j + 1, :] = square[1 + j : 2 + j, :]
 
 
 def sum_kernel(in_ref, out_ref):
     total = in_ref[0]
     for i in range(1, in_ref.shape[0]):
         total = total + in_ref[i]
-    for i in range(out_ref.shape[0]):
-        out_ref[i] = total
+    for i in range(NZ):
+        for h in range(2):
+            out_ref[2 * i + h] = total[32 * h : 32 * h + 32]
 
 
 def solve_kernel(places, info, ridge, *refs):
     n = len(places)
     pieces = refs[:n]
     out_ref, mass_ref = refs[n : n + 2]
-    slab, high, low, wide, vec, sem = refs[n + 2 :]
+    slab, high, low, wide, vec, square, sem = refs[n + 2 :]
     y, z, x, core = (info[i] for i in range(4))
     copies = []
     for piece, (other, parts) in zip(pieces, places):
-        at_core = 1 - core if other else core
-        for at, half, dy, dx, sub, size in parts:
+        holder = 1 - core if other else core
+        for at, inner, outer in parts:
+            dy = inner + holder * (outer - inner)
+            dx = outer + holder * (inner - outer)
             chunk = ((y + dy) & 3) * 4 + ((x + dx) & 3)
-            row = pl.multiple_of(64 * chunk + 32 * half, 32)
+            row = pl.multiple_of(64 * chunk + 32 * holder, 32)
             copies.append(
-                pltpu.make_async_copy(
-                    piece.at[pl.ds(at, size)],
-                    slab.at[at_core, pl.ds(sub, size), pl.ds(row, 32), :],
-                    sem,
-                )
+                pltpu.make_async_copy(piece.at[pl.ds(at, 16)], slab.at[:, pl.ds(row, 32), :], sem)
             )
     for copy in copies:
         copy.start()
@@ -145,24 +149,28 @@
         for s in range(3):
             for h in range(2):
                 for c in range(2):
-                    keep(3 * p + s, 128 * c, 128 * h, slab[c, p, 128 * (2 * s + h) : 128 * (2 * s + h) + 128, :])
+                    keep(3 * p + s, 128 * c, 128 * h, slab[2 * p + c, 128 * (2 * s + h) : 128 * (2 * s + h) + 128, :])
         return 0
 
     lax.fori_loop(0, M, build, 0)
 
     def build_far(p, _):
         for c in range(2):
-            keep(24 + p, 128 * c, 0, slab[c, p, 768:896, :])
-            keep(24 + p, 128 * c, 128, slab[c, p + 4, 768:896, :])
+            keep(24 + p, 128 * c, 0, slab[2 * p + c, 768:896, :])
+            keep(24 + p, 128 * c, 128, slab[2 * p + 8 + c, 768:896, :])
         return 0
 
     lax.fori_loop(0, 4, build_far, 0)
 
     group = 4 * y + x
-    start, remain, direction, precond = 0, 1, 2, 3
+    start, remain, direction, precond, right = 0, 1, 2, 3, 4
+    square[...] = jnp.zeros_like(square)
     for i in range(16):
-        tile = slab[group & 1, group >> 1, 896 + 8 * i : 904 + 8 * i, :]
+        tile = slab[group, 896 + 8 * i : 904 + 8 * i, :]
         vec[remain, :, 128 * i : 128 * i + 128] = tile
+        vec[right, :, 128 * i : 128 * i + 128] = tile
+        if i < 6:
+            square[1 + i : 2 + i, :] = tile[0:1]
     counts = vec[remain, 7:8, :]
     mass = jnp.sum(counts[:, 0:K], axis=1, keepdims=True)
     mass_ref[...] = jnp.broadcast_to(mass, mass_ref.shape)
@@ -173,8 +181,7 @@
     vec[direction] = scaled
     first_inner = jnp.sum(vec[remain] * scaled, axis=1, keepdims=True)
 
-    def step(_, inner):
-        d = vec[direction]
+    def operator(d):
         hi, mid, lo = split3(d)
         wide[...] = jnp.concatenate([hi, mid, lo, jnp.zeros_like(lo)], axis=0).astype(BF16)
         image = []
@@ -189,7 +196,11 @@
                 part = wide[:, K * q : K * q + K]
                 total = total + dot(part, high[block], dims) + dot(part, low[block], dims)
             image.append(total[0:8] + total[8:16] + total[16:24])
-        image = jnp.concatenate(image, axis=1) + vec[precond] * d
+        return jnp.concatenate(image, axis=1) + vec[precond] * d
+
+    def step(_, inner):
+        d = vec[direction]
+        image = operator(d)
         alpha = inner / jnp.sum(d * image, axis=1, keepdims=True)
         vec[start] = vec[start] + alpha * d
         r = vec[remain] - alpha * image
@@ -202,9 +213,14 @@
     lax.fori_loop(0, ITERS, step, first_inner)
     for i in range(16):
         out_ref[6 * i : 6 * i + 6, :] = vec[start, 1:7, 128 * i : 128 * i + 128]
-
-
-def residual_kernel(books_ref, codes_ref, mass_ref, vectors_ref, out_ref, table_ref, part_ref, left, hot):
+    c = vec[start]
+    fitted = c * (2.0 * vec[right] - operator(c) + lam * c)
+    left = jnp.sum(square[...], axis=1, keepdims=True) - jnp.sum(fitted, axis=1, keepdims=True)
+    left = jnp.sum(left[1:7], axis=0, keepdims=True)
+    out_ref[96:104, :] = jnp.broadcast_to(left, (8, 128))
+
+
+def residual_kernel(books_ref, mass_ref, codes_ref, vectors_ref, out_ref, table_ref, part_ref, left, hot):
     step = pl.program_id(0)
 
     @pl.when(step == 0)
@@ -217,7 +233,10 @@
         for m in range(M):
             for t, piece in enumerate(split3(table_ref[m])):
                 left[D * t : D * t + D, K * m : K * m + K] = piece.astype(BF16)
-        part_ref[...] = jnp.zeros_like(part_ref)
+        total = books_ref[0, 96:97, :]
+        for k in range(1, 16):
+            total = total + books_ref[k, 96:97, :]
+        part_ref[...] = jnp.broadcast_to(total / (mass_ref[0:1, :] * D), part_ref.shape)
 
     cols = codes_ref.shape[1]
     level = lax.broadcasted_iota(jnp.int32, (K, cols), 0).astype(F32).astype(BF16)
@@ -226,26 +245,28 @@
         hot[K * m : K * m + K, :] = jnp.where(level == code, jnp.ones((), BF16), jnp.zeros((), BF16))
     recon = dot(left[...], hot[...], NN)
     recon = recon[0:D] + recon[D : 2 * D] + recon[2 * D : 3 * D]
-    residual = vectors_ref[...] - recon
-    out_ref[...] = residual
-    total = jnp.sum(residual * residual, axis=0, keepdims=True) * mass_ref[...]
-    part_ref[...] += jnp.broadcast_to(jnp.sum(total, axis=1, keepdims=True), part_ref.shape)
-
-
-def shift(array, axis, by):
-    size = lax.axis_size(axis)
-    return lax.ppermute(array, axis, [(i, (i + by) % size) for i in range(size)])
+    out_ref[...] = vectors_ref[...] - recon
+
+
+def shift(array, stage, by):
+    pairs = []
+    for y in range(NY):
+        for x in range(NX):
+            for c in range(2):
+                ty, tx = ((y + by) % NY, x) if (c == 0) == (stage == 0) else (y, (x + by) % NX)
+                pairs.append(((y * NX + x) * 2 + c, (ty * NX + tx) * 2 + c))
+    return lax.ppermute(array, ("y", "x", "c"), pairs)
 
 
 def swap(array):
     return lax.ppermute(array, "c", [(0, 1), (1, 0)])
 
 
-def ring(array, axis):
-    up = shift(array, axis, 1)
-    down = shift(array, axis, -1)
+def ring(array, stage):
+    up = shift(array, stage, 1)
+    down = shift(array, stage, -1)
     half = array.shape[0] // 2
-    return up, down, shift(up[:half], axis, 1), shift(down[half:], axis, -1)
+    return up, down, shift(up[:half], stage, 1), shift(down[half:], stage, -1)
 
 
 def spread(array, axes):
@@ -278,6 +299,7 @@
             pltpu.VMEM((3, 128, K), F32),
             pltpu.VMEM((128, 128), F32),
             pltpu.VMEM((M, 32, K), F32),
+            pltpu.VMEM((8, 128), F32),
         ],
         compiler_params=params(dimension_semantics=("arbitrary",)),
         name="joint",
@@ -285,47 +307,41 @@
     slab = spread(slab, ("y", "x"))
     chunk = pl.pallas_call(
         sum_kernel,
-        out_shape=jax.ShapeDtypeStruct((NZ, 64, 128), F32),
+        out_shape=jax.ShapeDtypeStruct((16, 32, 128), F32),
         in_specs=[VMEM],
         out_specs=VMEM,
         compiler_params=params(),
         name="chunk",
     )(slab)
-    line = spread(chunk, "z")
-    pieces = []
-    for half, first, second in ((0, "y", "x"), (1, "x", "y")):
-        own = line[:, 32 * half : 32 * half + 32]
-        wide = jnp.concatenate([own, *ring(own, first)], axis=0)
-        pieces.extend(zip(("own", "up", "down", "far0", "far1"), (half,) * 5, (wide, *ring(wide, second))))
+    line = spread(chunk, ("z", "c"))
+    wide = jnp.concatenate([line, *ring(line, 0)], axis=0)
+    offsets = (0, -1, 1, 2)
     places, arrays = [], []
-    for name, half, array in pieces:
-        parts = []
-        units = {"far0": (0, 1), "far1": (2, 3)}.get(name, (0, 1, 2, 3))
-        outer = {"own": 0, "up": -1, "down": 1}.get(name, 2)
-        for n, u in enumerate(units):
-            inner = (0, -1, 1, 2)[u]
-            dy, dx = (inner, outer) if half == 0 else (outer, inner)
-            parts.append((8 * n, half, dy, dx, 0, 8))
+    for array, outer, units in zip(
+        (wide, *ring(wide, 1)), (0, -1, 1, 2, 2), ((0, 1, 2, 3),) * 3 + ((0, 1), (2, 3))
+    ):
+        parts = [(16 * n, offsets[u], outer) for n, u in enumerate(units)]
         for other in (False, True):
             places.append((other, parts))
             arrays.append(swap(array) if other else array)
     columns, total_mass = pl.pallas_call(
         functools.partial(solve_kernel, places),
-        out_shape=(jax.ShapeDtypeStruct((D, 128), F32), jax.ShapeDtypeStruct((8, 128), F32)),
+        out_shape=(jax.ShapeDtypeStruct((104, 128), F32), jax.ShapeDtypeStruct((8, 128), F32)),
         in_specs=[SMEM, SMEM] + [ANY] * len(arrays),
         out_specs=(VMEM, VMEM),
         scratch_shapes=[
-            pltpu.VMEM((2, NZ, 1024, 128), F32),
+            pltpu.VMEM((16, 1024, 128), F32),
             pltpu.VMEM((28, K, K), BF16),
             pltpu.VMEM((28, K, K), BF16),
             pltpu.VMEM((32, M * K), BF16),
-            pltpu.VMEM((4, 8, M * K), F32),
+            pltpu.VMEM((5, 8, M * K), F32),
+            pltpu.VMEM((8, 128), F32),
             pltpu.SemaphoreType.DMA,
         ],
         compiler_params=params(),
         name="solve",
     )(info, ridge, *arrays)
-    books = spread(jnp.broadcast_to(columns[None], (16, D, 128)), ("y", "x"))
+    books = spread(jnp.broadcast_to(columns[None], (16, *columns.shape)), ("y", "x"))
     lanes = 256
     residual, table, part = pl.pallas_call(
         residual_kernel,
@@ -336,9 +352,9 @@
             jax.ShapeDtypeStruct((8, 128), F32),
         ),
         in_specs=[
-            pl.BlockSpec((16, D, 128), lambda i: (0, 0, 0)),
+            pl.BlockSpec((16, 104, 128), lambda i: (0, 0, 0)),
+            pl.BlockSpec((8, 128), lambda i: (0, 0)),
             pl.BlockSpec((M, lanes), lambda i: (0, i)),
-            pl.BlockSpec((1, lanes), lambda i: (0, i)),
             pl.BlockSpec((D, lanes), lambda i: (0, i)),
         ],
         out_specs=(
@@ -349,13 +365,8 @@
         scratch_shapes=[pltpu.VMEM((3 * D, M * K), BF16), pltpu.VMEM((M * K, lanes), BF16)],
         compiler_params=params(dimension_semantics=("arbitrary",)),
         name="residual",
-    )(books, codes, mass, vectors)
-    plane = spread(jnp.broadcast_to(part[:1], (16, 128)), ("y", "x"))
-    plane = jnp.sum(plane, axis=0, keepdims=True)
-    total = spread(jnp.broadcast_to(plane, (NZ, 128)), "z")
-    total = jnp.sum(total[:, 0])
-    distortion = total / (total_mass[0, 0] * D)
-    return (table.transpose(0, 2, 1), residual.T, distortion)
+    )(books, total_mass, codes, vectors)
+    return (table.transpose(0, 2, 1), residual.T, part[0, 0])
 
 
 def solution(mesh):

time: 203 us -> 185 us (0.911)
  starting transfers between devices: 22.5 us -> 9.05 us
  blocking collectives: 84.6 us -> 75.6 us
  waiting for transfers between devices: 27.8 us -> 32.6 us
  Pallas kernels: 58.2 us -> 60.9 us
  between operations: 4.01 us -> 1.44 us
    ppermute x16 -> x8, waiting for transfers between devices: 18.7 us -> 31.4 us  [shift(): return lax.ppermute(array, ('y', 'x', 'c'), pairs)]
    ppermute x16 -> x8, starting transfers between devices: 17.9 us -> 8.54 us  [shift(): return lax.ppermute(array, ('y', 'x', 'c'), pairs)]
    all_to_all x5 -> x4, blocking collectives: 84.6 us -> 75.6 us  [spread(): return lax.all_to_all(array, axes, 0, 0, tiled=True)]
    all_to_all x1 -> x0, waiting for transfers between devices: 6.42 us -> none  [spread(): return lax.all_to_all(array, axes, 0, 0, tiled=True)]
    all_to_all x1 -> x0, starting transfers between devices: 3.32 us -> none  [spread(): return lax.all_to_all(array, axes, 0, 0, tiled=True)]
    pallas_call x1, Pallas kernels: 34.4 us -> 37.3 us  [body(): pl.pallas_call(functools.partial(solve_kernel, places), out_shape=(jax.Sh...]
  transfers between devices with their start and end apart: 27 -> 13, of which waited for: 11 -> 6; matrix products, arithmetic and copies ran while one was open for 0% -> 0% of each run, Pallas kernels for 0% -> 0%
where the time goes in v2:
time: 185 us; the launch traced here: 184 us
  blocking collectives  75.6 us (41%)
  Pallas kernels  60.9 us (33%)
  waiting for transfers between devices  32.6 us (18%)
  starting transfers between devices  9.05 us (5%)
  local copies, waits for them, and re-layouts  3.71 us (2%)
    all_to_all x4, blocking collectives, spread(): return lax.all_to_all(array, axes, 0, 0, tiled=True)  75.6 us
    pallas_call x1, Pallas kernels, body(): pl.pallas_call(functools.partial(solve_kernel, places), out_shape=(jax.Sh...  37.3 us
    ppermute x8, waiting for transfers between devices, shift(): return lax.ppermute(array, ('y', 'x', 'c'), pairs)  31.4 us
    pallas_call x1, Pallas kernels, body(): pl.pallas_call(joint_kernel, grid=(NZ,), out_shape=jax.ShapeDtypeStruct((...  19.7 us
    ppermute x8, starting transfers between devices, shift(): return lax.ppermute(array, ('y', 'x', 'c'), pairs)  8.54 us
  transfers between devices with their start and end apart: 13, of which 6 were waited for; matrix products, arithmetic and copies ran while one was open for 0% of the time, Pallas kernels for 0%

profile of v2, /device:TPU:2, one launch (start us, length us, event | category | flops | bytes accessed | tf_op | source)
XLA Modules:
  0.0 184.1 jit_solution(8970142000599494121)
XLA Ops:
  0.6 0.7 reshape.14
  1.4 1.0 copy-done
  2.4 0.7 message.1
  3.1 25.8 %all_to_all.20.msg_ref = f32[8,16,1024]{2,1,0:T(8,128)S(1)} all-to-all(f32[8,16,1024]{2,1,0:T(8,128)S(1)} %message.1), channel_id=1, replica_groups=mesh['y'=4,'z'=8,'x'=4,'c'=2] {'z'}, dimensions={0} | all-to-all | bytes 1048576 | tf_op jit(solution)/shard_map/all_to_all | solution.py:273
  28.8 19.7 %joint.1 = f32[16,64,128]{2,1,0:T(8,128)S(1)} custom-call(s32[4]{0:T(128)S(1)} %pad_add_fusion.info, f32[8,16,1024]{2,1,0:T(8,128)S(1)} %all_to_all.20.msg_ref), custom_call_target="tpu_custom_call" | custom-call | tf_op jit(solution)/shard_map/joint/pallas_call | solution.py:291
  48.5 16.0 %all_to_all.21.in_ref = f32[16,64,128]{2,1,0:T(8,128)S(1)} all-to-all(f32[16,64,128]{2,1,0:T(8,128)S(1)} %joint.1), channel_id=1, replica_groups=mesh['y'=4,'z'=8,'x'=4,'c'=2] {'y','x'}, dimensions={0} | all-to-all | bytes 1048576 | tf_op jit(solution)/shard_map/all_to_all | solution.py:273
  64.6 13.7 %all_to_all.22 = f32[16,32,128]{2,1,0:T(8,128)S(1)} all-to-all(f32[16,32,128]{2,1,0:T(8,128)S(1)} %chunk.1), channel_id=1, replica_groups=mesh['y'=4,'z'=8,'x'=4,'c'=2] {'z','c'}, dimensions={0} | all-to-all | bytes 524288 | tf_op jit(solution)/shard_map/all_to_all | solution.py:273
  78.3 0.9 collective-permute-start.1
  79.1 1.2 collective-permute-start
  80.3 4.3 %collective-permute-done.1 = f32[16,32,128]{2,1,0:T(8,128)S(1)} collective-permute-done((f32[16,32,128]{2,1,0:T(8,128)S(1)}, f32[16,32,128]{2,1,0:T(8,128)S(1)}, u32[]{:S(2)}, u32[]{:S(2)}) %collective-permute-start.1) | collective-permute-done | bytes 262176 | tf_op jit(solution)/shard_map/ppermute | solution.py:258
  84.7 2.1 %collective-permute-start.3 = (f32[8,32,128]{2,1,0:T(8,128)S(1)}, f32[8,32,128]{2,1,0:T(8,128)S(1)}, u32[]{:S(2)}, u32[]{:S(2)}) collective-permute-start(f32[8,32,128]{2,1,0:T(8,128)S(1)} %slice.21), channel_id=1, source_target_pairs={{0,192},{1,7},{2,194},{3,1},{4,196},{5,3},{6,198},{7,5},{64,0},{65... | collective-permute-start | bytes 393224 | tf_op jit(solution)/shard_map/ppermute | solution.py:258
  87.0 6.1 %collective-permute-done.2 = f32[8,32,128]{2,1,0:T(8,128)S(1)} collective-permute-done((f32[8,32,128]{2,1,0:T(8,128)S(1)}, f32[8,32,128]{2,1,0:T(8,128)S(1)}, u32[]{:S(2)}, u32[]{:S(2)}) %collective-permute-start.2) | collective-permute-done | bytes 131104 | tf_op jit(solution)/shard_map/ppermute | solution.py:258
  93.1 1.5 collective-permute-start.7
  95.2 12.8 %collective-permute-done.7.refs_4_ = f32[64,32,128]{2,1,0:T(8,128)S(1)} collective-permute-done((f32[64,32,128]{2,1,0:T(8,128)S(1)}, f32[64,32,128]{2,1,0:T(8,128)S(1)}, u32[]{:S(2)}, u32[]{:S(2)}) %collective-permute-start.7) | collective-permute-done | bytes 1048608 | tf_op jit(solution)/shard_map/ppermute | solution.py:258
  108.0 1.5 collective-permute-start.11
  109.6 0.7 collective-permute-start.9
  110.8 6.5 %collective-permute-done.11.refs_8_ = f32[32,32,128]{2,1,0:T(8,128)S(1)} collective-permute-done((f32[32,32,128]{2,1,0:T(8,128)S(1)}, f32[32,32,128]{2,1,0:T(8,128)S(1)}, u32[]{:S(2)}, u32[]{:S(2)}) %collective-permute-start.11) | collective-permute-done | bytes 524320 | tf_op jit(solution)/shard_map/ppermute | solution.py:258
  117.3 1.7 collective-permute-done.9.refs_6_
  119.6 1.2 collective-permute-done.10.refs_7_
  120.9 1.0 copy-done.4
  121.9 1.0 copy-done.5
  122.8 37.3 %solve.1 = (f32[104,128]{1,0:T(8,128)S(1)}, f32[8,128]{1,0:T(8,128)S(1)}) custom-call(s32[4]{0:T(128)S(1)} %pad_add_fusion.info, f32[1]{0:T(128)S(6)} %copy.11.ridge, f32[64,32,128]{2,1,0:T(8,128)S(1)} %constant_dynamic-update-slice_fusion.refs_0_, f32[64,32,128]{2,1,0:T(8,128)S(1)} %collective-permute-done.4.refs_1_, ...), custom_call_target="tpu_custom_call" | custom-call | tf_op jit(solution)/shard_map/solve/pallas_call | solution.py:327
  160.3 20.1 %all_to_all.23.books_ref = f32[16,104,128]{2,1,0:T(8,128)S(1)} all-to-all(f32[16,104,128]{2,1,0:T(8,128)S(1)} %broadcast_in_dim.2), channel_id=1, replica_groups=mesh['y'=4,'z'=8,'x'=4,'c'=2] {'y','x'}, dimensions={0} | all-to-all | bytes 1703936 | tf_op jit(solution)/shard_map/all_to_all | solution.py:273
  180.4 3.2 %residual.1 = (f32[96,1024]{1,0:T(8,128)}, f32[8,96,256]{2,1,0:T(8,128)}, f32[8,128]{1,0:T(8,128)S(1)}) custom-call(f32[16,104,128]{2,1,0:T(8,128)S(1)} %all_to_all.23.books_ref, f32[8,128]{1,0:T(8,128)S(1)} %get-tuple-element.9.mass_ref, s32[8,1024]{1,0:T(8,128)S(1)} %bitcast.13, f32[96,1024]{1,0:T(8,128)S(1)} %bitcast.11), custom_call_target="tpu_custom_call" | custom-call | tf_op jit(solution)/shard_map/residual/pallas_call | solution.py:346
  (36 shorter events, 2.1 us)
Async XLA Ops:
  0.6 0.8 copy-start.2
  1.4 1.0 copy-start
  78.3 6.4 %collective-permute-start.1 = (f32[16,32,128]{2,1,0:T(8,128)S(1)}, f32[16,32,128]{2,1,0:T(8,128)S(1)}, u32[]{:S(2)}, u32[]{:S(2)}) collective-permute-start(f32[16,32,128]{2,1,0:T(8,128)S(1)} %all_to_all.22), channel_id=1, source_target_pairs={{0,192},{1,7},{2,194},{3,1},{4,196},{5,3},{6,198},{7,5},{64,0},{65... | collective-permute-start | bytes 786440 | tf_op jit(solution)/shard_map/ppermute | solution.py:258
  79.1 7.7 %collective-permute-start = (f32[16,32,128]{2,1,0:T(8,128)S(1)}, f32[16,32,128]{2,1,0:T(8,128)S(1)}, u32[]{:S(2)}, u32[]{:S(2)}) collective-permute-start(f32[16,32,128]{2,1,0:T(8,128)S(1)} %all_to_all.22), channel_id=1, source_target_pairs={{0,64},{1,3},{2,66},{3,5},{4,68},{5,7},{6,70},{7,1},{64,128},{65,6... | collective-permute-start | bytes 786440 | tf_op jit(solution)/shard_map/ppermute | solution.py:258
  84.7 8.4 %collective-permute-start.3 = (f32[8,32,128]{2,1,0:T(8,128)S(1)}, f32[8,32,128]{2,1,0:T(8,128)S(1)}, u32[]{:S(2)}, u32[]{:S(2)}) collective-permute-start(f32[8,32,128]{2,1,0:T(8,128)S(1)} %slice.21), channel_id=1, source_target_pairs={{0,192},{1,7},{2,194},{3,1},{4,196},{5,3},{6,198},{7,5},{64,0},{65... | collective-permute-start | bytes 393224 | tf_op jit(solution)/shard_map/ppermute | solution.py:258
  86.8 6.3 %collective-permute-start.2 = (f32[8,32,128]{2,1,0:T(8,128)S(1)}, f32[8,32,128]{2,1,0:T(8,128)S(1)}, u32[]{:S(2)}, u32[]{:S(2)}) collective-permute-start(f32[8,32,128]{2,1,0:T(8,128)S(1)} %slice.20), channel_id=1, source_target_pairs={{0,64},{1,3},{2,66},{3,5},{4,68},{5,7},{6,70},{7,1},{64,128},{65,6... | collective-permute-start | bytes 393224 | tf_op jit(solution)/shard_map/ppermute | solution.py:258
  93.1 14.9 %collective-permute-start.7 = (f32[64,32,128]{2,1,0:T(8,128)S(1)}, f32[64,32,128]{2,1,0:T(8,128)S(1)}, u32[]{:S(2)}, u32[]{:S(2)}) collective-permute-start(f32[64,32,128]{2,1,0:T(8,128)S(1)} %constant_dynamic-update-slice_fusion.refs_0_), channel_id=1, source_target_pairs={{0,6},{1,193},{2,0},{3,195},{4,2},{5,197},{6,4},{7,199},{64,70},{6... | collective-permute-start | bytes 3145736 | tf_op jit(solution)/shard_map/ppermute | solution.py:258
  94.6 14.9 %collective-permute-start.5 = (f32[64,32,128]{2,1,0:T(8,128)S(1)}, f32[64,32,128]{2,1,0:T(8,128)S(1)}, u32[]{:S(2)}, u32[]{:S(2)}) collective-permute-start(f32[64,32,128]{2,1,0:T(8,128)S(1)} %constant_dynamic-update-slice_fusion.refs_0_), channel_id=1, source_target_pairs={{0,2},{1,65},{2,4},{3,67},{4,6},{5,69},{6,0},{7,71},{64,66},{65,12... | collective-permute-start | bytes 3145736 | tf_op jit(solution)/shard_map/ppermute | solution.py:258
  95.2 24.4 %collective-permute-start.4 = (f32[64,32,128]{2,1,0:T(8,128)S(1)}, f32[64,32,128]{2,1,0:T(8,128)S(1)}, u32[]{:S(2)}, u32[]{:S(2)}) collective-permute-start(f32[64,32,128]{2,1,0:T(8,128)S(1)} %constant_dynamic-update-slice_fusion.refs_0_), channel_id=1, source_target_pairs={{0,1},{1,0},{2,3},{3,2},{4,5},{5,4},{6,7},{7,6},{8,9},{9,8},{10,11... | collective-permute-start | bytes 3145736 | tf_op jit(solution)/shard_map/ppermute | solution.py:262
  108.0 2.3 %copy-start.3 = (f32[64,32,128]{2,1,0:T(8,128)}, f32[64,32,128]{2,1,0:T(8,128)S(1)}, u32[]{:S(2)}) copy-start(f32[64,32,128]{2,1,0:T(8,128)S(1)} %collective-permute-done.7.refs_4_) | copy-start | bytes 3145732
  108.0 9.3 %collective-permute-start.11 = (f32[32,32,128]{2,1,0:T(8,128)S(1)}, f32[32,32,128]{2,1,0:T(8,128)S(1)}, u32[]{:S(2)}, u32[]{:S(2)}) collective-permute-start(f32[32,32,128]{2,1,0:T(8,128)S(1)} %slice.23), channel_id=1, source_target_pairs={{0,6},{1,193},{2,0},{3,195},{4,2},{5,197},{6,4},{7,199},{64,70},{6... | collective-permute-start | bytes 1572872 | tf_op jit(solution)/shard_map/ppermute | solution.py:258
  109.6 9.4 %collective-permute-start.9 = (f32[32,32,128]{2,1,0:T(8,128)S(1)}, f32[32,32,128]{2,1,0:T(8,128)S(1)}, u32[]{:S(2)}, u32[]{:S(2)}) collective-permute-start(f32[32,32,128]{2,1,0:T(8,128)S(1)} %slice.22), channel_id=1, source_target_pairs={{0,2},{1,65},{2,4},{3,67},{4,6},{5,69},{6,0},{7,71},{64,66},{65,12... | collective-permute-start | bytes 1572872 | tf_op jit(solution)/shard_map/ppermute | solution.py:258
  110.3 10.6 %collective-permute-start.8 = (f32[64,32,128]{2,1,0:T(8,128)S(1)}, f32[64,32,128]{2,1,0:T(8,128)S(1)}, u32[]{:S(2)}, u32[]{:S(2)}) collective-permute-start(f32[64,32,128]{2,1,0:T(8,128)S(1)} %collective-permute-done.7.refs_4_), channel_id=1, source_target_pairs={{0,1},{1,0},{2,3},{3,2},{4,5},{5,4},{6,7},{7,6},{8,9},{9,8},{10,11... | collective-permute-start | bytes 3145736 | tf_op jit(solution)/shard_map/ppermute | solution.py:262
  110.3 10.6 %collective-permute-start.6 = (f32[64,32,128]{2,1,0:T(8,128)S(1)}, f32[64,32,128]{2,1,0:T(8,128)S(1)}, u32[]{:S(2)}, u32[]{:S(2)}) collective-permute-start(f32[64,32,128]{2,1,0:T(8,128)S(1)} %collective-permute-done.5.refs_2_), channel_id=1, source_target_pairs={{0,1},{1,0},{2,3},{3,2},{4,5},{5,4},{6,7},{7,6},{8,9},{9,8},{10,11... | collective-permute-start | bytes 3145736 | tf_op jit(solution)/shard_map/ppermute | solution.py:262
  117.3 2.3 %collective-permute-start.12 = (f32[32,32,128]{2,1,0:T(8,128)S(1)}, f32[32,32,128]{2,1,0:T(8,128)S(1)}, u32[]{:S(2)}, u32[]{:S(2)}) collective-permute-start(f32[32,32,128]{2,1,0:T(8,128)S(1)} %collective-permute-done.11.refs_8_), channel_id=1, source_target_pairs={{0,1},{1,0},{2,3},{3,2},{4,5},{5,4},{6,7},{7,6},{8,9},{9,8},{10,11... | collective-permute-start | bytes 1572872 | tf_op jit(solution)/shard_map/ppermute | solution.py:262
  119.0 1.9 %collective-permute-start.10 = (f32[32,32,128]{2,1,0:T(8,128)S(1)}, f32[32,32,128]{2,1,0:T(8,128)S(1)}, u32[]{:S(2)}, u32[]{:S(2)}) collective-permute-start(f32[32,32,128]{2,1,0:T(8,128)S(1)} %collective-permute-done.9.refs_6_), channel_id=1, source_target_pairs={{0,1},{1,0},{2,3},{3,2},{4,5},{5,4},{6,7},{7,6},{8,9},{9,8},{10,11... | collective-permute-start | bytes 1572872 | tf_op jit(solution)/shard_map/ppermute | solution.py:262
  120.9 1.0 copy-start.4
  121.9 1.0 copy-start.5
  160.3 20.1 %copy-start.1 = (f32[1024,96]{0,1:T(8,128)S(1)}, f32[1024,96]{0,1:T(8,128)}, u32[]{:S(2)}) copy-start(f32[1024,96]{0,1:T(8,128)} %param.4) | copy-start | bytes 1179652

commit v3 on v2

v3 whole, which is shorter than its diff:
```python
import functools

import jax
import jax.numpy as jnp
from jax import lax
from jax.experimental import pallas as pl
from jax.experimental.pallas import tpu as pltpu
from jax.sharding import Mesh
from jax.sharding import PartitionSpec as P

K = 256
M = 8
D = 96
ITERS = 8
NY, NZ, NX = 4, 8, 4
DP = ("y", "z", "x")
F32 = jnp.float32
BF16 = jnp.bfloat16
NT = (((1,), (1,)), ((), ()))
NN = (((1,), (0,)), ((), ()))


def dot(a, b, dims):
    return lax.dot_general(a, b, dims, preferred_element_type=F32)


def split3(a):
    hi = a.astype(BF16).astype(F32)
    rest = a - hi
    mid = rest.astype(BF16).astype(F32)
    return hi, mid, rest - mid


def params(mib, **more):
    return pltpu.CompilerParams(vmem_limit_bytes=mib << 20, **more)


VMEM = pl.BlockSpec(memory_space=pltpu.VMEM)
SMEM = pl.BlockSpec(memory_space=pltpu.SMEM)
ANY = pl.BlockSpec(memory_space=pl.ANY)


def message_kernel(info, codes_ref, mass_ref, vectors_ref, *out_refs):
    z = info[1]
    core = info[3]

    def half(a):
        n = a.shape[1] // 2
        return jnp.where(core == 0, a[:, :n], a[:, n:])

    codes = codes_ref[...].astype(F32)
    mass = mass_ref[...]
    for d, out_ref in enumerate(out_refs):
        keep = half if d == 4 else (lambda a: a)
        to = (z + d * (1 - 2 * core)) & 7
        out_ref[0:8, :] = keep(codes)
        for c in range(2):
            out_ref[8 + 8 * c : 9 + 8 * c, :] = keep(mass)
            for j in range(6):
                row = keep(vectors_ref[pl.ds(12 * to + 6 * c + j, 1), :])
                out_ref[9 + 8 * c + j : 10 + 8 * c + j, :] = row
            out_ref[15 + 8 * c : 16 + 8 * c, :] = keep(jnp.ones_like(mass))


def joint_kernel(count, first, last, info, *refs):
    messages, refs = refs[:count], refs[count:]
    if not first:
        before, refs = refs[:4], refs[4:]
    if last:
        out_ref, refs = refs[0], refs[1:]
    near, far, right, square, left, *hots = refs
    z = info[1]
    core = info[3]
    for n, ref in enumerate((near, far, right, square)):
        ref[...] = jnp.zeros_like(ref) if first else before[n][...]
    wide = hots[0].shape[2]
    level = lax.broadcasted_iota(jnp.int32, (K, wide), 0).astype(F32).astype(BF16)
    low = z & 3
    levels = lax.broadcasted_iota(jnp.int32, (128, wide), 0)
    based = (levels + 128 * core).astype(F32).astype(BF16)
    sided = (levels + 128 * (z >> 2)).astype(F32).astype(BF16)
    turn = 0
    for message in messages:
        for at in range(0, message.shape[1], wide):
            hot, turn = hots[turn % 2], turn + 1
            lanes = pl.ds(at, wide)
            for s in range(M):
                code = message[pl.ds((z + s) & 7, 1), lanes].astype(BF16)
                hot[s] = jnp.where(level == code, jnp.ones((), BF16), jnp.zeros((), BF16))
            own = message[pl.ds(pl.multiple_of(8 + 8 * core, 8), 8), lanes]
            weighted = own * own_mass(message, lanes)
            squares = weighted * own
            square[...] += sum(squares[:, 128 * i : 128 * i + 128] for i in range(wide // 128))
            hi, mid, lo = split3(weighted)
            mass = own_mass(message, lanes).astype(BF16)
            part = left.at[turn % 2]
            part[0:128] = jnp.where(based == message[pl.ds(z, 1), lanes].astype(BF16), mass, jnp.zeros((), BF16))
            part[128:160] = jnp.concatenate([hi, mid, lo, jnp.zeros_like(lo)], axis=0).astype(BF16)
            part[160:288] = jnp.where(based == message[pl.ds(low, 1), lanes].astype(BF16), mass, jnp.zeros((), BF16))
            code = message[pl.ds(low + 4, 1), lanes].astype(BF16)
            part[288:416] = jnp.where(sided == code, jnp.ones((), BF16), jnp.zeros((), BF16))
            for s in range(M):
                if 1 <= s <= 3:
                    near[s - 1] += dot(part[0:160], hot[s], NT)
                else:
                    right[s] += dot(part[128:160], hot[s], NT)
            far[...] += dot(part[160:288], part[288:416], NT)
    if last:
        for s in range(3):
            for h in range(2):
                t = 2 * s + h
                out_ref[2 * t] = near[s, 0:64, 128 * h : 128 * h + 128]
                out_ref[2 * t + 1] = near[s, 64:128, 128 * h : 128 * h + 128]
        out_ref[12] = far[0:64, :]
        out_ref[13] = far[64:128, :]
        for s in range(M):
            total = near[s - 1, 128:160] if 1 <= s <= 3 else right[s]
            total = total[0:8] + total[8:16] + total[16:24]
            for h in range(2):
                i = 2 * ((z + s) & 7) + h
                row = pl.multiple_of(8 * (i & 7), 8)
                out_ref[14 + (i >> 3), pl.ds(row, 8), :] = total[:, 128 * h : 128 * h + 128]
        for j in range(6):
            out_ref[14, 8 * j : 8 * j + 1, :] = square[1 + j : 2 + j, :]


def own_mass(message, lanes):
    return message[8:9, lanes]


def joint(info, messages, before, last):
    shapes = [(3, 160, K), (128, 128), (M, 32, K), (8, 128)]
    state = [jax.ShapeDtypeStruct(a, F32) for a in shapes]
    wide = 512
    scratch = [pltpu.VMEM((2, 416, wide), BF16), pltpu.VMEM((M, K, wide), BF16), pltpu.VMEM((M, K, wide), BF16)]
    if last:
        scratch = [pltpu.VMEM(a, F32) for a in shapes] + scratch
    count = len(messages)
    return pl.pallas_call(
        functools.partial(joint_kernel, count, not before, last),
        out_shape=jax.ShapeDtypeStruct((16, 64, 128), F32) if last else state,
        in_specs=[SMEM] + [VMEM] * (count + len(before)),
        out_specs=VMEM if last else [VMEM] * 4,
        scratch_shapes=scratch,
        compiler_params=params(16),
        cost_estimate=pl.CostEstimate(flops=5 * 10**8 * count, bytes_accessed=10**6, transcendentals=0),
        name="joint",
    )(info, *messages, *before)


def sum_kernel(in_ref, out_ref):
    total = in_ref[0]
    for i in range(1, in_ref.shape[0]):
        total = total + in_ref[i]
    for i in range(NZ):
        out_ref[i] = total


OFFSETS = (0, -1, 1, 2)


def position(info, holder, inner, outer):
    dy = inner + holder * (outer - inner)
    dx = outer + holder * (inner - outer)
    return ((info[0] + dy) & 3) * 4 + ((info[2] + dx) & 3)


def solve_kernel(places, info, ridge, *refs):
    n = len(places)
    pieces = refs[:n]
    out_ref, mass_ref = refs[n : n + 2]
    slab, high, low, wide, vec, square, result = refs[n + 2 :]
    core = info[3]
    for piece, (other, parts) in zip(pieces, places):
        holder = 1 - core if other else core
        for at, inner, outer in parts:
            row = pl.multiple_of(64 * position(info, holder, inner, outer), 64)
            for z in range(NZ):
                slab[2 * z + holder, pl.ds(row, 64), :] = piece[at + z]

    def keep(m, r, c, tile):
        hi = tile.astype(BF16)
        high[m, r : r + 128, c : c + 128] = hi
        low[m, r : r + 128, c : c + 128] = (tile - hi.astype(F32)).astype(BF16)

    def build(p, _):
        for s in range(1, 4):
            for h in range(2):
                for c in range(2):
                    tile = slab[2 * p + c, 128 * (2 * s - 2 + h) : 128 * (2 * s - 1 + h), :]
                    keep((p + s) & 7, K * (7 - s) + 128 * c, 128 * h, tile)
                    keep(p, K * (s - 1) + 128 * h, 128 * c, tile.T)
        return 0

    lax.fori_loop(0, M, build, 0)

    def build_far(p, _):
        for h in range(2):
            for c in range(2):
                tile = slab[2 * p + 8 * h + c, 768:896, :]
                keep(p + 4, 3 * K + 128 * c, 128 * h, tile)
                keep(p, 3 * K + 128 * h, 128 * c, tile.T)
        return 0

    lax.fori_loop(0, 4, build_far, 0)

    group = 4 * info[0] + info[2]
    start, remain, direction, precond, inverse, right = range(6)
    square[...] = jnp.zeros_like(square)
    for i in range(16):
        tile = slab[group, 896 + 8 * i : 904 + 8 * i, :]
        vec[remain, :, 128 * i : 128 * i + 128] = tile
        vec[right, :, 128 * i : 128 * i + 128] = tile
        if i < 6:
            square[1 + i : 2 + i, :] = tile[0:1]
    counts = vec[remain, 7:8, :]
    mass = jnp.sum(counts[:, 0:K], axis=1, keepdims=True)
    mass_ref[...] = jnp.broadcast_to(mass, mass_ref.shape)
    lam = ridge[0] * mass / K
    vec[precond] = jnp.broadcast_to(counts + lam, vec.shape[1:])
    vec[inverse] = jnp.broadcast_to(1.0 / (counts + lam), vec.shape[1:])
    vec[start] = jnp.zeros(vec.shape[1:], F32)
    scaled = vec[remain] * vec[inverse]
    vec[direction] = scaled
    first_inner = jnp.sum(vec[remain] * scaled, axis=1, keepdims=True)

    def operator(d):
        pieces = jnp.concatenate(split3(d), axis=0).astype(BF16)
        wide[:, 0 : M * K] = pieces
        wide[:, M * K :] = pieces
        image = []
        for m in range(M):
            part = wide[:, K * (m + 1) : K * (m + 8)]
            total = dot(part, high[m], NN) + dot(part, low[m], NN)
            image.append(total[0:8] + total[8:16] + total[16:24])
        return jnp.concatenate(image, axis=1) + vec[precond] * d

    def step(_, inner):
        d = vec[direction]
        image = operator(d)
        alpha = inner / jnp.sum(d * image, axis=1, keepdims=True)
        vec[start] = vec[start] + alpha * d
        r = vec[remain] - alpha * image
        vec[remain] = r
        scaled = r * vec[inverse]
        fresh = jnp.sum(r * scaled, axis=1, keepdims=True)
        vec[direction] = scaled + fresh / inner * d
        return fresh

    lax.fori_loop(0, ITERS, step, first_inner)
    for i in range(16):
        result[6 * i : 6 * i + 6, :] = vec[start, 1:7, 128 * i : 128 * i + 128]
    c = vec[start]
    fitted = c * (vec[right] + vec[remain] + lam * c)
    left = jnp.sum(square[...], axis=1, keepdims=True) - jnp.sum(fitted, axis=1, keepdims=True)
    left = jnp.sum(left[1:7], axis=0, keepdims=True)
    result[96:112, :] = jnp.broadcast_to(left, (16, 128))
    out_ref[...] = result[pl.ds(pl.multiple_of(56 * core, 8), 56), :]


def residual_kernel(
    info, wide_ref, rest_ref, wide_other, rest_other, mass_ref, codes_ref, vectors_ref,
    out_ref, table_ref, part_ref, left, hot, books_ref,
):
    step = pl.program_id(0)

    @pl.when(step == 0)
    def _():
        core = info[3]
        for holder, first, second in ((core, wide_ref, rest_ref), (1 - core, wide_other, rest_other)):
            row = pl.multiple_of(56 * holder, 8)
            for u in range(16):
                k = position(info, holder, OFFSETS[u % 4], OFFSETS[u // 4])
                books_ref[k, pl.ds(row, 56), :] = first[u] if u < 4 else second[u - 4]
        for m in range(M):
            for h in range(2):
                for k in range(16):
                    i = 2 * m + h
                    table_ref[m, 6 * k : 6 * k + 6, 128 * h : 128 * h + 128] = books_ref[k, 6 * i : 6 * i + 6, :]
        for m in range(M):
            for t, piece in enumerate(split3(table_ref[m])):
                left[D * t : D * t + D, K * m : K * m + K] = piece.astype(BF16)
        total = books_ref[0, 96:97, :]
        for k in range(1, 16):
            total = total + books_ref[k, 96:97, :]
        part_ref[...] = jnp.broadcast_to(total / (mass_ref[0:1, :] * D), part_ref.shape)

    cols = codes_ref.shape[1]
    level = lax.broadcasted_iota(jnp.int32, (K, cols), 0).astype(F32).astype(BF16)
    for m in range(M):
        code = codes_ref[m : m + 1, :].astype(F32).astype(BF16)
        hot[K * m : K * m + K, :] = jnp.where(level == code, jnp.ones((), BF16), jnp.zeros((), BF16))
    recon = dot(left[...], hot[...], NN)
    recon = recon[0:D] + recon[D : 2 * D] + recon[2 * D : 3 * D]
    out_ref[...] = vectors_ref[...] - recon


def shift(array, stage, by):
    pairs = []
    for y in range(NY):
        for x in range(NX):
            for c in range(2):
                ty, tx = ((y + by) % NY, x) if (c == 0) == (stage == 0) else (y, (x + by) % NX)
                pairs.append(((y * NX + x) * 2 + c, (ty * NX + tx) * 2 + c))
    return lax.ppermute(array, ("y", "x", "c"), pairs)


def swap(array):
    return lax.ppermute(array, "c", [(0, 1), (1, 0)])


def ring(array, stage):
    up = shift(array, stage, 1)
    down = shift(array, stage, -1)
    half = array.shape[0] // 2
    return up, down, shift(up[:half], stage, 1), shift(down[half:], stage, -1)


def along_z(array, by):
    pairs = []
    for z in range(NZ):
        for c in range(2):
            pairs.append((2 * z + c, 2 * ((z + by * (1 - 2 * c)) % NZ) + c))
    return lax.ppermute(array, ("z", "c"), pairs)


def spread(array, axes):
    return lax.all_to_all(array, axes, 0, 0, tiled=True)


def body(vectors, codes, weights, ridge):
    rows = vectors.shape[0]
    vectors = vectors.T
    codes = codes.T
    mass = weights.astype(F32).reshape(1, rows)
    info = jnp.stack([lax.axis_index(a) for a in ("y", "z", "x", "c")]).astype(jnp.int32)
    own, *messages = pl.pallas_call(
        message_kernel,
        out_shape=[jax.ShapeDtypeStruct((24, rows if d < 4 else rows // 2), F32) for d in range(5)],
        in_specs=[SMEM, VMEM, VMEM, VMEM],
        out_specs=[VMEM] * 5,
        compiler_params=params(16),
        name="message",
    )(info, codes, mass, vectors)
    messages = [along_z(message, d + 1) for d, message in enumerate(messages)]
    state = joint(info, [own], [], False)
    others = [swap(message) for message in messages]
    state = joint(info, messages, state, False)
    slab = joint(info, others, state, True)
    slab = spread(slab, ("y", "x"))
    chunk = pl.pallas_call(
        sum_kernel,
        out_shape=jax.ShapeDtypeStruct((NZ, 64, 128), F32),
        in_specs=[VMEM],
        out_specs=VMEM,
        compiler_params=params(8),
        name="chunk",
    )(slab)
    line = spread(chunk, "z")
    wide = jnp.concatenate([line, *ring(line, 0)], axis=0)
    places, arrays = [], []
    for array, outer, units in zip(
        (wide, *ring(wide, 1)), (0, -1, 1, 2, 2), ((0, 1, 2, 3),) * 3 + ((0, 1), (2, 3))
    ):
        parts = [(8 * n, OFFSETS[u], outer) for n, u in enumerate(units)]
        for other in (False, True):
            places.append((other, parts))
            arrays.append(swap(array) if other else array)
    columns, total_mass = pl.pallas_call(
        functools.partial(solve_kernel, places),
        out_shape=(jax.ShapeDtypeStruct((56, 128), F32), jax.ShapeDtypeStruct((8, 128), F32)),
        in_specs=[SMEM, SMEM] + [VMEM] * len(arrays),
        out_specs=(VMEM, VMEM),
        scratch_shapes=[
            pltpu.VMEM((16, 1024, 128), F32),
            pltpu.VMEM((M, 7 * K, K), BF16),
            pltpu.VMEM((M, 7 * K, K), BF16),
            pltpu.VMEM((24, 2 * M * K), BF16),
            pltpu.VMEM((6, 8, M * K), F32),
            pltpu.VMEM((8, 128), F32),
            pltpu.VMEM((112, 128), F32),
        ],
        compiler_params=params(40),
        name="solve",
    )(info, ridge, *arrays)
    wide = jnp.stack([columns] + [shift(columns, 0, by) for by in (1, -1, 2)])
    rest = jnp.concatenate([shift(wide, 1, by) for by in (1, -1, 2)], axis=0)
    lanes = 256
    residual, table, part = pl.pallas_call(
        residual_kernel,
        grid=(rows // lanes,),
        out_shape=(
            jax.ShapeDtypeStruct((D, rows), F32),
            jax.ShapeDtypeStruct((M, D, K), F32),
            jax.ShapeDtypeStruct((8, 128), F32),
        ),
        in_specs=[
            SMEM,
            pl.BlockSpec((4, 56, 128), lambda i: (0, 0, 0)),
            pl.BlockSpec((12, 56, 128), lambda i: (0, 0, 0)),
            pl.BlockSpec((4, 56, 128), lambda i: (0, 0, 0)),
            pl.BlockSpec((12, 56, 128), lambda i: (0, 0, 0)),
            pl.BlockSpec((8, 128), lambda i: (0, 0)),
            pl.BlockSpec((M, lanes), lambda i: (0, i)),
            pl.BlockSpec((D, lanes), lambda i: (0, i)),
        ],
        out_specs=(
            pl.BlockSpec((D, lanes), lambda i: (0, i)),
            pl.BlockSpec((M, D, K), lambda i: (0, 0, 0)),
            pl.BlockSpec((8, 128), lambda i: (0, 0)),
        ),
        scratch_shapes=[
            pltpu.VMEM((3 * D, M * K), BF16),
            pltpu.VMEM((M * K, lanes), BF16),
            pltpu.VMEM((16, 112, 128), F32),
        ],
        compiler_params=params(24, dimension_semantics=("arbitrary",)),
        name="residual",
    )(info, wide, rest, swap(wide), swap(rest), total_mass, codes, vectors)
    return (table.transpose(0, 2, 1), residual.T, part[0, 0])


def solution(mesh):
    finer = Mesh(mesh.devices.reshape(NY, NZ, NX, 2), ("y", "z", "x", "c"))
    placed = (P(DP, None), P(DP, None), P(DP), P())
    return jax.shard_map(
        body, mesh=finer, in_specs=placed, out_specs=(P(), P(DP, None), P()), check_vma=False
    )
```

time: 185 us -> 163 us (0.88)
  blocking collectives: 75.6 us -> 33.5 us
  starting transfers between devices: 9.05 us -> 28.3 us
  waiting for transfers between devices: 32.6 us -> 50 us
  Pallas kernels: 60.9 us -> 44.6 us
  local copies, waits for them, and re-layouts: 3.71 us -> 1.73 us
    all_to_all x4 -> x2, blocking collectives: 75.6 us -> 33.5 us  [spread(): return lax.all_to_all(array, axes, 0, 0, tiled=True)]
    ppermute x8 -> x14, waiting for transfers between devices: 31.4 us -> 41.6 us  [shift(): return lax.ppermute(array, ('y', 'x', 'c'), pairs)]
    pallas_call x1, Pallas kernels: 37.3 us -> 27.5 us  [body(): pl.pallas_call(functools.partial(solve_kernel, places), out_shape=(jax.Sh...]
    ppermute x0 -> x4, starting transfers between devices: none -> 9.85 us  [along_z(): return lax.ppermute(array, ('z', 'c'), pairs)]
    ppermute x8 -> x14, starting transfers between devices: 8.54 us -> 16.3 us  [shift(): return lax.ppermute(array, ('y', 'x', 'c'), pairs)]
    pallas_call x3 -> x5, Pallas kernels: 20.4 us -> 13.3 us  [the longest x3 12.6 us: joint(): pl.pallas_call(functools.partial(joint_kernel, count, not before, last),...]
    ppermute x0 -> x4, waiting for transfers between devices: none -> 5.79 us  [along_z(): return lax.ppermute(array, ('z', 'c'), pairs)]
    unnamed x16 -> x12, local copies, waits for them, and re-layouts: 3.05 us -> 1.09 us
  transfers between devices with their start and end apart: 13 -> 29, of which waited for: 6 -> 12; matrix products, arithmetic and copies ran while one was open for 0% -> 0% of each run, Pallas kernels for 0% -> 5%
where the time goes in v3:
time: 163 us; the launch traced here: 160 us
  waiting for transfers between devices  50 us (31%)
  Pallas kernels  44.6 us (27%)
  blocking collectives  33.5 us (21%)
  starting transfers between devices  28.3 us (17%)
  local copies, waits for them, and re-layouts  1.73 us (1%)
    ppermute x14, waiting for transfers between devices, shift(): return lax.ppermute(array, ('y', 'x', 'c'), pairs)  41.6 us
    all_to_all x2, blocking collectives, spread(): return lax.all_to_all(array, axes, 0, 0, tiled=True)  33.5 us
    pallas_call x1, Pallas kernels, body(): pl.pallas_call(functools.partial(solve_kernel, places), out_shape=(jax.Sh...  27.5 us
    ppermute x14, starting transfers between devices, shift(): return lax.ppermute(array, ('y', 'x', 'c'), pairs)  16.3 us
    pallas_call x3, Pallas kernels, joint(): pl.pallas_call(functools.partial(joint_kernel, count, not before, last),...  12.6 us
    ppermute x4, starting transfers between devices, along_z(): return lax.ppermute(array, ('z', 'c'), pairs)  9.85 us
    ppermute x4, waiting for transfers between devices, along_z(): return lax.ppermute(array, ('z', 'c'), pairs)  5.79 us
    pallas_call x1, Pallas kernels, body(): pl.pallas_call(residual_kernel, grid=(rows // lanes,), out_shape=(jax.Sha...  3.85 us
  transfers between devices with their start and end apart: 29, of which 12 were waited for; matrix products, arithmetic and copies ran while one was open for 0% of the time, Pallas kernels for 5%

profile of v3, /device:TPU:2, one launch (start us, length us, event | category | flops | bytes accessed | tf_op | source)
XLA Modules:
  0.0 160.4 jit_solution(10713897919150942096)
XLA Ops:
  3.1 2.0 %collective-permute-start = (f32[24,1024]{1,0:T(8,128)S(1)}, f32[24,1024]{1,0:T(8,128)S(1)}, u32[]{:S(2)}, u32[]{:S(2)}) collective-permute-start(f32[24,1024]{1,0:T(8,128)S(1)} %get-tuple-element.21), channel_id=1, source_target_pairs={{0,8},{1,57},{8,16},{9,1},{16,24},{17,9},{24,32},{25,17},{32,40},{... | collective-permute-start | bytes 294920 | tf_op jit(solution)/shard_map/ppermute | solution.py:324
  5.1 3.3 %collective-permute-start.2 = (f32[24,1024]{1,0:T(8,128)S(1)}, f32[24,1024]{1,0:T(8,128)S(1)}, u32[]{:S(2)}, u32[]{:S(2)}) collective-permute-start(f32[24,1024]{1,0:T(8,128)S(1)} %get-tuple-element.22), channel_id=1, source_target_pairs={{0,16},{1,49},{8,24},{9,57},{16,32},{17,1},{24,40},{25,9},{32,48},... | collective-permute-start | bytes 294920 | tf_op jit(solution)/shard_map/ppermute | solution.py:324
  8.4 4.0 %collective-permute-start.4 = (f32[24,1024]{1,0:T(8,128)S(1)}, f32[24,1024]{1,0:T(8,128)S(1)}, u32[]{:S(2)}, u32[]{:S(2)}) collective-permute-start(f32[24,1024]{1,0:T(8,128)S(1)} %get-tuple-element.23), channel_id=1, source_target_pairs={{0,24},{1,41},{8,32},{9,49},{16,40},{17,57},{24,48},{25,1},{32,56}... | collective-permute-start | bytes 294920 | tf_op jit(solution)/shard_map/ppermute | solution.py:324
  12.9 2.0 %joint.3 = (f32[3,160,256]{2,1,0:T(8,128)S(1)}, f32[128,128]{1,0:T(8,128)S(1)}, f32[8,32,256]{2,1,0:T(8,128)S(1)}, f32[8,128]{1,0:T(8,128)S(1)}) custom-call(s32[4]{0:T(128)S(1)} %pad_add_fusion.info, f32[24,1024]{1,0:T(8,128)S(1)} %get-tuple-element.25.refs_0_), custom_call_target="tpu_custom_call" | custom-call | flops 500000000 | bytes 1000000 | tf_op jit(solution)/shard_map/joint/pallas_call | solution.py:139
  15.0 5.8 %collective-permute-done.6.refs_3_ = f32[24,512]{1,0:T(8,128)S(1)} collective-permute-done((f32[24,512]{1,0:T(8,128)S(1)}, f32[24,512]{1,0:T(8,128)S(1)}, u32[]{:S(2)}, u32[]{:S(2)}) %collective-permute-start.6) | collective-permute-done | bytes 49184 | tf_op jit(solution)/shard_map/ppermute | solution.py:324
  21.8 5.3 %joint.4 = (f32[3,160,256]{2,1,0:T(8,128)S(1)}, f32[128,128]{1,0:T(8,128)S(1)}, f32[8,32,256]{2,1,0:T(8,128)S(1)}, f32[8,128]{1,0:T(8,128)S(1)}) custom-call(s32[4]{0:T(128)S(1)} %pad_add_fusion.info, f32[24,1024]{1,0:T(8,128)S(1)} %collective-permute-done.refs_0_, f32[24,1024]{1,0:T(8,128)S(1)} %collective-permute-done.2.refs_1_, ...), custom_call_target="tpu_custom_call" | custom-call | flops 2000000000 | bytes 1000000 | tf_op jit(solution)/shard_map/joint/pallas_call | solution.py:139
  27.1 5.3 %joint.5 = f32[16,64,128]{2,1,0:T(8,128)S(1)} custom-call(s32[4]{0:T(128)S(1)} %pad_add_fusion.info, f32[24,1024]{1,0:T(8,128)S(1)} %collective-permute-done.1.refs_0_, f32[24,1024]{1,0:T(8,128)S(1)} %collective-permute-done.3.refs_1_, f32[24,1024]{1,0:T(8,128)S(1)} %collective-permute-done.5.refs_2_, f32[24,512]{1,0:T(8,128)S(1)} %collective-permute-done.7.refs_3_, ...), custom_call_target="tpu_custom_call" | custom-call | flops 2000000000 | bytes 1000000 | tf_op jit(solution)/shard_map/joint/pallas_call | solution.py:139
  32.4 17.9 %all_to_all.10.in_ref = f32[16,64,128]{2,1,0:T(8,128)S(1)} all-to-all(f32[16,64,128]{2,1,0:T(8,128)S(1)} %joint.5), channel_id=1, replica_groups=mesh['y'=4,'z'=8,'x'=4,'c'=2] {'y','x'}, dimensions={0} | all-to-all | bytes 1048576 | tf_op jit(solution)/shard_map/all_to_all | solution.py:328
  50.3 15.6 %all_to_all.11 = f32[8,64,128]{2,1,0:T(8,128)S(1)} all-to-all(f32[8,64,128]{2,1,0:T(8,128)S(1)} %chunk.1), channel_id=1, replica_groups=mesh['y'=4,'z'=8,'x'=4,'c'=2] {'z'}, dimensions={0} | all-to-all | bytes 524288 | tf_op jit(solution)/shard_map/all_to_all | solution.py:328
  68.0 4.3 %collective-permute-done.9 = f32[8,64,128]{2,1,0:T(8,128)S(1)} collective-permute-done((f32[8,64,128]{2,1,0:T(8,128)S(1)}, f32[8,64,128]{2,1,0:T(8,128)S(1)}, u32[]{:S(2)}, u32[]{:S(2)}) %collective-permute-start.9) | collective-permute-done | bytes 262176 | tf_op jit(solution)/shard_map/ppermute | solution.py:305
  72.3 2.1 %collective-permute-start.11 = (f32[4,64,128]{2,1,0:T(8,128)S(1)}, f32[4,64,128]{2,1,0:T(8,128)S(1)}, u32[]{:S(2)}, u32[]{:S(2)}) collective-permute-start(f32[4,64,128]{2,1,0:T(8,128)S(1)} %slice.21), channel_id=1, source_target_pairs={{0,192},{1,7},{2,194},{3,1},{4,196},{5,3},{6,198},{7,5},{64,0},{65... | collective-permute-start | bytes 393224 | tf_op jit(solution)/shard_map/ppermute | solution.py:305
  74.6 7.5 %collective-permute-done.10 = f32[4,64,128]{2,1,0:T(8,128)S(1)} collective-permute-done((f32[4,64,128]{2,1,0:T(8,128)S(1)}, f32[4,64,128]{2,1,0:T(8,128)S(1)}, u32[]{:S(2)}, u32[]{:S(2)}) %collective-permute-start.10) | collective-permute-done | bytes 131104 | tf_op jit(solution)/shard_map/ppermute | solution.py:305
  82.4 1.9 %collective-permute-start.13 = (f32[32,64,128]{2,1,0:T(8,128)S(1)}, f32[32,64,128]{2,1,0:T(8,128)S(1)}, u32[]{:S(2)}, u32[]{:S(2)}) collective-permute-start(f32[32,64,128]{2,1,0:T(8,128)S(1)} %constant_dynamic-update-slice_fusion.refs_0_), channel_id=1, source_target_pairs={{0,2},{1,65},{2,4},{3,67},{4,6},{5,69},{6,0},{7,71},{64,66},{65,12... | collective-permute-start | bytes 3145736 | tf_op jit(solution)/shard_map/ppermute | solution.py:305
  84.3 12.8 %collective-permute-done.15.refs_4_ = f32[32,64,128]{2,1,0:T(8,128)S(1)} collective-permute-done((f32[32,64,128]{2,1,0:T(8,128)S(1)}, f32[32,64,128]{2,1,0:T(8,128)S(1)}, u32[]{:S(2)}, u32[]{:S(2)}) %collective-permute-start.15) | collective-permute-done | bytes 1048608 | tf_op jit(solution)/shard_map/ppermute | solution.py:305
  97.7 1.9 %collective-permute-start.17 = (f32[16,64,128]{2,1,0:T(8,128)S(1)}, f32[16,64,128]{2,1,0:T(8,128)S(1)}, u32[]{:S(2)}, u32[]{:S(2)}) collective-permute-start(f32[16,64,128]{2,1,0:T(8,128)S(1)} %slice.22), channel_id=1, source_target_pairs={{0,2},{1,65},{2,4},{3,67},{4,6},{5,69},{6,0},{7,71},{64,66},{65,12... | collective-permute-start | bytes 1572872 | tf_op jit(solution)/shard_map/ppermute | solution.py:305
  100.1 6.5 %collective-permute-done.19.refs_8_ = f32[16,64,128]{2,1,0:T(8,128)S(1)} collective-permute-done((f32[16,64,128]{2,1,0:T(8,128)S(1)}, f32[16,64,128]{2,1,0:T(8,128)S(1)}, u32[]{:S(2)}, u32[]{:S(2)}) %collective-permute-start.19) | collective-permute-done | bytes 524320 | tf_op jit(solution)/shard_map/ppermute | solution.py:305
  106.6 1.9 %collective-permute-done.17.refs_6_ = f32[16,64,128]{2,1,0:T(8,128)S(1)} collective-permute-done((f32[16,64,128]{2,1,0:T(8,128)S(1)}, f32[16,64,128]{2,1,0:T(8,128)S(1)}, u32[]{:S(2)}, u32[]{:S(2)}) %collective-permute-start.17) | collective-permute-done | bytes 524320 | tf_op jit(solution)/shard_map/ppermute | solution.py:305
  110.4 27.5 %solve.1 = (f32[56,128]{1,0:T(8,128)S(1)}, f32[8,128]{1,0:T(8,128)S(1)}) custom-call(s32[4]{0:T(128)S(1)} %pad_add_fusion.info, f32[1]{0:T(128)S(6)} %copy.13.ridge, f32[32,64,128]{2,1,0:T(8,128)S(1)} %constant_dynamic-update-slice_fusion.refs_0_, f32[32,64,128]{2,1,0:T(8,128)S(1)} %collective-permute-done.12.refs_1_, ...), custom_call_target="tpu_custom_call" | custom-call | tf_op jit(solution)/shard_map/solve/pallas_call | solution.py:369
  138.7 1.4 collective-permute-start.21
  140.1 3.3 %collective-permute-done.23 = f32[56,128]{1,0:T(8,128)S(1)} collective-permute-done((f32[56,128]{1,0:T(8,128)S(1)}, f32[56,128]{1,0:T(8,128)S(1)}, u32[]{:S(2)}, u32[]{:S(2)}) %collective-permute-start.23) | collective-permute-done | bytes 28704 | tf_op jit(solution)/shard_map/ppermute | solution.py:305
  144.8 4.5 %collective-permute-start.26 = (f32[4,56,128]{2,1,0:T(8,128)S(1)}, f32[4,56,128]{2,1,0:T(8,128)S(1)}, u32[]{:S(2)}, u32[]{:S(2)}) collective-permute-start(f32[4,56,128]{2,1,0:T(8,128)S(1)} %pad_maximum_fusion.wide_ref), channel_id=1, source_target_pairs={{0,4},{1,129},{2,6},{3,131},{4,0},{5,133},{6,2},{7,135},{64,68},{6... | collective-permute-start | bytes 344072 | tf_op jit(solution)/shard_map/ppermute | solution.py:305
  150.0 4.1 %collective-permute-done.25 = f32[4,56,128]{2,1,0:T(8,128)S(1)} collective-permute-done((f32[4,56,128]{2,1,0:T(8,128)S(1)}, f32[4,56,128]{2,1,0:T(8,128)S(1)}, u32[]{:S(2)}, u32[]{:S(2)}) %collective-permute-start.25) | collective-permute-done | bytes 114720 | tf_op jit(solution)/shard_map/ppermute | solution.py:305
  154.8 1.3 collective-permute-done.27.wide_other
  156.1 3.9 %residual.1 = (f32[96,1024]{1,0:T(8,128)}, f32[8,96,256]{2,1,0:T(8,128)}, f32[8,128]{1,0:T(8,128)S(1)}) custom-call(s32[4]{0:T(128)S(1)} %pad_add_fusion.info, f32[4,56,128]{2,1,0:T(8,128)S(1)} %pad_maximum_fusion.wide_ref, f32[12,56,128]{2,1,0:T(8,128)S(1)} %constant_dynamic-update-slice_fusion.5.rest_ref, ...), custom_call_target="tpu_custom_call" | custom-call | tf_op jit(solution)/shard_map/residual/pallas_call | solution.py:389
  (65 shorter events, 12.9 us)
Async XLA Ops:
  3.1 17.7 %collective-permute-start = (f32[24,1024]{1,0:T(8,128)S(1)}, f32[24,1024]{1,0:T(8,128)S(1)}, u32[]{:S(2)}, u32[]{:S(2)}) collective-permute-start(f32[24,1024]{1,0:T(8,128)S(1)} %get-tuple-element.21), channel_id=1, source_target_pairs={{0,8},{1,57},{8,16},{9,1},{16,24},{17,9},{24,32},{25,17},{32,40},{... | collective-permute-start | bytes 294920 | tf_op jit(solution)/shard_map/ppermute | solution.py:324
  5.1 16.2 %collective-permute-start.2 = (f32[24,1024]{1,0:T(8,128)S(1)}, f32[24,1024]{1,0:T(8,128)S(1)}, u32[]{:S(2)}, u32[]{:S(2)}) collective-permute-start(f32[24,1024]{1,0:T(8,128)S(1)} %get-tuple-element.22), channel_id=1, source_target_pairs={{0,16},{1,49},{8,24},{9,57},{16,32},{17,1},{24,40},{25,9},{32,48},... | collective-permute-start | bytes 294920 | tf_op jit(solution)/shard_map/ppermute | solution.py:324
  8.4 13.0 %collective-permute-start.4 = (f32[24,1024]{1,0:T(8,128)S(1)}, f32[24,1024]{1,0:T(8,128)S(1)}, u32[]{:S(2)}, u32[]{:S(2)}) collective-permute-start(f32[24,1024]{1,0:T(8,128)S(1)} %get-tuple-element.23), channel_id=1, source_target_pairs={{0,24},{1,41},{8,32},{9,49},{16,40},{17,57},{24,48},{25,1},{32,56}... | collective-permute-start | bytes 294920 | tf_op jit(solution)/shard_map/ppermute | solution.py:324
  12.4 8.4 %collective-permute-start.6 = (f32[24,512]{1,0:T(8,128)S(1)}, f32[24,512]{1,0:T(8,128)S(1)}, u32[]{:S(2)}, u32[]{:S(2)}) collective-permute-start(f32[24,512]{1,0:T(8,128)S(1)} %get-tuple-element.24), channel_id=1, source_target_pairs={{0,32},{1,33},{8,40},{9,41},{16,48},{17,49},{24,56},{25,57},{32,0}... | collective-permute-start | bytes 147464 | tf_op jit(solution)/shard_map/ppermute | solution.py:324
  20.8 6.3 %collective-permute-start.7 = (f32[24,512]{1,0:T(8,128)S(1)}, f32[24,512]{1,0:T(8,128)S(1)}, u32[]{:S(2)}, u32[]{:S(2)}) collective-permute-start(f32[24,512]{1,0:T(8,128)S(1)} %collective-permute-done.6.refs_3_), channel_id=1, source_target_pairs={{0,1},{1,0},{2,3},{3,2},{4,5},{5,4},{6,7},{7,6},{8,9},{9,8},{10,11... | collective-permute-start | bytes 147464 | tf_op jit(solution)/shard_map/ppermute | solution.py:309
  20.8 6.3 %collective-permute-start.1 = (f32[24,1024]{1,0:T(8,128)S(1)}, f32[24,1024]{1,0:T(8,128)S(1)}, u32[]{:S(2)}, u32[]{:S(2)}) collective-permute-start(f32[24,1024]{1,0:T(8,128)S(1)} %collective-permute-done.refs_0_), channel_id=1, source_target_pairs={{0,1},{1,0},{2,3},{3,2},{4,5},{5,4},{6,7},{7,6},{8,9},{9,8},{10,11... | collective-permute-start | bytes 294920 | tf_op jit(solution)/shard_map/ppermute | solution.py:309
  21.3 5.8 %collective-permute-start.3 = (f32[24,1024]{1,0:T(8,128)S(1)}, f32[24,1024]{1,0:T(8,128)S(1)}, u32[]{:S(2)}, u32[]{:S(2)}) collective-permute-start(f32[24,1024]{1,0:T(8,128)S(1)} %collective-permute-done.2.refs_1_), channel_id=1, source_target_pairs={{0,1},{1,0},{2,3},{3,2},{4,5},{5,4},{6,7},{7,6},{8,9},{9,8},{10,11... | collective-permute-start | bytes 294920 | tf_op jit(solution)/shard_map/ppermute | solution.py:309
  21.4 5.7 %collective-permute-start.5 = (f32[24,1024]{1,0:T(8,128)S(1)}, f32[24,1024]{1,0:T(8,128)S(1)}, u32[]{:S(2)}, u32[]{:S(2)}) collective-permute-start(f32[24,1024]{1,0:T(8,128)S(1)} %collective-permute-done.4.refs_2_), channel_id=1, source_target_pairs={{0,1},{1,0},{2,3},{3,2},{4,5},{5,4},{6,7},{7,6},{8,9},{9,8},{10,11... | collective-permute-start | bytes 294920 | tf_op jit(solution)/shard_map/ppermute | solution.py:309
  66.0 6.4 %collective-permute-start.9 = (f32[8,64,128]{2,1,0:T(8,128)S(1)}, f32[8,64,128]{2,1,0:T(8,128)S(1)}, u32[]{:S(2)}, u32[]{:S(2)}) collective-permute-start(f32[8,64,128]{2,1,0:T(8,128)S(1)} %all_to_all.11), channel_id=1, source_target_pairs={{0,192},{1,7},{2,194},{3,1},{4,196},{5,3},{6,198},{7,5},{64,0},{65... | collective-permute-start | bytes 786440 | tf_op jit(solution)/shard_map/ppermute | solution.py:305
  66.8 7.7 %collective-permute-start.8 = (f32[8,64,128]{2,1,0:T(8,128)S(1)}, f32[8,64,128]{2,1,0:T(8,128)S(1)}, u32[]{:S(2)}, u32[]{:S(2)}) collective-permute-start(f32[8,64,128]{2,1,0:T(8,128)S(1)} %all_to_all.11), channel_id=1, source_target_pairs={{0,64},{1,3},{2,66},{3,5},{4,68},{5,7},{6,70},{7,1},{64,128},{65,6... | collective-permute-start | bytes 786440 | tf_op jit(solution)/shard_map/ppermute | solution.py:305
  72.3 9.8 %collective-permute-start.11 = (f32[4,64,128]{2,1,0:T(8,128)S(1)}, f32[4,64,128]{2,1,0:T(8,128)S(1)}, u32[]{:S(2)}, u32[]{:S(2)}) collective-permute-start(f32[4,64,128]{2,1,0:T(8,128)S(1)} %slice.21), channel_id=1, source_target_pairs={{0,192},{1,7},{2,194},{3,1},{4,196},{5,3},{6,198},{7,5},{64,0},{65... | collective-permute-start | bytes 393224 | tf_op jit(solution)/shard_map/ppermute | solution.py:305
  74.5 7.7 %collective-permute-start.10 = (f32[4,64,128]{2,1,0:T(8,128)S(1)}, f32[4,64,128]{2,1,0:T(8,128)S(1)}, u32[]{:S(2)}, u32[]{:S(2)}) collective-permute-start(f32[4,64,128]{2,1,0:T(8,128)S(1)} %slice.20), channel_id=1, source_target_pairs={{0,64},{1,3},{2,66},{3,5},{4,68},{5,7},{6,70},{7,1},{64,128},{65,6... | collective-permute-start | bytes 393224 | tf_op jit(solution)/shard_map/ppermute | solution.py:305
  82.2 14.9 %collective-permute-start.15 = (f32[32,64,128]{2,1,0:T(8,128)S(1)}, f32[32,64,128]{2,1,0:T(8,128)S(1)}, u32[]{:S(2)}, u32[]{:S(2)}) collective-permute-start(f32[32,64,128]{2,1,0:T(8,128)S(1)} %constant_dynamic-update-slice_fusion.refs_0_), channel_id=1, source_target_pairs={{0,6},{1,193},{2,0},{3,195},{4,2},{5,197},{6,4},{7,199},{64,70},{6... | collective-permute-start | bytes 3145736 | tf_op jit(solution)/shard_map/ppermute | solution.py:305
  82.4 15.2 %collective-permute-start.13 = (f32[32,64,128]{2,1,0:T(8,128)S(1)}, f32[32,64,128]{2,1,0:T(8,128)S(1)}, u32[]{:S(2)}, u32[]{:S(2)}) collective-permute-start(f32[32,64,128]{2,1,0:T(8,128)S(1)} %constant_dynamic-update-slice_fusion.refs_0_), channel_id=1, source_target_pairs={{0,2},{1,65},{2,4},{3,67},{4,6},{5,69},{6,0},{7,71},{64,66},{65,12... | collective-permute-start | bytes 3145736 | tf_op jit(solution)/shard_map/ppermute | solution.py:305
  84.3 24.8 %collective-permute-start.12 = (f32[32,64,128]{2,1,0:T(8,128)S(1)}, f32[32,64,128]{2,1,0:T(8,128)S(1)}, u32[]{:S(2)}, u32[]{:S(2)}) collective-permute-start(f32[32,64,128]{2,1,0:T(8,128)S(1)} %constant_dynamic-update-slice_fusion.refs_0_), channel_id=1, source_target_pairs={{0,1},{1,0},{2,3},{3,2},{4,5},{5,4},{6,7},{7,6},{8,9},{9,8},{10,11... | collective-permute-start | bytes 3145736 | tf_op jit(solution)/shard_map/ppermute | solution.py:309
  97.1 9.5 %collective-permute-start.19 = (f32[16,64,128]{2,1,0:T(8,128)S(1)}, f32[16,64,128]{2,1,0:T(8,128)S(1)}, u32[]{:S(2)}, u32[]{:S(2)}) collective-permute-start(f32[16,64,128]{2,1,0:T(8,128)S(1)} %slice.23), channel_id=1, source_target_pairs={{0,6},{1,193},{2,0},{3,195},{4,2},{5,197},{6,4},{7,199},{64,70},{6... | collective-permute-start | bytes 1572872 | tf_op jit(solution)/shard_map/ppermute | solution.py:305
  97.7 10.8 %collective-permute-start.17 = (f32[16,64,128]{2,1,0:T(8,128)S(1)}, f32[16,64,128]{2,1,0:T(8,128)S(1)}, u32[]{:S(2)}, u32[]{:S(2)}) collective-permute-start(f32[16,64,128]{2,1,0:T(8,128)S(1)} %slice.22), channel_id=1, source_target_pairs={{0,2},{1,65},{2,4},{3,67},{4,6},{5,69},{6,0},{7,71},{64,66},{65,12... | collective-permute-start | bytes 1572872 | tf_op jit(solution)/shard_map/ppermute | solution.py:305
  99.6 9.6 %collective-permute-start.16 = (f32[32,64,128]{2,1,0:T(8,128)S(1)}, f32[32,64,128]{2,1,0:T(8,128)S(1)}, u32[]{:S(2)}, u32[]{:S(2)}) collective-permute-start(f32[32,64,128]{2,1,0:T(8,128)S(1)} %collective-permute-done.15.refs_4_), channel_id=1, source_target_pairs={{0,1},{1,0},{2,3},{3,2},{4,5},{5,4},{6,7},{7,6},{8,9},{9,8},{10,11... | collective-permute-start | bytes 3145736 | tf_op jit(solution)/shard_map/ppermute | solution.py:309
  99.6 10.8 %collective-permute-start.14 = (f32[32,64,128]{2,1,0:T(8,128)S(1)}, f32[32,64,128]{2,1,0:T(8,128)S(1)}, u32[]{:S(2)}, u32[]{:S(2)}) collective-permute-start(f32[32,64,128]{2,1,0:T(8,128)S(1)} %collective-permute-done.13.refs_2_), channel_id=1, source_target_pairs={{0,1},{1,0},{2,3},{3,2},{4,5},{5,4},{6,7},{7,6},{8,9},{9,8},{10,11... | collective-permute-start | bytes 3145736 | tf_op jit(solution)/shard_map/ppermute | solution.py:309
  137.9 5.5 %collective-permute-start.23 = (f32[56,128]{1,0:T(8,128)S(1)}, f32[56,128]{1,0:T(8,128)S(1)}, u32[]{:S(2)}, u32[]{:S(2)}) collective-permute-start(f32[56,128]{1,0:T(8,128)S(1)} %get-tuple-element.34), channel_id=1, source_target_pairs={{0,128},{1,5},{2,130},{3,7},{4,132},{5,1},{6,134},{7,3},{64,192},{... | collective-permute-start | bytes 86024 | tf_op jit(solution)/shard_map/ppermute | solution.py:305
  138.0 5.4 %collective-permute-start.22 = (f32[56,128]{1,0:T(8,128)S(1)}, f32[56,128]{1,0:T(8,128)S(1)}, u32[]{:S(2)}, u32[]{:S(2)}) collective-permute-start(f32[56,128]{1,0:T(8,128)S(1)} %get-tuple-element.34), channel_id=1, source_target_pairs={{0,192},{1,7},{2,194},{3,1},{4,196},{5,3},{6,198},{7,5},{64,0},{65... | collective-permute-start | bytes 86024 | tf_op jit(solution)/shard_map/ppermute | solution.py:305
  138.7 5.2 %collective-permute-start.21 = (f32[56,128]{1,0:T(8,128)S(1)}, f32[56,128]{1,0:T(8,128)S(1)}, u32[]{:S(2)}, u32[]{:S(2)}) collective-permute-start(f32[56,128]{1,0:T(8,128)S(1)} %get-tuple-element.34), channel_id=1, source_target_pairs={{0,64},{1,3},{2,66},{3,5},{4,68},{5,7},{6,70},{7,1},{64,128},{65,6... | collective-permute-start | bytes 86024 | tf_op jit(solution)/shard_map/ppermute | solution.py:305
  143.9 6.1 %collective-permute-start.24 = (f32[4,56,128]{2,1,0:T(8,128)S(1)}, f32[4,56,128]{2,1,0:T(8,128)S(1)}, u32[]{:S(2)}, u32[]{:S(2)}) collective-permute-start(f32[4,56,128]{2,1,0:T(8,128)S(1)} %pad_maximum_fusion.wide_ref), channel_id=1, source_target_pairs={{0,2},{1,65},{2,4},{3,67},{4,6},{5,69},{6,0},{7,71},{64,66},{65,12... | collective-permute-start | bytes 344072 | tf_op jit(solution)/shard_map/ppermute | solution.py:305
  144.8 9.3 %collective-permute-start.26 = (f32[4,56,128]{2,1,0:T(8,128)S(1)}, f32[4,56,128]{2,1,0:T(8,128)S(1)}, u32[]{:S(2)}, u32[]{:S(2)}) collective-permute-start(f32[4,56,128]{2,1,0:T(8,128)S(1)} %pad_maximum_fusion.wide_ref), channel_id=1, source_target_pairs={{0,4},{1,129},{2,6},{3,131},{4,0},{5,133},{6,2},{7,135},{64,68},{6... | collective-permute-start | bytes 344072 | tf_op jit(solution)/shard_map/ppermute | solution.py:305
  (8 other events, 26.9 us)

commit v4 on v3

--- a/solution.py
+++ b/solution.py
@@ -283,7 +283,7 @@
         total = books_ref[0, 96:97, :]
         for k in range(1, 16):
             total = total + books_ref[k, 96:97, :]
-        part_ref[...] = jnp.broadcast_to(total / (mass_ref[0:1, :] * D), part_ref.shape)
+        part_ref[0] = (total / (mass_ref[0:1, :] * D))[0, 0]
 
     cols = codes_ref.shape[1]
     level = lax.broadcasted_iota(jnp.int32, (K, cols), 0).astype(F32).astype(BF16)
@@ -344,8 +344,12 @@
     )(info, codes, mass, vectors)
     messages = [along_z(message, d + 1) for d, message in enumerate(messages)]
     state = joint(info, [own], [], False)
-    others = [swap(message) for message in messages]
-    state = joint(info, messages, state, False)
+    near, later = messages[:2], messages[2:]
+    others = [swap(message) for message in near]
+    state = joint(info, near, state, False)
+    later, state = lax.optimization_barrier((later, state))
+    others += [swap(message) for message in later]
+    state = joint(info, later, state, False)
     slab = joint(info, others, state, True)
     slab = spread(slab, ("y", "x"))
     chunk = pl.pallas_call(
@@ -392,7 +396,7 @@
         out_shape=(
             jax.ShapeDtypeStruct((D, rows), F32),
             jax.ShapeDtypeStruct((M, D, K), F32),
-            jax.ShapeDtypeStruct((8, 128), F32),
+            jax.ShapeDtypeStruct((1,), F32),
         ),
         in_specs=[
             SMEM,
@@ -407,7 +411,7 @@
         out_specs=(
             pl.BlockSpec((D, lanes), lambda i: (0, i)),
             pl.BlockSpec((M, D, K), lambda i: (0, 0, 0)),
-            pl.BlockSpec((8, 128), lambda i: (0, 0)),
+            SMEM,
         ),
         scratch_shapes=[
             pltpu.VMEM((3 * D, M * K), BF16),
@@ -417,7 +421,7 @@
         compiler_params=params(24, dimension_semantics=("arbitrary",)),
         name="residual",
     )(info, wide, rest, swap(wide), swap(rest), total_mass, codes, vectors)
-    return (table.transpose(0, 2, 1), residual.T, part[0, 0])
+    return (table.transpose(0, 2, 1), residual.T, part[0])
 
 
 def solution(mesh):

time: 163 us -> 160 us (0.982)
    pallas_call x3 -> x4, Pallas kernels: 12.6 us -> 13.3 us  [joint(): pl.pallas_call(functools.partial(joint_kernel, count, not before, last),...]
  transfers between devices with their start and end apart: 29 -> 29, of which waited for: 12 -> 13; matrix products, arithmetic and copies ran while one was open for 0% -> 0% of each run, Pallas kernels for 5% -> 5%
where the time goes in v4:
time: 160 us; the launch traced here: 158 us
  waiting for transfers between devices  48.5 us (30%)
  Pallas kernels  45.4 us (28%)
  blocking collectives  32 us (20%)
  starting transfers between devices  28.2 us (18%)
    ppermute x14, waiting for transfers between devices, shift(): return lax.ppermute(array, ('y', 'x', 'c'), pairs)  41.8 us
    all_to_all x2, blocking collectives, spread(): return lax.all_to_all(array, axes, 0, 0, tiled=True)  32 us
    pallas_call x1, Pallas kernels, body(): pl.pallas_call(functools.partial(solve_kernel, places), out_shape=(jax.Sh...  27.5 us
    ppermute x14, starting transfers between devices, shift(): return lax.ppermute(array, ('y', 'x', 'c'), pairs)  16.2 us
    pallas_call x4, Pallas kernels, joint(): pl.pallas_call(functools.partial(joint_kernel, count, not before, last),...  13.3 us
    ppermute x4, starting transfers between devices, along_z(): return lax.ppermute(array, ('z', 'c'), pairs)  9.85 us
    ppermute x4, waiting for transfers between devices, along_z(): return lax.ppermute(array, ('z', 'c'), pairs)  4.17 us
    pallas_call x1, Pallas kernels, body(): pl.pallas_call(residual_kernel, grid=(rows // lanes,), out_shape=(jax.Sha...  3.89 us
  transfers between devices with their start and end apart: 29, of which 13 were waited for; matrix products, arithmetic and copies ran while one was open for 0% of the time, Pallas kernels for 5%

profile of v4, /device:TPU:2, one launch (start us, length us, event | category | flops | bytes accessed | tf_op | source)
XLA Modules:
  0.0 157.6 jit_solution(7163265013911822289)
XLA Ops:
  3.1 2.0 %collective-permute-start = (f32[24,1024]{1,0:T(8,128)S(1)}, f32[24,1024]{1,0:T(8,128)S(1)}, u32[]{:S(2)}, u32[]{:S(2)}) collective-permute-start(f32[24,1024]{1,0:T(8,128)S(1)} %get-tuple-element.31), channel_id=1, source_target_pairs={{0,8},{1,57},{8,16},{9,1},{16,24},{17,9},{24,32},{25,17},{32,40},{... | collective-permute-start | bytes 294920 | tf_op jit(solution)/shard_map/ppermute | solution.py:324
  5.1 3.3 %collective-permute-start.2 = (f32[24,1024]{1,0:T(8,128)S(1)}, f32[24,1024]{1,0:T(8,128)S(1)}, u32[]{:S(2)}, u32[]{:S(2)}) collective-permute-start(f32[24,1024]{1,0:T(8,128)S(1)} %get-tuple-element.32), channel_id=1, source_target_pairs={{0,16},{1,49},{8,24},{9,57},{16,32},{17,1},{24,40},{25,9},{32,48},... | collective-permute-start | bytes 294920 | tf_op jit(solution)/shard_map/ppermute | solution.py:324
  8.4 4.5 %collective-permute-start.5 = (f32[24,512]{1,0:T(8,128)S(1)}, f32[24,512]{1,0:T(8,128)S(1)}, u32[]{:S(2)}, u32[]{:S(2)}) collective-permute-start(f32[24,512]{1,0:T(8,128)S(1)} %get-tuple-element.34), channel_id=1, source_target_pairs={{0,32},{1,33},{8,40},{9,41},{16,48},{17,49},{24,56},{25,57},{32,0}... | collective-permute-start | bytes 147464 | tf_op jit(solution)/shard_map/ppermute | solution.py:324
  12.9 2.0 %joint.4 = (f32[3,160,256]{2,1,0:T(8,128)S(1)}, f32[128,128]{1,0:T(8,128)S(1)}, f32[8,32,256]{2,1,0:T(8,128)S(1)}, f32[8,128]{1,0:T(8,128)S(1)}) custom-call(s32[4]{0:T(128)S(1)} %pad_add_fusion.info, f32[24,1024]{1,0:T(8,128)S(1)} %get-tuple-element.35.refs_0_), custom_call_target="tpu_custom_call" | custom-call | flops 500000000 | bytes 1000000 | tf_op jit(solution)/shard_map/joint/pallas_call | solution.py:139
  15.1 3.3 %joint.5 = (f32[3,160,256]{2,1,0:T(8,128)S(1)}, f32[128,128]{1,0:T(8,128)S(1)}, f32[8,32,256]{2,1,0:T(8,128)S(1)}, f32[8,128]{1,0:T(8,128)S(1)}) custom-call(s32[4]{0:T(128)S(1)} %pad_add_fusion.info, f32[24,1024]{1,0:T(8,128)S(1)} %collective-permute-done.refs_0_, f32[24,1024]{1,0:T(8,128)S(1)} %collective-permute-done.2.refs_1_, ...), custom_call_target="tpu_custom_call" | custom-call | flops 1000000000 | bytes 1000000 | tf_op jit(solution)/shard_map/joint/pallas_call | solution.py:139
  18.5 4.1 %collective-permute-done.4.refs_0_ = f32[24,1024]{1,0:T(8,128)S(1)} collective-permute-done((f32[24,1024]{1,0:T(8,128)S(1)}, f32[24,1024]{1,0:T(8,128)S(1)}, u32[]{:S(2)}, u32[]{:S(2)}) %collective-permute-start.4) | collective-permute-done | bytes 98336 | tf_op jit(solution)/shard_map/ppermute | solution.py:324
  23.5 2.7 %joint.6 = (f32[3,160,256]{2,1,0:T(8,128)S(1)}, f32[128,128]{1,0:T(8,128)S(1)}, f32[8,32,256]{2,1,0:T(8,128)S(1)}, f32[8,128]{1,0:T(8,128)S(1)}) custom-call(s32[4]{0:T(128)S(1)} %pad_add_fusion.info, f32[24,1024]{1,0:T(8,128)S(1)} %collective-permute-done.4.refs_0_, f32[24,512]{1,0:T(8,128)S(1)} %collective-permute-done.5.refs_1_, ...), custom_call_target="tpu_custom_call" | custom-call | flops 1000000000 | bytes 1000000 | tf_op jit(solution)/shard_map/joint/pallas_call | solution.py:139
  26.3 5.3 %joint.7 = f32[16,64,128]{2,1,0:T(8,128)S(1)} custom-call(s32[4]{0:T(128)S(1)} %pad_add_fusion.info, f32[24,1024]{1,0:T(8,128)S(1)} %collective-permute-done.1.refs_0_, f32[24,1024]{1,0:T(8,128)S(1)} %collective-permute-done.3.refs_1_, f32[24,1024]{1,0:T(8,128)S(1)} %collective-permute-done.6.refs_2_, f32[24,512]{1,0:T(8,128)S(1)} %collective-permute-done.7.refs_3_, ...), custom_call_target="tpu_custom_call" | custom-call | flops 2000000000 | bytes 1000000 | tf_op jit(solution)/shard_map/joint/pallas_call | solution.py:139
  31.6 17.6 %all_to_all.10.in_ref = f32[16,64,128]{2,1,0:T(8,128)S(1)} all-to-all(f32[16,64,128]{2,1,0:T(8,128)S(1)} %joint.7), channel_id=1, replica_groups=mesh['y'=4,'z'=8,'x'=4,'c'=2] {'y','x'}, dimensions={0} | all-to-all | bytes 1048576 | tf_op jit(solution)/shard_map/all_to_all | solution.py:328
  49.2 14.4 %all_to_all.11 = f32[8,64,128]{2,1,0:T(8,128)S(1)} all-to-all(f32[8,64,128]{2,1,0:T(8,128)S(1)} %chunk.1), channel_id=1, replica_groups=mesh['y'=4,'z'=8,'x'=4,'c'=2] {'z'}, dimensions={0} | all-to-all | bytes 524288 | tf_op jit(solution)/shard_map/all_to_all | solution.py:328
  65.6 4.3 %collective-permute-done.9 = f32[8,64,128]{2,1,0:T(8,128)S(1)} collective-permute-done((f32[8,64,128]{2,1,0:T(8,128)S(1)}, f32[8,64,128]{2,1,0:T(8,128)S(1)}, u32[]{:S(2)}, u32[]{:S(2)}) %collective-permute-start.9) | collective-permute-done | bytes 262176 | tf_op jit(solution)/shard_map/ppermute | solution.py:305
  69.9 2.2 %collective-permute-start.11 = (f32[4,64,128]{2,1,0:T(8,128)S(1)}, f32[4,64,128]{2,1,0:T(8,128)S(1)}, u32[]{:S(2)}, u32[]{:S(2)}) collective-permute-start(f32[4,64,128]{2,1,0:T(8,128)S(1)} %slice.17), channel_id=1, source_target_pairs={{0,192},{1,7},{2,194},{3,1},{4,196},{5,3},{6,198},{7,5},{64,0},{65... | collective-permute-start | bytes 393224 | tf_op jit(solution)/shard_map/ppermute | solution.py:305
  72.3 7.5 %collective-permute-done.10 = f32[4,64,128]{2,1,0:T(8,128)S(1)} collective-permute-done((f32[4,64,128]{2,1,0:T(8,128)S(1)}, f32[4,64,128]{2,1,0:T(8,128)S(1)}, u32[]{:S(2)}, u32[]{:S(2)}) %collective-permute-start.10) | collective-permute-done | bytes 131104 | tf_op jit(solution)/shard_map/ppermute | solution.py:305
  79.9 1.3 collective-permute-start.15
  82.0 12.8 %collective-permute-done.15.refs_4_ = f32[32,64,128]{2,1,0:T(8,128)S(1)} collective-permute-done((f32[32,64,128]{2,1,0:T(8,128)S(1)}, f32[32,64,128]{2,1,0:T(8,128)S(1)}, u32[]{:S(2)}, u32[]{:S(2)}) %collective-permute-start.15) | collective-permute-done | bytes 1048608 | tf_op jit(solution)/shard_map/ppermute | solution.py:305
  94.8 1.3 collective-permute-start.19
  97.5 6.5 %collective-permute-done.19.refs_8_ = f32[16,64,128]{2,1,0:T(8,128)S(1)} collective-permute-done((f32[16,64,128]{2,1,0:T(8,128)S(1)}, f32[16,64,128]{2,1,0:T(8,128)S(1)}, u32[]{:S(2)}, u32[]{:S(2)}) %collective-permute-start.19) | collective-permute-done | bytes 524320 | tf_op jit(solution)/shard_map/ppermute | solution.py:305
  104.1 1.8 %collective-permute-done.17.refs_6_ = f32[16,64,128]{2,1,0:T(8,128)S(1)} collective-permute-done((f32[16,64,128]{2,1,0:T(8,128)S(1)}, f32[16,64,128]{2,1,0:T(8,128)S(1)}, u32[]{:S(2)}, u32[]{:S(2)}) %collective-permute-start.17) | collective-permute-done | bytes 524320 | tf_op jit(solution)/shard_map/ppermute | solution.py:305
  107.8 27.5 %solve.1 = (f32[56,128]{1,0:T(8,128)S(1)}, f32[8,128]{1,0:T(8,128)S(1)}) custom-call(s32[4]{0:T(128)S(1)} %pad_add_fusion.info, f32[1]{0:T(128)S(6)} %copy.13.ridge, f32[32,64,128]{2,1,0:T(8,128)S(1)} %constant_dynamic-update-slice_fusion.refs_0_, f32[32,64,128]{2,1,0:T(8,128)S(1)} %collective-permute-done.12.refs_1_, ...), custom_call_target="tpu_custom_call" | custom-call | tf_op jit(solution)/shard_map/solve/pallas_call | solution.py:373
  137.5 3.3 %collective-permute-done.23 = f32[56,128]{1,0:T(8,128)S(1)} collective-permute-done((f32[56,128]{1,0:T(8,128)S(1)}, f32[56,128]{1,0:T(8,128)S(1)}, u32[]{:S(2)}, u32[]{:S(2)}) %collective-permute-start.23) | collective-permute-done | bytes 28704 | tf_op jit(solution)/shard_map/ppermute | solution.py:305
  142.1 4.8 %collective-permute-start.26 = (f32[4,56,128]{2,1,0:T(8,128)S(1)}, f32[4,56,128]{2,1,0:T(8,128)S(1)}, u32[]{:S(2)}, u32[]{:S(2)}) collective-permute-start(f32[4,56,128]{2,1,0:T(8,128)S(1)} %pad_maximum_fusion.wide_ref), channel_id=1, source_target_pairs={{0,4},{1,129},{2,6},{3,131},{4,0},{5,133},{6,2},{7,135},{64,68},{6... | collective-permute-start | bytes 344072 | tf_op jit(solution)/shard_map/ppermute | solution.py:305
  147.7 4.1 %collective-permute-done.25 = f32[4,56,128]{2,1,0:T(8,128)S(1)} collective-permute-done((f32[4,56,128]{2,1,0:T(8,128)S(1)}, f32[4,56,128]{2,1,0:T(8,128)S(1)}, u32[]{:S(2)}, u32[]{:S(2)}) %collective-permute-start.25) | collective-permute-done | bytes 114720 | tf_op jit(solution)/shard_map/ppermute | solution.py:305
  152.4 1.3 collective-permute-done.27.wide_other
  153.7 3.9 %residual.1 = (f32[96,1024]{1,0:T(8,128)}, f32[8,96,256]{2,1,0:T(8,128)}, f32[1]{0:T(128)}) custom-call(s32[4]{0:T(128)S(1)} %pad_add_fusion.info, f32[4,56,128]{2,1,0:T(8,128)S(1)} %pad_maximum_fusion.wide_ref, f32[12,56,128]{2,1,0:T(8,128)S(1)} %constant_dynamic-update-slice_fusion.5.rest_ref, f32[4,56,128]{2,1,0:T(8,128)S(1)} %collective-permute-done.27.wide_other, ...), custom_call_target="tpu_custom_call" | custom-call | tf_op jit(solution)/shard_map/residual/pallas_call | solution.py:393
  (65 shorter events, 14.3 us)
Async XLA Ops:
  3.1 11.9 %collective-permute-start = (f32[24,1024]{1,0:T(8,128)S(1)}, f32[24,1024]{1,0:T(8,128)S(1)}, u32[]{:S(2)}, u32[]{:S(2)}) collective-permute-start(f32[24,1024]{1,0:T(8,128)S(1)} %get-tuple-element.31), channel_id=1, source_target_pairs={{0,8},{1,57},{8,16},{9,1},{16,24},{17,9},{24,32},{25,17},{32,40},{... | collective-permute-start | bytes 294920 | tf_op jit(solution)/shard_map/ppermute | solution.py:324
  5.1 10.0 %collective-permute-start.2 = (f32[24,1024]{1,0:T(8,128)S(1)}, f32[24,1024]{1,0:T(8,128)S(1)}, u32[]{:S(2)}, u32[]{:S(2)}) collective-permute-start(f32[24,1024]{1,0:T(8,128)S(1)} %get-tuple-element.32), channel_id=1, source_target_pairs={{0,16},{1,49},{8,24},{9,57},{16,32},{17,1},{24,40},{25,9},{32,48},... | collective-permute-start | bytes 294920 | tf_op jit(solution)/shard_map/ppermute | solution.py:324
  8.4 10.1 %collective-permute-start.5 = (f32[24,512]{1,0:T(8,128)S(1)}, f32[24,512]{1,0:T(8,128)S(1)}, u32[]{:S(2)}, u32[]{:S(2)}) collective-permute-start(f32[24,512]{1,0:T(8,128)S(1)} %get-tuple-element.34), channel_id=1, source_target_pairs={{0,32},{1,33},{8,40},{9,41},{16,48},{17,49},{24,56},{25,57},{32,0}... | collective-permute-start | bytes 147464 | tf_op jit(solution)/shard_map/ppermute | solution.py:324
  12.9 9.7 %collective-permute-start.4 = (f32[24,1024]{1,0:T(8,128)S(1)}, f32[24,1024]{1,0:T(8,128)S(1)}, u32[]{:S(2)}, u32[]{:S(2)}) collective-permute-start(f32[24,1024]{1,0:T(8,128)S(1)} %get-tuple-element.33), channel_id=1, source_target_pairs={{0,24},{1,41},{8,32},{9,49},{16,40},{17,57},{24,48},{25,1},{32,56}... | collective-permute-start | bytes 294920 | tf_op jit(solution)/shard_map/ppermute | solution.py:324
  22.5 3.7 %collective-permute-start.1 = (f32[24,1024]{1,0:T(8,128)S(1)}, f32[24,1024]{1,0:T(8,128)S(1)}, u32[]{:S(2)}, u32[]{:S(2)}) collective-permute-start(f32[24,1024]{1,0:T(8,128)S(1)} %collective-permute-done.refs_0_), channel_id=1, source_target_pairs={{0,1},{1,0},{2,3},{3,2},{4,5},{5,4},{6,7},{7,6},{8,9},{9,8},{10,11... | collective-permute-start | bytes 294920 | tf_op jit(solution)/shard_map/ppermute | solution.py:309
  22.5 3.7 %collective-permute-start.3 = (f32[24,1024]{1,0:T(8,128)S(1)}, f32[24,1024]{1,0:T(8,128)S(1)}, u32[]{:S(2)}, u32[]{:S(2)}) collective-permute-start(f32[24,1024]{1,0:T(8,128)S(1)} %collective-permute-done.2.refs_1_), channel_id=1, source_target_pairs={{0,1},{1,0},{2,3},{3,2},{4,5},{5,4},{6,7},{7,6},{8,9},{9,8},{10,11... | collective-permute-start | bytes 294920 | tf_op jit(solution)/shard_map/ppermute | solution.py:309
  23.0 3.2 %collective-permute-start.6 = (f32[24,1024]{1,0:T(8,128)S(1)}, f32[24,1024]{1,0:T(8,128)S(1)}, u32[]{:S(2)}, u32[]{:S(2)}) collective-permute-start(f32[24,1024]{1,0:T(8,128)S(1)} %collective-permute-done.4.refs_0_), channel_id=1, source_target_pairs={{0,1},{1,0},{2,3},{3,2},{4,5},{5,4},{6,7},{7,6},{8,9},{9,8},{10,11... | collective-permute-start | bytes 294920 | tf_op jit(solution)/shard_map/ppermute | solution.py:309
  63.5 6.4 %collective-permute-start.9 = (f32[8,64,128]{2,1,0:T(8,128)S(1)}, f32[8,64,128]{2,1,0:T(8,128)S(1)}, u32[]{:S(2)}, u32[]{:S(2)}) collective-permute-start(f32[8,64,128]{2,1,0:T(8,128)S(1)} %all_to_all.11), channel_id=1, source_target_pairs={{0,192},{1,7},{2,194},{3,1},{4,196},{5,3},{6,198},{7,5},{64,0},{65... | collective-permute-start | bytes 786440 | tf_op jit(solution)/shard_map/ppermute | solution.py:305
  64.5 7.7 %collective-permute-start.8 = (f32[8,64,128]{2,1,0:T(8,128)S(1)}, f32[8,64,128]{2,1,0:T(8,128)S(1)}, u32[]{:S(2)}, u32[]{:S(2)}) collective-permute-start(f32[8,64,128]{2,1,0:T(8,128)S(1)} %all_to_all.11), channel_id=1, source_target_pairs={{0,64},{1,3},{2,66},{3,5},{4,68},{5,7},{6,70},{7,1},{64,128},{65,6... | collective-permute-start | bytes 786440 | tf_op jit(solution)/shard_map/ppermute | solution.py:305
  69.9 9.9 %collective-permute-start.11 = (f32[4,64,128]{2,1,0:T(8,128)S(1)}, f32[4,64,128]{2,1,0:T(8,128)S(1)}, u32[]{:S(2)}, u32[]{:S(2)}) collective-permute-start(f32[4,64,128]{2,1,0:T(8,128)S(1)} %slice.17), channel_id=1, source_target_pairs={{0,192},{1,7},{2,194},{3,1},{4,196},{5,3},{6,198},{7,5},{64,0},{65... | collective-permute-start | bytes 393224 | tf_op jit(solution)/shard_map/ppermute | solution.py:305
  72.2 7.7 %collective-permute-start.10 = (f32[4,64,128]{2,1,0:T(8,128)S(1)}, f32[4,64,128]{2,1,0:T(8,128)S(1)}, u32[]{:S(2)}, u32[]{:S(2)}) collective-permute-start(f32[4,64,128]{2,1,0:T(8,128)S(1)} %slice.16), channel_id=1, source_target_pairs={{0,64},{1,3},{2,66},{3,5},{4,68},{5,7},{6,70},{7,1},{64,128},{65,6... | collective-permute-start | bytes 393224 | tf_op jit(solution)/shard_map/ppermute | solution.py:305
  79.9 14.9 %collective-permute-start.15 = (f32[32,64,128]{2,1,0:T(8,128)S(1)}, f32[32,64,128]{2,1,0:T(8,128)S(1)}, u32[]{:S(2)}, u32[]{:S(2)}) collective-permute-start(f32[32,64,128]{2,1,0:T(8,128)S(1)} %constant_dynamic-update-slice_fusion.refs_0_), channel_id=1, source_target_pairs={{0,6},{1,193},{2,0},{3,195},{4,2},{5,197},{6,4},{7,199},{64,70},{6... | collective-permute-start | bytes 3145736 | tf_op jit(solution)/shard_map/ppermute | solution.py:305
  81.2 14.9 %collective-permute-start.13 = (f32[32,64,128]{2,1,0:T(8,128)S(1)}, f32[32,64,128]{2,1,0:T(8,128)S(1)}, u32[]{:S(2)}, u32[]{:S(2)}) collective-permute-start(f32[32,64,128]{2,1,0:T(8,128)S(1)} %constant_dynamic-update-slice_fusion.refs_0_), channel_id=1, source_target_pairs={{0,2},{1,65},{2,4},{3,67},{4,6},{5,69},{6,0},{7,71},{64,66},{65,12... | collective-permute-start | bytes 3145736 | tf_op jit(solution)/shard_map/ppermute | solution.py:305
  82.0 24.5 %collective-permute-start.12 = (f32[32,64,128]{2,1,0:T(8,128)S(1)}, f32[32,64,128]{2,1,0:T(8,128)S(1)}, u32[]{:S(2)}, u32[]{:S(2)}) collective-permute-start(f32[32,64,128]{2,1,0:T(8,128)S(1)} %constant_dynamic-update-slice_fusion.refs_0_), channel_id=1, source_target_pairs={{0,1},{1,0},{2,3},{3,2},{4,5},{5,4},{6,7},{7,6},{8,9},{9,8},{10,11... | collective-permute-start | bytes 3145736 | tf_op jit(solution)/shard_map/ppermute | solution.py:309
  94.8 9.3 %collective-permute-start.19 = (f32[16,64,128]{2,1,0:T(8,128)S(1)}, f32[16,64,128]{2,1,0:T(8,128)S(1)}, u32[]{:S(2)}, u32[]{:S(2)}) collective-permute-start(f32[16,64,128]{2,1,0:T(8,128)S(1)} %slice.19), channel_id=1, source_target_pairs={{0,6},{1,193},{2,0},{3,195},{4,2},{5,197},{6,4},{7,199},{64,70},{6... | collective-permute-start | bytes 1572872 | tf_op jit(solution)/shard_map/ppermute | solution.py:305
  96.2 9.7 %collective-permute-start.17 = (f32[16,64,128]{2,1,0:T(8,128)S(1)}, f32[16,64,128]{2,1,0:T(8,128)S(1)}, u32[]{:S(2)}, u32[]{:S(2)}) collective-permute-start(f32[16,64,128]{2,1,0:T(8,128)S(1)} %slice.18), channel_id=1, source_target_pairs={{0,2},{1,65},{2,4},{3,67},{4,6},{5,69},{6,0},{7,71},{64,66},{65,12... | collective-permute-start | bytes 1572872 | tf_op jit(solution)/shard_map/ppermute | solution.py:305
  97.0 9.5 %collective-permute-start.16 = (f32[32,64,128]{2,1,0:T(8,128)S(1)}, f32[32,64,128]{2,1,0:T(8,128)S(1)}, u32[]{:S(2)}, u32[]{:S(2)}) collective-permute-start(f32[32,64,128]{2,1,0:T(8,128)S(1)} %collective-permute-done.15.refs_4_), channel_id=1, source_target_pairs={{0,1},{1,0},{2,3},{3,2},{4,5},{5,4},{6,7},{7,6},{8,9},{9,8},{10,11... | collective-permute-start | bytes 3145736 | tf_op jit(solution)/shard_map/ppermute | solution.py:309
  97.0 10.7 %collective-permute-start.14 = (f32[32,64,128]{2,1,0:T(8,128)S(1)}, f32[32,64,128]{2,1,0:T(8,128)S(1)}, u32[]{:S(2)}, u32[]{:S(2)}) collective-permute-start(f32[32,64,128]{2,1,0:T(8,128)S(1)} %collective-permute-done.13.refs_2_), channel_id=1, source_target_pairs={{0,1},{1,0},{2,3},{3,2},{4,5},{5,4},{6,7},{7,6},{8,9},{9,8},{10,11... | collective-permute-start | bytes 3145736 | tf_op jit(solution)/shard_map/ppermute | solution.py:309
  135.3 5.5 %collective-permute-start.23 = (f32[56,128]{1,0:T(8,128)S(1)}, f32[56,128]{1,0:T(8,128)S(1)}, u32[]{:S(2)}, u32[]{:S(2)}) collective-permute-start(f32[56,128]{1,0:T(8,128)S(1)} %get-tuple-element.54), channel_id=1, source_target_pairs={{0,128},{1,5},{2,130},{3,7},{4,132},{5,1},{6,134},{7,3},{64,192},{... | collective-permute-start | bytes 86024 | tf_op jit(solution)/shard_map/ppermute | solution.py:305
  135.4 5.4 %collective-permute-start.22 = (f32[56,128]{1,0:T(8,128)S(1)}, f32[56,128]{1,0:T(8,128)S(1)}, u32[]{:S(2)}, u32[]{:S(2)}) collective-permute-start(f32[56,128]{1,0:T(8,128)S(1)} %get-tuple-element.54), channel_id=1, source_target_pairs={{0,192},{1,7},{2,194},{3,1},{4,196},{5,3},{6,198},{7,5},{64,0},{65... | collective-permute-start | bytes 86024 | tf_op jit(solution)/shard_map/ppermute | solution.py:305
  136.5 5.1 %collective-permute-start.21 = (f32[56,128]{1,0:T(8,128)S(1)}, f32[56,128]{1,0:T(8,128)S(1)}, u32[]{:S(2)}, u32[]{:S(2)}) collective-permute-start(f32[56,128]{1,0:T(8,128)S(1)} %get-tuple-element.54), channel_id=1, source_target_pairs={{0,64},{1,3},{2,66},{3,5},{4,68},{5,7},{6,70},{7,1},{64,128},{65,6... | collective-permute-start | bytes 86024 | tf_op jit(solution)/shard_map/ppermute | solution.py:305
  141.6 6.1 %collective-permute-start.24 = (f32[4,56,128]{2,1,0:T(8,128)S(1)}, f32[4,56,128]{2,1,0:T(8,128)S(1)}, u32[]{:S(2)}, u32[]{:S(2)}) collective-permute-start(f32[4,56,128]{2,1,0:T(8,128)S(1)} %pad_maximum_fusion.wide_ref), channel_id=1, source_target_pairs={{0,2},{1,65},{2,4},{3,67},{4,6},{5,69},{6,0},{7,71},{64,66},{65,12... | collective-permute-start | bytes 344072 | tf_op jit(solution)/shard_map/ppermute | solution.py:305
  142.1 9.6 %collective-permute-start.26 = (f32[4,56,128]{2,1,0:T(8,128)S(1)}, f32[4,56,128]{2,1,0:T(8,128)S(1)}, u32[]{:S(2)}, u32[]{:S(2)}) collective-permute-start(f32[4,56,128]{2,1,0:T(8,128)S(1)} %pad_maximum_fusion.wide_ref), channel_id=1, source_target_pairs={{0,4},{1,129},{2,6},{3,131},{4,0},{5,133},{6,2},{7,135},{64,68},{6... | collective-permute-start | bytes 344072 | tf_op jit(solution)/shard_map/ppermute | solution.py:305
  147.0 4.8 %collective-permute-start.25 = (f32[4,56,128]{2,1,0:T(8,128)S(1)}, f32[4,56,128]{2,1,0:T(8,128)S(1)}, u32[]{:S(2)}, u32[]{:S(2)}) collective-permute-start(f32[4,56,128]{2,1,0:T(8,128)S(1)} %pad_maximum_fusion.wide_ref), channel_id=1, source_target_pairs={{0,6},{1,193},{2,0},{3,195},{4,2},{5,197},{6,4},{7,199},{64,70},{6... | collective-permute-start | bytes 344072 | tf_op jit(solution)/shard_map/ppermute | solution.py:305
  (8 other events, 25.2 us)

commit v5 on v4

--- a/solution.py
+++ b/solution.py
@@ -389,7 +389,7 @@
     )(info, ridge, *arrays)
     wide = jnp.stack([columns] + [shift(columns, 0, by) for by in (1, -1, 2)])
     rest = jnp.concatenate([shift(wide, 1, by) for by in (1, -1, 2)], axis=0)
-    lanes = 256
+    lanes = 512
     residual, table, part = pl.pallas_call(
         residual_kernel,
         grid=(rows // lanes,),

time: 160 us -> 159 us (level)
  no operation moved by 1% of the time
where the time goes in v5:
time: 159 us; the launch traced here: 157 us
  waiting for transfers between devices  48.5 us (31%)
  Pallas kernels  44.9 us (28%)
  blocking collectives  32 us (20%)
  starting transfers between devices  28.2 us (18%)
    ppermute x14, waiting for transfers between devices, shift(): return lax.ppermute(array, ('y', 'x', 'c'), pairs)  41.8 us
    all_to_all x2, blocking collectives, spread(): return lax.all_to_all(array, axes, 0, 0, tiled=True)  32 us
    pallas_call x1, Pallas kernels, body(): pl.pallas_call(functools.partial(solve_kernel, places), out_shape=(jax.Sh...  27.5 us
    ppermute x14, starting transfers between devices, shift(): return lax.ppermute(array, ('y', 'x', 'c'), pairs)  16.2 us
    pallas_call x4, Pallas kernels, joint(): pl.pallas_call(functools.partial(joint_kernel, count, not before, last),...  13.3 us
    ppermute x4, starting transfers between devices, along_z(): return lax.ppermute(array, ('z', 'c'), pairs)  9.85 us
    ppermute x4, waiting for transfers between devices, along_z(): return lax.ppermute(array, ('z', 'c'), pairs)  4.17 us
    pallas_call x1, Pallas kernels, body(): pl.pallas_call(residual_kernel, grid=(rows // lanes,), out_shape=(jax.Sha...  3.39 us
  transfers between devices with their start and end apart: 29, of which 13 were waited for; matrix products, arithmetic and copies ran while one was open for 0% of the time, Pallas kernels for 5%

profile of v5, /device:TPU:2, one launch (start us, length us, event | category | flops | bytes accessed | tf_op | source)
XLA Modules:
  0.0 157.1 jit_solution(15943715193255056303)
XLA Ops:
  3.1 2.0 %collective-permute-start = (f32[24,1024]{1,0:T(8,128)S(1)}, f32[24,1024]{1,0:T(8,128)S(1)}, u32[]{:S(2)}, u32[]{:S(2)}) collective-permute-start(f32[24,1024]{1,0:T(8,128)S(1)} %get-tuple-element.31), channel_id=1, source_target_pairs={{0,8},{1,57},{8,16},{9,1},{16,24},{17,9},{24,32},{25,17},{32,40},{... | collective-permute-start | bytes 294920 | tf_op jit(solution)/shard_map/ppermute | solution.py:324
  5.1 3.3 %collective-permute-start.2 = (f32[24,1024]{1,0:T(8,128)S(1)}, f32[24,1024]{1,0:T(8,128)S(1)}, u32[]{:S(2)}, u32[]{:S(2)}) collective-permute-start(f32[24,1024]{1,0:T(8,128)S(1)} %get-tuple-element.32), channel_id=1, source_target_pairs={{0,16},{1,49},{8,24},{9,57},{16,32},{17,1},{24,40},{25,9},{32,48},... | collective-permute-start | bytes 294920 | tf_op jit(solution)/shard_map/ppermute | solution.py:324
  8.4 4.5 %collective-permute-start.5 = (f32[24,512]{1,0:T(8,128)S(1)}, f32[24,512]{1,0:T(8,128)S(1)}, u32[]{:S(2)}, u32[]{:S(2)}) collective-permute-start(f32[24,512]{1,0:T(8,128)S(1)} %get-tuple-element.34), channel_id=1, source_target_pairs={{0,32},{1,33},{8,40},{9,41},{16,48},{17,49},{24,56},{25,57},{32,0}... | collective-permute-start | bytes 147464 | tf_op jit(solution)/shard_map/ppermute | solution.py:324
  12.9 2.0 %joint.4 = (f32[3,160,256]{2,1,0:T(8,128)S(1)}, f32[128,128]{1,0:T(8,128)S(1)}, f32[8,32,256]{2,1,0:T(8,128)S(1)}, f32[8,128]{1,0:T(8,128)S(1)}) custom-call(s32[4]{0:T(128)S(1)} %pad_add_fusion.info, f32[24,1024]{1,0:T(8,128)S(1)} %get-tuple-element.35.refs_0_), custom_call_target="tpu_custom_call" | custom-call | flops 500000000 | bytes 1000000 | tf_op jit(solution)/shard_map/joint/pallas_call | solution.py:139
  15.1 3.3 %joint.5 = (f32[3,160,256]{2,1,0:T(8,128)S(1)}, f32[128,128]{1,0:T(8,128)S(1)}, f32[8,32,256]{2,1,0:T(8,128)S(1)}, f32[8,128]{1,0:T(8,128)S(1)}) custom-call(s32[4]{0:T(128)S(1)} %pad_add_fusion.info, f32[24,1024]{1,0:T(8,128)S(1)} %collective-permute-done.refs_0_, f32[24,1024]{1,0:T(8,128)S(1)} %collective-permute-done.2.refs_1_, ...), custom_call_target="tpu_custom_call" | custom-call | flops 1000000000 | bytes 1000000 | tf_op jit(solution)/shard_map/joint/pallas_call | solution.py:139
  18.5 4.1 %collective-permute-done.4.refs_0_ = f32[24,1024]{1,0:T(8,128)S(1)} collective-permute-done((f32[24,1024]{1,0:T(8,128)S(1)}, f32[24,1024]{1,0:T(8,128)S(1)}, u32[]{:S(2)}, u32[]{:S(2)}) %collective-permute-start.4) | collective-permute-done | bytes 98336 | tf_op jit(solution)/shard_map/ppermute | solution.py:324
  23.5 2.7 %joint.6 = (f32[3,160,256]{2,1,0:T(8,128)S(1)}, f32[128,128]{1,0:T(8,128)S(1)}, f32[8,32,256]{2,1,0:T(8,128)S(1)}, f32[8,128]{1,0:T(8,128)S(1)}) custom-call(s32[4]{0:T(128)S(1)} %pad_add_fusion.info, f32[24,1024]{1,0:T(8,128)S(1)} %collective-permute-done.4.refs_0_, f32[24,512]{1,0:T(8,128)S(1)} %collective-permute-done.5.refs_1_, ...), custom_call_target="tpu_custom_call" | custom-call | flops 1000000000 | bytes 1000000 | tf_op jit(solution)/shard_map/joint/pallas_call | solution.py:139
  26.3 5.3 %joint.7 = f32[16,64,128]{2,1,0:T(8,128)S(1)} custom-call(s32[4]{0:T(128)S(1)} %pad_add_fusion.info, f32[24,1024]{1,0:T(8,128)S(1)} %collective-permute-done.1.refs_0_, f32[24,1024]{1,0:T(8,128)S(1)} %collective-permute-done.3.refs_1_, f32[24,1024]{1,0:T(8,128)S(1)} %collective-permute-done.6.refs_2_, f32[24,512]{1,0:T(8,128)S(1)} %collective-permute-done.7.refs_3_, ...), custom_call_target="tpu_custom_call" | custom-call | flops 2000000000 | bytes 1000000 | tf_op jit(solution)/shard_map/joint/pallas_call | solution.py:139
  31.6 17.6 %all_to_all.10.in_ref = f32[16,64,128]{2,1,0:T(8,128)S(1)} all-to-all(f32[16,64,128]{2,1,0:T(8,128)S(1)} %joint.7), channel_id=1, replica_groups=mesh['y'=4,'z'=8,'x'=4,'c'=2] {'y','x'}, dimensions={0} | all-to-all | bytes 1048576 | tf_op jit(solution)/shard_map/all_to_all | solution.py:328
  49.2 14.4 %all_to_all.11 = f32[8,64,128]{2,1,0:T(8,128)S(1)} all-to-all(f32[8,64,128]{2,1,0:T(8,128)S(1)} %chunk.1), channel_id=1, replica_groups=mesh['y'=4,'z'=8,'x'=4,'c'=2] {'z'}, dimensions={0} | all-to-all | bytes 524288 | tf_op jit(solution)/shard_map/all_to_all | solution.py:328
  65.6 4.3 %collective-permute-done.9 = f32[8,64,128]{2,1,0:T(8,128)S(1)} collective-permute-done((f32[8,64,128]{2,1,0:T(8,128)S(1)}, f32[8,64,128]{2,1,0:T(8,128)S(1)}, u32[]{:S(2)}, u32[]{:S(2)}) %collective-permute-start.9) | collective-permute-done | bytes 262176 | tf_op jit(solution)/shard_map/ppermute | solution.py:305
  69.9 2.2 %collective-permute-start.11 = (f32[4,64,128]{2,1,0:T(8,128)S(1)}, f32[4,64,128]{2,1,0:T(8,128)S(1)}, u32[]{:S(2)}, u32[]{:S(2)}) collective-permute-start(f32[4,64,128]{2,1,0:T(8,128)S(1)} %slice.17), channel_id=1, source_target_pairs={{0,192},{1,7},{2,194},{3,1},{4,196},{5,3},{6,198},{7,5},{64,0},{65... | collective-permute-start | bytes 393224 | tf_op jit(solution)/shard_map/ppermute | solution.py:305
  72.3 7.5 %collective-permute-done.10 = f32[4,64,128]{2,1,0:T(8,128)S(1)} collective-permute-done((f32[4,64,128]{2,1,0:T(8,128)S(1)}, f32[4,64,128]{2,1,0:T(8,128)S(1)}, u32[]{:S(2)}, u32[]{:S(2)}) %collective-permute-start.10) | collective-permute-done | bytes 131104 | tf_op jit(solution)/shard_map/ppermute | solution.py:305
  79.9 1.3 collective-permute-start.15
  82.0 12.8 %collective-permute-done.15.refs_4_ = f32[32,64,128]{2,1,0:T(8,128)S(1)} collective-permute-done((f32[32,64,128]{2,1,0:T(8,128)S(1)}, f32[32,64,128]{2,1,0:T(8,128)S(1)}, u32[]{:S(2)}, u32[]{:S(2)}) %collective-permute-start.15) | collective-permute-done | bytes 1048608 | tf_op jit(solution)/shard_map/ppermute | solution.py:305
  94.8 1.3 collective-permute-start.19
  97.5 6.5 %collective-permute-done.19.refs_8_ = f32[16,64,128]{2,1,0:T(8,128)S(1)} collective-permute-done((f32[16,64,128]{2,1,0:T(8,128)S(1)}, f32[16,64,128]{2,1,0:T(8,128)S(1)}, u32[]{:S(2)}, u32[]{:S(2)}) %collective-permute-start.19) | collective-permute-done | bytes 524320 | tf_op jit(solution)/shard_map/ppermute | solution.py:305
  104.1 1.8 %collective-permute-done.17.refs_6_ = f32[16,64,128]{2,1,0:T(8,128)S(1)} collective-permute-done((f32[16,64,128]{2,1,0:T(8,128)S(1)}, f32[16,64,128]{2,1,0:T(8,128)S(1)}, u32[]{:S(2)}, u32[]{:S(2)}) %collective-permute-start.17) | collective-permute-done | bytes 524320 | tf_op jit(solution)/shard_map/ppermute | solution.py:305
  107.8 27.5 %solve.1 = (f32[56,128]{1,0:T(8,128)S(1)}, f32[8,128]{1,0:T(8,128)S(1)}) custom-call(s32[4]{0:T(128)S(1)} %pad_add_fusion.info, f32[1]{0:T(128)S(6)} %copy.13.ridge, f32[32,64,128]{2,1,0:T(8,128)S(1)} %constant_dynamic-update-slice_fusion.refs_0_, f32[32,64,128]{2,1,0:T(8,128)S(1)} %collective-permute-done.12.refs_1_, ...), custom_call_target="tpu_custom_call" | custom-call | tf_op jit(solution)/shard_map/solve/pallas_call | solution.py:373
  137.5 3.3 %collective-permute-done.23 = f32[56,128]{1,0:T(8,128)S(1)} collective-permute-done((f32[56,128]{1,0:T(8,128)S(1)}, f32[56,128]{1,0:T(8,128)S(1)}, u32[]{:S(2)}, u32[]{:S(2)}) %collective-permute-start.23) | collective-permute-done | bytes 28704 | tf_op jit(solution)/shard_map/ppermute | solution.py:305
  142.1 4.8 %collective-permute-start.26 = (f32[4,56,128]{2,1,0:T(8,128)S(1)}, f32[4,56,128]{2,1,0:T(8,128)S(1)}, u32[]{:S(2)}, u32[]{:S(2)}) collective-permute-start(f32[4,56,128]{2,1,0:T(8,128)S(1)} %pad_maximum_fusion.wide_ref), channel_id=1, source_target_pairs={{0,4},{1,129},{2,6},{3,131},{4,0},{5,133},{6,2},{7,135},{64,68},{6... | collective-permute-start | bytes 344072 | tf_op jit(solution)/shard_map/ppermute | solution.py:305
  147.7 4.1 %collective-permute-done.25 = f32[4,56,128]{2,1,0:T(8,128)S(1)} collective-permute-done((f32[4,56,128]{2,1,0:T(8,128)S(1)}, f32[4,56,128]{2,1,0:T(8,128)S(1)}, u32[]{:S(2)}, u32[]{:S(2)}) %collective-permute-start.25) | collective-permute-done | bytes 114720 | tf_op jit(solution)/shard_map/ppermute | solution.py:305
  152.4 1.3 collective-permute-done.27.wide_other
  153.7 3.4 %residual.1 = (f32[96,1024]{1,0:T(8,128)}, f32[8,96,256]{2,1,0:T(8,128)}, f32[1]{0:T(128)}) custom-call(s32[4]{0:T(128)S(1)} %pad_add_fusion.info, f32[4,56,128]{2,1,0:T(8,128)S(1)} %pad_maximum_fusion.wide_ref, f32[12,56,128]{2,1,0:T(8,128)S(1)} %constant_dynamic-update-slice_fusion.5.rest_ref, f32[4,56,128]{2,1,0:T(8,128)S(1)} %collective-permute-done.27.wide_other, ...), custom_call_target="tpu_custom_call" | custom-call | tf_op jit(solution)/shard_map/residual/pallas_call | solution.py:393
  (65 shorter events, 14.3 us)
Async XLA Ops:
  3.1 11.9 %collective-permute-start = (f32[24,1024]{1,0:T(8,128)S(1)}, f32[24,1024]{1,0:T(8,128)S(1)}, u32[]{:S(2)}, u32[]{:S(2)}) collective-permute-start(f32[24,1024]{1,0:T(8,128)S(1)} %get-tuple-element.31), channel_id=1, source_target_pairs={{0,8},{1,57},{8,16},{9,1},{16,24},{17,9},{24,32},{25,17},{32,40},{... | collective-permute-start | bytes 294920 | tf_op jit(solution)/shard_map/ppermute | solution.py:324
  5.1 10.0 %collective-permute-start.2 = (f32[24,1024]{1,0:T(8,128)S(1)}, f32[24,1024]{1,0:T(8,128)S(1)}, u32[]{:S(2)}, u32[]{:S(2)}) collective-permute-start(f32[24,1024]{1,0:T(8,128)S(1)} %get-tuple-element.32), channel_id=1, source_target_pairs={{0,16},{1,49},{8,24},{9,57},{16,32},{17,1},{24,40},{25,9},{32,48},... | collective-permute-start | bytes 294920 | tf_op jit(solution)/shard_map/ppermute | solution.py:324
  8.4 10.1 %collective-permute-start.5 = (f32[24,512]{1,0:T(8,128)S(1)}, f32[24,512]{1,0:T(8,128)S(1)}, u32[]{:S(2)}, u32[]{:S(2)}) collective-permute-start(f32[24,512]{1,0:T(8,128)S(1)} %get-tuple-element.34), channel_id=1, source_target_pairs={{0,32},{1,33},{8,40},{9,41},{16,48},{17,49},{24,56},{25,57},{32,0}... | collective-permute-start | bytes 147464 | tf_op jit(solution)/shard_map/ppermute | solution.py:324
  12.9 9.7 %collective-permute-start.4 = (f32[24,1024]{1,0:T(8,128)S(1)}, f32[24,1024]{1,0:T(8,128)S(1)}, u32[]{:S(2)}, u32[]{:S(2)}) collective-permute-start(f32[24,1024]{1,0:T(8,128)S(1)} %get-tuple-element.33), channel_id=1, source_target_pairs={{0,24},{1,41},{8,32},{9,49},{16,40},{17,57},{24,48},{25,1},{32,56}... | collective-permute-start | bytes 294920 | tf_op jit(solution)/shard_map/ppermute | solution.py:324
  22.5 3.7 %collective-permute-start.1 = (f32[24,1024]{1,0:T(8,128)S(1)}, f32[24,1024]{1,0:T(8,128)S(1)}, u32[]{:S(2)}, u32[]{:S(2)}) collective-permute-start(f32[24,1024]{1,0:T(8,128)S(1)} %collective-permute-done.refs_0_), channel_id=1, source_target_pairs={{0,1},{1,0},{2,3},{3,2},{4,5},{5,4},{6,7},{7,6},{8,9},{9,8},{10,11... | collective-permute-start | bytes 294920 | tf_op jit(solution)/shard_map/ppermute | solution.py:309
  22.5 3.7 %collective-permute-start.3 = (f32[24,1024]{1,0:T(8,128)S(1)}, f32[24,1024]{1,0:T(8,128)S(1)}, u32[]{:S(2)}, u32[]{:S(2)}) collective-permute-start(f32[24,1024]{1,0:T(8,128)S(1)} %collective-permute-done.2.refs_1_), channel_id=1, source_target_pairs={{0,1},{1,0},{2,3},{3,2},{4,5},{5,4},{6,7},{7,6},{8,9},{9,8},{10,11... | collective-permute-start | bytes 294920 | tf_op jit(solution)/shard_map/ppermute | solution.py:309
  23.0 3.2 %collective-permute-start.6 = (f32[24,1024]{1,0:T(8,128)S(1)}, f32[24,1024]{1,0:T(8,128)S(1)}, u32[]{:S(2)}, u32[]{:S(2)}) collective-permute-start(f32[24,1024]{1,0:T(8,128)S(1)} %collective-permute-done.4.refs_0_), channel_id=1, source_target_pairs={{0,1},{1,0},{2,3},{3,2},{4,5},{5,4},{6,7},{7,6},{8,9},{9,8},{10,11... | collective-permute-start | bytes 294920 | tf_op jit(solution)/shard_map/ppermute | solution.py:309
  63.5 6.4 %collective-permute-start.9 = (f32[8,64,128]{2,1,0:T(8,128)S(1)}, f32[8,64,128]{2,1,0:T(8,128)S(1)}, u32[]{:S(2)}, u32[]{:S(2)}) collective-permute-start(f32[8,64,128]{2,1,0:T(8,128)S(1)} %all_to_all.11), channel_id=1, source_target_pairs={{0,192},{1,7},{2,194},{3,1},{4,196},{5,3},{6,198},{7,5},{64,0},{65... | collective-permute-start | bytes 786440 | tf_op jit(solution)/shard_map/ppermute | solution.py:305
  64.5 7.7 %collective-permute-start.8 = (f32[8,64,128]{2,1,0:T(8,128)S(1)}, f32[8,64,128]{2,1,0:T(8,128)S(1)}, u32[]{:S(2)}, u32[]{:S(2)}) collective-permute-start(f32[8,64,128]{2,1,0:T(8,128)S(1)} %all_to_all.11), channel_id=1, source_target_pairs={{0,64},{1,3},{2,66},{3,5},{4,68},{5,7},{6,70},{7,1},{64,128},{65,6... | collective-permute-start | bytes 786440 | tf_op jit(solution)/shard_map/ppermute | solution.py:305
  69.9 9.9 %collective-permute-start.11 = (f32[4,64,128]{2,1,0:T(8,128)S(1)}, f32[4,64,128]{2,1,0:T(8,128)S(1)}, u32[]{:S(2)}, u32[]{:S(2)}) collective-permute-start(f32[4,64,128]{2,1,0:T(8,128)S(1)} %slice.17), channel_id=1, source_target_pairs={{0,192},{1,7},{2,194},{3,1},{4,196},{5,3},{6,198},{7,5},{64,0},{65... | collective-permute-start | bytes 393224 | tf_op jit(solution)/shard_map/ppermute | solution.py:305
  72.2 7.7 %collective-permute-start.10 = (f32[4,64,128]{2,1,0:T(8,128)S(1)}, f32[4,64,128]{2,1,0:T(8,128)S(1)}, u32[]{:S(2)}, u32[]{:S(2)}) collective-permute-start(f32[4,64,128]{2,1,0:T(8,128)S(1)} %slice.16), channel_id=1, source_target_pairs={{0,64},{1,3},{2,66},{3,5},{4,68},{5,7},{6,70},{7,1},{64,128},{65,6... | collective-permute-start | bytes 393224 | tf_op jit(solution)/shard_map/ppermute | solution.py:305
  79.9 14.9 %collective-permute-start.15 = (f32[32,64,128]{2,1,0:T(8,128)S(1)}, f32[32,64,128]{2,1,0:T(8,128)S(1)}, u32[]{:S(2)}, u32[]{:S(2)}) collective-permute-start(f32[32,64,128]{2,1,0:T(8,128)S(1)} %constant_dynamic-update-slice_fusion.refs_0_), channel_id=1, source_target_pairs={{0,6},{1,193},{2,0},{3,195},{4,2},{5,197},{6,4},{7,199},{64,70},{6... | collective-permute-start | bytes 3145736 | tf_op jit(solution)/shard_map/ppermute | solution.py:305
  81.2 14.9 %collective-permute-start.13 = (f32[32,64,128]{2,1,0:T(8,128)S(1)}, f32[32,64,128]{2,1,0:T(8,128)S(1)}, u32[]{:S(2)}, u32[]{:S(2)}) collective-permute-start(f32[32,64,128]{2,1,0:T(8,128)S(1)} %constant_dynamic-update-slice_fusion.refs_0_), channel_id=1, source_target_pairs={{0,2},{1,65},{2,4},{3,67},{4,6},{5,69},{6,0},{7,71},{64,66},{65,12... | collective-permute-start | bytes 3145736 | tf_op jit(solution)/shard_map/ppermute | solution.py:305
  82.0 24.5 %collective-permute-start.12 = (f32[32,64,128]{2,1,0:T(8,128)S(1)}, f32[32,64,128]{2,1,0:T(8,128)S(1)}, u32[]{:S(2)}, u32[]{:S(2)}) collective-permute-start(f32[32,64,128]{2,1,0:T(8,128)S(1)} %constant_dynamic-update-slice_fusion.refs_0_), channel_id=1, source_target_pairs={{0,1},{1,0},{2,3},{3,2},{4,5},{5,4},{6,7},{7,6},{8,9},{9,8},{10,11... | collective-permute-start | bytes 3145736 | tf_op jit(solution)/shard_map/ppermute | solution.py:309
  94.8 9.3 %collective-permute-start.19 = (f32[16,64,128]{2,1,0:T(8,128)S(1)}, f32[16,64,128]{2,1,0:T(8,128)S(1)}, u32[]{:S(2)}, u32[]{:S(2)}) collective-permute-start(f32[16,64,128]{2,1,0:T(8,128)S(1)} %slice.19), channel_id=1, source_target_pairs={{0,6},{1,193},{2,0},{3,195},{4,2},{5,197},{6,4},{7,199},{64,70},{6... | collective-permute-start | bytes 1572872 | tf_op jit(solution)/shard_map/ppermute | solution.py:305
  96.2 9.7 %collective-permute-start.17 = (f32[16,64,128]{2,1,0:T(8,128)S(1)}, f32[16,64,128]{2,1,0:T(8,128)S(1)}, u32[]{:S(2)}, u32[]{:S(2)}) collective-permute-start(f32[16,64,128]{2,1,0:T(8,128)S(1)} %slice.18), channel_id=1, source_target_pairs={{0,2},{1,65},{2,4},{3,67},{4,6},{5,69},{6,0},{7,71},{64,66},{65,12... | collective-permute-start | bytes 1572872 | tf_op jit(solution)/shard_map/ppermute | solution.py:305
  97.0 9.5 %collective-permute-start.16 = (f32[32,64,128]{2,1,0:T(8,128)S(1)}, f32[32,64,128]{2,1,0:T(8,128)S(1)}, u32[]{:S(2)}, u32[]{:S(2)}) collective-permute-start(f32[32,64,128]{2,1,0:T(8,128)S(1)} %collective-permute-done.15.refs_4_), channel_id=1, source_target_pairs={{0,1},{1,0},{2,3},{3,2},{4,5},{5,4},{6,7},{7,6},{8,9},{9,8},{10,11... | collective-permute-start | bytes 3145736 | tf_op jit(solution)/shard_map/ppermute | solution.py:309
  97.0 10.7 %collective-permute-start.14 = (f32[32,64,128]{2,1,0:T(8,128)S(1)}, f32[32,64,128]{2,1,0:T(8,128)S(1)}, u32[]{:S(2)}, u32[]{:S(2)}) collective-permute-start(f32[32,64,128]{2,1,0:T(8,128)S(1)} %collective-permute-done.13.refs_2_), channel_id=1, source_target_pairs={{0,1},{1,0},{2,3},{3,2},{4,5},{5,4},{6,7},{7,6},{8,9},{9,8},{10,11... | collective-permute-start | bytes 3145736 | tf_op jit(solution)/shard_map/ppermute | solution.py:309
  135.3 5.5 %collective-permute-start.23 = (f32[56,128]{1,0:T(8,128)S(1)}, f32[56,128]{1,0:T(8,128)S(1)}, u32[]{:S(2)}, u32[]{:S(2)}) collective-permute-start(f32[56,128]{1,0:T(8,128)S(1)} %get-tuple-element.54), channel_id=1, source_target_pairs={{0,128},{1,5},{2,130},{3,7},{4,132},{5,1},{6,134},{7,3},{64,192},{... | collective-permute-start | bytes 86024 | tf_op jit(solution)/shard_map/ppermute | solution.py:305
  135.4 5.4 %collective-permute-start.22 = (f32[56,128]{1,0:T(8,128)S(1)}, f32[56,128]{1,0:T(8,128)S(1)}, u32[]{:S(2)}, u32[]{:S(2)}) collective-permute-start(f32[56,128]{1,0:T(8,128)S(1)} %get-tuple-element.54), channel_id=1, source_target_pairs={{0,192},{1,7},{2,194},{3,1},{4,196},{5,3},{6,198},{7,5},{64,0},{65... | collective-permute-start | bytes 86024 | tf_op jit(solution)/shard_map/ppermute | solution.py:305
  136.5 5.1 %collective-permute-start.21 = (f32[56,128]{1,0:T(8,128)S(1)}, f32[56,128]{1,0:T(8,128)S(1)}, u32[]{:S(2)}, u32[]{:S(2)}) collective-permute-start(f32[56,128]{1,0:T(8,128)S(1)} %get-tuple-element.54), channel_id=1, source_target_pairs={{0,64},{1,3},{2,66},{3,5},{4,68},{5,7},{6,70},{7,1},{64,128},{65,6... | collective-permute-start | bytes 86024 | tf_op jit(solution)/shard_map/ppermute | solution.py:305
  141.6 6.1 %collective-permute-start.24 = (f32[4,56,128]{2,1,0:T(8,128)S(1)}, f32[4,56,128]{2,1,0:T(8,128)S(1)}, u32[]{:S(2)}, u32[]{:S(2)}) collective-permute-start(f32[4,56,128]{2,1,0:T(8,128)S(1)} %pad_maximum_fusion.wide_ref), channel_id=1, source_target_pairs={{0,2},{1,65},{2,4},{3,67},{4,6},{5,69},{6,0},{7,71},{64,66},{65,12... | collective-permute-start | bytes 344072 | tf_op jit(solution)/shard_map/ppermute | solution.py:305
  142.1 9.6 %collective-permute-start.26 = (f32[4,56,128]{2,1,0:T(8,128)S(1)}, f32[4,56,128]{2,1,0:T(8,128)S(1)}, u32[]{:S(2)}, u32[]{:S(2)}) collective-permute-start(f32[4,56,128]{2,1,0:T(8,128)S(1)} %pad_maximum_fusion.wide_ref), channel_id=1, source_target_pairs={{0,4},{1,129},{2,6},{3,131},{4,0},{5,133},{6,2},{7,135},{64,68},{6... | collective-permute-start | bytes 344072 | tf_op jit(solution)/shard_map/ppermute | solution.py:305
  147.0 4.8 %collective-permute-start.25 = (f32[4,56,128]{2,1,0:T(8,128)S(1)}, f32[4,56,128]{2,1,0:T(8,128)S(1)}, u32[]{:S(2)}, u32[]{:S(2)}) collective-permute-start(f32[4,56,128]{2,1,0:T(8,128)S(1)} %pad_maximum_fusion.wide_ref), channel_id=1, source_target_pairs={{0,6},{1,193},{2,0},{3,195},{4,2},{5,197},{6,4},{7,199},{64,70},{6... | collective-permute-start | bytes 344072 | tf_op jit(solution)/shard_map/ppermute | solution.py:305
  (8 other events, 25.2 us)

commit v6 on v5

--- a/solution.py
+++ b/solution.py
@@ -347,8 +347,9 @@
     near, later = messages[:2], messages[2:]
     others = [swap(message) for message in near]
     state = joint(info, near, state, False)
+    state = joint(info, others, state, False)
     later, state = lax.optimization_barrier((later, state))
-    others += [swap(message) for message in later]
+    others = [swap(message) for message in later]
     state = joint(info, later, state, False)
     slab = joint(info, others, state, True)
     slab = spread(slab, ("y", "x"))

time: 159 us -> 160 us (level)
  waiting for transfers between devices: 48.5 us -> 44.3 us
  blocking collectives: 32 us -> 35.1 us
    ppermute x4, waiting for transfers between devices: 4.17 us -> 0.42 us  [along_z(): return lax.ppermute(array, ('z', 'c'), pairs)]
    all_to_all x2, blocking collectives: 32 us -> 35.1 us  [spread(): return lax.all_to_all(array, axes, 0, 0, tiled=True)]
    pallas_call x4 -> x5, Pallas kernels: 13.3 us -> 14.1 us  [joint(): pl.pallas_call(functools.partial(joint_kernel, count, not before, last),...]
  transfers between devices with their start and end apart: 29 -> 29, of which waited for: 13 -> 12; matrix products, arithmetic and copies ran while one was open for 0% -> 0% of each run, Pallas kernels for 5% -> 7%
where the time goes in v6:
time: 160 us; the launch traced here: 158 us
  Pallas kernels  45.7 us (29%)
  waiting for transfers between devices  44.3 us (28%)
  blocking collectives  35.1 us (22%)
  starting transfers between devices  29.5 us (18%)
    ppermute x14, waiting for transfers between devices, shift(): return lax.ppermute(array, ('y', 'x', 'c'), pairs)  41.3 us
    all_to_all x2, blocking collectives, spread(): return lax.all_to_all(array, axes, 0, 0, tiled=True)  35.1 us
    pallas_call x1, Pallas kernels, body(): pl.pallas_call(functools.partial(solve_kernel, places), out_shape=(jax.Sh...  27.5 us
    ppermute x14, starting transfers between devices, shift(): return lax.ppermute(array, ('y', 'x', 'c'), pairs)  16.1 us
    pallas_call x5, Pallas kernels, joint(): pl.pallas_call(functools.partial(joint_kernel, count, not before, last),...  14.1 us
    ppermute x4, starting transfers between devices, along_z(): return lax.ppermute(array, ('z', 'c'), pairs)  9.85 us
    ppermute x11, starting transfers between devices, swap(): return lax.ppermute(array, 'c', [(0, 1), (1, 0)])  3.54 us
    pallas_call x1, Pallas kernels, body(): pl.pallas_call(residual_kernel, grid=(rows // lanes,), out_shape=(jax.Sha...  3.39 us
  transfers between devices with their start and end apart: 29, of which 12 were waited for; matrix products, arithmetic and copies ran while one was open for 0% of the time, Pallas kernels for 7%

profile of v6, /device:TPU:2, one launch (start us, length us, event | category | flops | bytes accessed | tf_op | source)
XLA Modules:
  0.0 158.1 jit_solution(17273567282163792191)
XLA Ops:
  3.1 2.0 %collective-permute-start.2 = (f32[24,1024]{1,0:T(8,128)S(1)}, f32[24,1024]{1,0:T(8,128)S(1)}, u32[]{:S(2)}, u32[]{:S(2)}) collective-permute-start(f32[24,1024]{1,0:T(8,128)S(1)} %get-tuple-element.37), channel_id=1, source_target_pairs={{0,8},{1,57},{8,16},{9,1},{16,24},{17,9},{24,32},{25,17},{32,40},{... | collective-permute-start | bytes 294920 | tf_op jit(solution)/shard_map/ppermute | solution.py:324
  5.1 3.3 %collective-permute-start.4 = (f32[24,1024]{1,0:T(8,128)S(1)}, f32[24,1024]{1,0:T(8,128)S(1)}, u32[]{:S(2)}, u32[]{:S(2)}) collective-permute-start(f32[24,1024]{1,0:T(8,128)S(1)} %get-tuple-element.38), channel_id=1, source_target_pairs={{0,16},{1,49},{8,24},{9,57},{16,32},{17,1},{24,40},{25,9},{32,48},... | collective-permute-start | bytes 294920 | tf_op jit(solution)/shard_map/ppermute | solution.py:324
  8.4 4.5 %collective-permute-start.1 = (f32[24,512]{1,0:T(8,128)S(1)}, f32[24,512]{1,0:T(8,128)S(1)}, u32[]{:S(2)}, u32[]{:S(2)}) collective-permute-start(f32[24,512]{1,0:T(8,128)S(1)} %get-tuple-element.36), channel_id=1, source_target_pairs={{0,32},{1,33},{8,40},{9,41},{16,48},{17,49},{24,56},{25,57},{32,0}... | collective-permute-start | bytes 147464 | tf_op jit(solution)/shard_map/ppermute | solution.py:324
  12.9 1.7 %collective-permute-start.3 = (f32[24,1024]{1,0:T(8,128)S(1)}, f32[24,1024]{1,0:T(8,128)S(1)}, u32[]{:S(2)}, u32[]{:S(2)}) collective-permute-start(f32[24,1024]{1,0:T(8,128)S(1)} %collective-permute-done.2.refs_0_), channel_id=1, source_target_pairs={{0,1},{1,0},{2,3},{3,2},{4,5},{5,4},{6,7},{7,6},{8,9},{9,8},{10,11... | collective-permute-start | bytes 294920 | tf_op jit(solution)/shard_map/ppermute | solution.py:309
  15.1 2.0 %joint.5 = (f32[3,160,256]{2,1,0:T(8,128)S(1)}, f32[128,128]{1,0:T(8,128)S(1)}, f32[8,32,256]{2,1,0:T(8,128)S(1)}, f32[8,128]{1,0:T(8,128)S(1)}) custom-call(s32[4]{0:T(128)S(1)} %pad_add_fusion.info, f32[24,1024]{1,0:T(8,128)S(1)} %get-tuple-element.39.refs_0_), custom_call_target="tpu_custom_call" | custom-call | flops 500000000 | bytes 1000000 | tf_op jit(solution)/shard_map/joint/pallas_call | solution.py:139
  17.1 3.3 %joint.6 = (f32[3,160,256]{2,1,0:T(8,128)S(1)}, f32[128,128]{1,0:T(8,128)S(1)}, f32[8,32,256]{2,1,0:T(8,128)S(1)}, f32[8,128]{1,0:T(8,128)S(1)}) custom-call(s32[4]{0:T(128)S(1)} %pad_add_fusion.info, f32[24,1024]{1,0:T(8,128)S(1)} %collective-permute-done.2.refs_0_, f32[24,1024]{1,0:T(8,128)S(1)} %collective-permute-done.4.refs_1_, ...), custom_call_target="tpu_custom_call" | custom-call | flops 1000000000 | bytes 1000000 | tf_op jit(solution)/shard_map/joint/pallas_call | solution.py:139
  20.5 3.3 %joint.7 = (f32[3,160,256]{2,1,0:T(8,128)S(1)}, f32[128,128]{1,0:T(8,128)S(1)}, f32[8,32,256]{2,1,0:T(8,128)S(1)}, f32[8,128]{1,0:T(8,128)S(1)}) custom-call(s32[4]{0:T(128)S(1)} %pad_add_fusion.info, f32[24,1024]{1,0:T(8,128)S(1)} %collective-permute-done.3.refs_0_, f32[24,1024]{1,0:T(8,128)S(1)} %collective-permute-done.5.refs_1_, ...), custom_call_target="tpu_custom_call" | custom-call | flops 1000000000 | bytes 1000000 | tf_op jit(solution)/shard_map/joint/pallas_call | solution.py:139
  24.6 2.7 %joint.8 = (f32[3,160,256]{2,1,0:T(8,128)S(1)}, f32[128,128]{1,0:T(8,128)S(1)}, f32[8,32,256]{2,1,0:T(8,128)S(1)}, f32[8,128]{1,0:T(8,128)S(1)}) custom-call(s32[4]{0:T(128)S(1)} %pad_add_fusion.info, f32[24,1024]{1,0:T(8,128)S(1)} %collective-permute-done.refs_0_, f32[24,512]{1,0:T(8,128)S(1)} %collective-permute-done.1.refs_1_, ...), custom_call_target="tpu_custom_call" | custom-call | flops 1000000000 | bytes 1000000 | tf_op jit(solution)/shard_map/joint/pallas_call | solution.py:139
  27.3 2.7 %joint.9 = f32[16,64,128]{2,1,0:T(8,128)S(1)} custom-call(s32[4]{0:T(128)S(1)} %pad_add_fusion.info, f32[24,1024]{1,0:T(8,128)S(1)} %collective-permute-done.6.refs_0_, f32[24,512]{1,0:T(8,128)S(1)} %collective-permute-done.7.refs_1_, f32[3,160,256]{2,1,0:T(8,128)S(1)} %get-tuple-element.58.refs_2_, f32[128,128]{1,0:T(8,128)S(1)} %get-tuple-element.59.refs_3_, ...), custom_call_target="tpu_custom_call" | custom-call | flops 1000000000 | bytes 1000000 | tf_op jit(solution)/shard_map/joint/pallas_call | solution.py:139
  30.0 18.0 %all_to_all.10.in_ref = f32[16,64,128]{2,1,0:T(8,128)S(1)} all-to-all(f32[16,64,128]{2,1,0:T(8,128)S(1)} %joint.9), channel_id=1, replica_groups=mesh['y'=4,'z'=8,'x'=4,'c'=2] {'y','x'}, dimensions={0} | all-to-all | bytes 1048576 | tf_op jit(solution)/shard_map/all_to_all | solution.py:328
  48.1 17.1 %all_to_all.11 = f32[8,64,128]{2,1,0:T(8,128)S(1)} all-to-all(f32[8,64,128]{2,1,0:T(8,128)S(1)} %chunk.1), channel_id=1, replica_groups=mesh['y'=4,'z'=8,'x'=4,'c'=2] {'z'}, dimensions={0} | all-to-all | bytes 524288 | tf_op jit(solution)/shard_map/all_to_all | solution.py:328
  67.2 4.3 %collective-permute-done.9 = f32[8,64,128]{2,1,0:T(8,128)S(1)} collective-permute-done((f32[8,64,128]{2,1,0:T(8,128)S(1)}, f32[8,64,128]{2,1,0:T(8,128)S(1)}, u32[]{:S(2)}, u32[]{:S(2)}) %collective-permute-start.9) | collective-permute-done | bytes 262176 | tf_op jit(solution)/shard_map/ppermute | solution.py:305
  71.5 2.1 %collective-permute-start.11 = (f32[4,64,128]{2,1,0:T(8,128)S(1)}, f32[4,64,128]{2,1,0:T(8,128)S(1)}, u32[]{:S(2)}, u32[]{:S(2)}) collective-permute-start(f32[4,64,128]{2,1,0:T(8,128)S(1)} %slice.17), channel_id=1, source_target_pairs={{0,192},{1,7},{2,194},{3,1},{4,196},{5,3},{6,198},{7,5},{64,0},{65... | collective-permute-start | bytes 393224 | tf_op jit(solution)/shard_map/ppermute | solution.py:305
  73.9 7.3 %collective-permute-done.10 = f32[4,64,128]{2,1,0:T(8,128)S(1)} collective-permute-done((f32[4,64,128]{2,1,0:T(8,128)S(1)}, f32[4,64,128]{2,1,0:T(8,128)S(1)}, u32[]{:S(2)}, u32[]{:S(2)}) %collective-permute-start.10) | collective-permute-done | bytes 131104 | tf_op jit(solution)/shard_map/ppermute | solution.py:305
  81.5 1.8 %collective-permute-start.13 = (f32[32,64,128]{2,1,0:T(8,128)S(1)}, f32[32,64,128]{2,1,0:T(8,128)S(1)}, u32[]{:S(2)}, u32[]{:S(2)}) collective-permute-start(f32[32,64,128]{2,1,0:T(8,128)S(1)} %constant_dynamic-update-slice_fusion.refs_0_), channel_id=1, source_target_pairs={{0,2},{1,65},{2,4},{3,67},{4,6},{5,69},{6,0},{7,71},{64,66},{65,12... | collective-permute-start | bytes 3145736 | tf_op jit(solution)/shard_map/ppermute | solution.py:305
  83.3 12.8 %collective-permute-done.15.refs_4_ = f32[32,64,128]{2,1,0:T(8,128)S(1)} collective-permute-done((f32[32,64,128]{2,1,0:T(8,128)S(1)}, f32[32,64,128]{2,1,0:T(8,128)S(1)}, u32[]{:S(2)}, u32[]{:S(2)}) %collective-permute-start.15) | collective-permute-done | bytes 1048608 | tf_op jit(solution)/shard_map/ppermute | solution.py:305
  96.5 1.8 %collective-permute-start.17 = (f32[16,64,128]{2,1,0:T(8,128)S(1)}, f32[16,64,128]{2,1,0:T(8,128)S(1)}, u32[]{:S(2)}, u32[]{:S(2)}) collective-permute-start(f32[16,64,128]{2,1,0:T(8,128)S(1)} %slice.18), channel_id=1, source_target_pairs={{0,2},{1,65},{2,4},{3,67},{4,6},{5,69},{6,0},{7,71},{64,66},{65,12... | collective-permute-start | bytes 1572872 | tf_op jit(solution)/shard_map/ppermute | solution.py:305
  98.9 6.5 %collective-permute-done.19.refs_8_ = f32[16,64,128]{2,1,0:T(8,128)S(1)} collective-permute-done((f32[16,64,128]{2,1,0:T(8,128)S(1)}, f32[16,64,128]{2,1,0:T(8,128)S(1)}, u32[]{:S(2)}, u32[]{:S(2)}) %collective-permute-start.19) | collective-permute-done | bytes 524320 | tf_op jit(solution)/shard_map/ppermute | solution.py:305
  105.4 1.8 %collective-permute-done.17.refs_6_ = f32[16,64,128]{2,1,0:T(8,128)S(1)} collective-permute-done((f32[16,64,128]{2,1,0:T(8,128)S(1)}, f32[16,64,128]{2,1,0:T(8,128)S(1)}, u32[]{:S(2)}, u32[]{:S(2)}) %collective-permute-start.17) | collective-permute-done | bytes 524320 | tf_op jit(solution)/shard_map/ppermute | solution.py:305
  109.1 27.5 %solve.1 = (f32[56,128]{1,0:T(8,128)S(1)}, f32[8,128]{1,0:T(8,128)S(1)}) custom-call(s32[4]{0:T(128)S(1)} %pad_add_fusion.info, f32[1]{0:T(128)S(6)} %copy.13.ridge, f32[32,64,128]{2,1,0:T(8,128)S(1)} %constant_dynamic-update-slice_fusion.refs_0_, f32[32,64,128]{2,1,0:T(8,128)S(1)} %collective-permute-done.12.refs_1_, ...), custom_call_target="tpu_custom_call" | custom-call | tf_op jit(solution)/shard_map/solve/pallas_call | solution.py:374
  138.8 3.3 %collective-permute-done.23 = f32[56,128]{1,0:T(8,128)S(1)} collective-permute-done((f32[56,128]{1,0:T(8,128)S(1)}, f32[56,128]{1,0:T(8,128)S(1)}, u32[]{:S(2)}, u32[]{:S(2)}) %collective-permute-start.23) | collective-permute-done | bytes 28704 | tf_op jit(solution)/shard_map/ppermute | solution.py:305
  143.4 4.6 %collective-permute-start.26 = (f32[4,56,128]{2,1,0:T(8,128)S(1)}, f32[4,56,128]{2,1,0:T(8,128)S(1)}, u32[]{:S(2)}, u32[]{:S(2)}) collective-permute-start(f32[4,56,128]{2,1,0:T(8,128)S(1)} %pad_maximum_fusion.wide_ref), channel_id=1, source_target_pairs={{0,4},{1,129},{2,6},{3,131},{4,0},{5,133},{6,2},{7,135},{64,68},{6... | collective-permute-start | bytes 344072 | tf_op jit(solution)/shard_map/ppermute | solution.py:305
  148.7 4.1 %collective-permute-done.25 = f32[4,56,128]{2,1,0:T(8,128)S(1)} collective-permute-done((f32[4,56,128]{2,1,0:T(8,128)S(1)}, f32[4,56,128]{2,1,0:T(8,128)S(1)}, u32[]{:S(2)}, u32[]{:S(2)}) %collective-permute-start.25) | collective-permute-done | bytes 114720 | tf_op jit(solution)/shard_map/ppermute | solution.py:305
  154.7 3.4 %residual.1 = (f32[96,1024]{1,0:T(8,128)}, f32[8,96,256]{2,1,0:T(8,128)}, f32[1]{0:T(128)}) custom-call(s32[4]{0:T(128)S(1)} %pad_add_fusion.info, f32[4,56,128]{2,1,0:T(8,128)S(1)} %pad_maximum_fusion.wide_ref, f32[12,56,128]{2,1,0:T(8,128)S(1)} %constant_dynamic-update-slice_fusion.5.rest_ref, f32[4,56,128]{2,1,0:T(8,128)S(1)} %collective-permute-done.27.wide_other, ...), custom_call_target="tpu_custom_call" | custom-call | tf_op jit(solution)/shard_map/residual/pallas_call | solution.py:394
  (66 shorter events, 14.7 us)
Async XLA Ops:
  3.1 9.8 %collective-permute-start.2 = (f32[24,1024]{1,0:T(8,128)S(1)}, f32[24,1024]{1,0:T(8,128)S(1)}, u32[]{:S(2)}, u32[]{:S(2)}) collective-permute-start(f32[24,1024]{1,0:T(8,128)S(1)} %get-tuple-element.37), channel_id=1, source_target_pairs={{0,8},{1,57},{8,16},{9,1},{16,24},{17,9},{24,32},{25,17},{32,40},{... | collective-permute-start | bytes 294920 | tf_op jit(solution)/shard_map/ppermute | solution.py:324
  5.1 10.0 %collective-permute-start.4 = (f32[24,1024]{1,0:T(8,128)S(1)}, f32[24,1024]{1,0:T(8,128)S(1)}, u32[]{:S(2)}, u32[]{:S(2)}) collective-permute-start(f32[24,1024]{1,0:T(8,128)S(1)} %get-tuple-element.38), channel_id=1, source_target_pairs={{0,16},{1,49},{8,24},{9,57},{16,32},{17,1},{24,40},{25,9},{32,48},... | collective-permute-start | bytes 294920 | tf_op jit(solution)/shard_map/ppermute | solution.py:324
  8.4 15.5 %collective-permute-start.1 = (f32[24,512]{1,0:T(8,128)S(1)}, f32[24,512]{1,0:T(8,128)S(1)}, u32[]{:S(2)}, u32[]{:S(2)}) collective-permute-start(f32[24,512]{1,0:T(8,128)S(1)} %get-tuple-element.36), channel_id=1, source_target_pairs={{0,32},{1,33},{8,40},{9,41},{16,48},{17,49},{24,56},{25,57},{32,0}... | collective-permute-start | bytes 147464 | tf_op jit(solution)/shard_map/ppermute | solution.py:324
  12.9 11.0 %collective-permute-start = (f32[24,1024]{1,0:T(8,128)S(1)}, f32[24,1024]{1,0:T(8,128)S(1)}, u32[]{:S(2)}, u32[]{:S(2)}) collective-permute-start(f32[24,1024]{1,0:T(8,128)S(1)} %get-tuple-element.35), channel_id=1, source_target_pairs={{0,24},{1,41},{8,32},{9,49},{16,40},{17,57},{24,48},{25,1},{32,56}... | collective-permute-start | bytes 294920 | tf_op jit(solution)/shard_map/ppermute | solution.py:324
  12.9 7.5 %collective-permute-start.3 = (f32[24,1024]{1,0:T(8,128)S(1)}, f32[24,1024]{1,0:T(8,128)S(1)}, u32[]{:S(2)}, u32[]{:S(2)}) collective-permute-start(f32[24,1024]{1,0:T(8,128)S(1)} %collective-permute-done.2.refs_0_), channel_id=1, source_target_pairs={{0,1},{1,0},{2,3},{3,2},{4,5},{5,4},{6,7},{7,6},{8,9},{9,8},{10,11... | collective-permute-start | bytes 294920 | tf_op jit(solution)/shard_map/ppermute | solution.py:309
  15.1 5.4 %collective-permute-start.5 = (f32[24,1024]{1,0:T(8,128)S(1)}, f32[24,1024]{1,0:T(8,128)S(1)}, u32[]{:S(2)}, u32[]{:S(2)}) collective-permute-start(f32[24,1024]{1,0:T(8,128)S(1)} %collective-permute-done.4.refs_1_), channel_id=1, source_target_pairs={{0,1},{1,0},{2,3},{3,2},{4,5},{5,4},{6,7},{7,6},{8,9},{9,8},{10,11... | collective-permute-start | bytes 294920 | tf_op jit(solution)/shard_map/ppermute | solution.py:309
  23.9 3.4 %collective-permute-start.6 = (f32[24,1024]{1,0:T(8,128)S(1)}, f32[24,1024]{1,0:T(8,128)S(1)}, u32[]{:S(2)}, u32[]{:S(2)}) collective-permute-start(f32[24,1024]{1,0:T(8,128)S(1)} %collective-permute-done.refs_0_), channel_id=1, source_target_pairs={{0,1},{1,0},{2,3},{3,2},{4,5},{5,4},{6,7},{7,6},{8,9},{9,8},{10,11... | collective-permute-start | bytes 294920 | tf_op jit(solution)/shard_map/ppermute | solution.py:309
  65.2 6.4 %collective-permute-start.9 = (f32[8,64,128]{2,1,0:T(8,128)S(1)}, f32[8,64,128]{2,1,0:T(8,128)S(1)}, u32[]{:S(2)}, u32[]{:S(2)}) collective-permute-start(f32[8,64,128]{2,1,0:T(8,128)S(1)} %all_to_all.11), channel_id=1, source_target_pairs={{0,192},{1,7},{2,194},{3,1},{4,196},{5,3},{6,198},{7,5},{64,0},{65... | collective-permute-start | bytes 786440 | tf_op jit(solution)/shard_map/ppermute | solution.py:305
  66.0 7.7 %collective-permute-start.8 = (f32[8,64,128]{2,1,0:T(8,128)S(1)}, f32[8,64,128]{2,1,0:T(8,128)S(1)}, u32[]{:S(2)}, u32[]{:S(2)}) collective-permute-start(f32[8,64,128]{2,1,0:T(8,128)S(1)} %all_to_all.11), channel_id=1, source_target_pairs={{0,64},{1,3},{2,66},{3,5},{4,68},{5,7},{6,70},{7,1},{64,128},{65,6... | collective-permute-start | bytes 786440 | tf_op jit(solution)/shard_map/ppermute | solution.py:305
  71.5 9.6 %collective-permute-start.11 = (f32[4,64,128]{2,1,0:T(8,128)S(1)}, f32[4,64,128]{2,1,0:T(8,128)S(1)}, u32[]{:S(2)}, u32[]{:S(2)}) collective-permute-start(f32[4,64,128]{2,1,0:T(8,128)S(1)} %slice.17), channel_id=1, source_target_pairs={{0,192},{1,7},{2,194},{3,1},{4,196},{5,3},{6,198},{7,5},{64,0},{65... | collective-permute-start | bytes 393224 | tf_op jit(solution)/shard_map/ppermute | solution.py:305
  73.7 7.5 %collective-permute-start.10 = (f32[4,64,128]{2,1,0:T(8,128)S(1)}, f32[4,64,128]{2,1,0:T(8,128)S(1)}, u32[]{:S(2)}, u32[]{:S(2)}) collective-permute-start(f32[4,64,128]{2,1,0:T(8,128)S(1)} %slice.16), channel_id=1, source_target_pairs={{0,64},{1,3},{2,66},{3,5},{4,68},{5,7},{6,70},{7,1},{64,128},{65,6... | collective-permute-start | bytes 393224 | tf_op jit(solution)/shard_map/ppermute | solution.py:305
  81.2 14.9 %collective-permute-start.15 = (f32[32,64,128]{2,1,0:T(8,128)S(1)}, f32[32,64,128]{2,1,0:T(8,128)S(1)}, u32[]{:S(2)}, u32[]{:S(2)}) collective-permute-start(f32[32,64,128]{2,1,0:T(8,128)S(1)} %constant_dynamic-update-slice_fusion.refs_0_), channel_id=1, source_target_pairs={{0,6},{1,193},{2,0},{3,195},{4,2},{5,197},{6,4},{7,199},{64,70},{6... | collective-permute-start | bytes 3145736 | tf_op jit(solution)/shard_map/ppermute | solution.py:305
  81.5 14.9 %collective-permute-start.13 = (f32[32,64,128]{2,1,0:T(8,128)S(1)}, f32[32,64,128]{2,1,0:T(8,128)S(1)}, u32[]{:S(2)}, u32[]{:S(2)}) collective-permute-start(f32[32,64,128]{2,1,0:T(8,128)S(1)} %constant_dynamic-update-slice_fusion.refs_0_), channel_id=1, source_target_pairs={{0,2},{1,65},{2,4},{3,67},{4,6},{5,69},{6,0},{7,71},{64,66},{65,12... | collective-permute-start | bytes 3145736 | tf_op jit(solution)/shard_map/ppermute | solution.py:305
  83.3 24.5 %collective-permute-start.12 = (f32[32,64,128]{2,1,0:T(8,128)S(1)}, f32[32,64,128]{2,1,0:T(8,128)S(1)}, u32[]{:S(2)}, u32[]{:S(2)}) collective-permute-start(f32[32,64,128]{2,1,0:T(8,128)S(1)} %constant_dynamic-update-slice_fusion.refs_0_), channel_id=1, source_target_pairs={{0,1},{1,0},{2,3},{3,2},{4,5},{5,4},{6,7},{7,6},{8,9},{9,8},{10,11... | collective-permute-start | bytes 3145736 | tf_op jit(solution)/shard_map/ppermute | solution.py:309
  96.1 9.3 %collective-permute-start.19 = (f32[16,64,128]{2,1,0:T(8,128)S(1)}, f32[16,64,128]{2,1,0:T(8,128)S(1)}, u32[]{:S(2)}, u32[]{:S(2)}) collective-permute-start(f32[16,64,128]{2,1,0:T(8,128)S(1)} %slice.19), channel_id=1, source_target_pairs={{0,6},{1,193},{2,0},{3,195},{4,2},{5,197},{6,4},{7,199},{64,70},{6... | collective-permute-start | bytes 1572872 | tf_op jit(solution)/shard_map/ppermute | solution.py:305
  96.5 10.6 %collective-permute-start.17 = (f32[16,64,128]{2,1,0:T(8,128)S(1)}, f32[16,64,128]{2,1,0:T(8,128)S(1)}, u32[]{:S(2)}, u32[]{:S(2)}) collective-permute-start(f32[16,64,128]{2,1,0:T(8,128)S(1)} %slice.18), channel_id=1, source_target_pairs={{0,2},{1,65},{2,4},{3,67},{4,6},{5,69},{6,0},{7,71},{64,66},{65,12... | collective-permute-start | bytes 1572872 | tf_op jit(solution)/shard_map/ppermute | solution.py:305
  98.4 9.5 %collective-permute-start.16 = (f32[32,64,128]{2,1,0:T(8,128)S(1)}, f32[32,64,128]{2,1,0:T(8,128)S(1)}, u32[]{:S(2)}, u32[]{:S(2)}) collective-permute-start(f32[32,64,128]{2,1,0:T(8,128)S(1)} %collective-permute-done.15.refs_4_), channel_id=1, source_target_pairs={{0,1},{1,0},{2,3},{3,2},{4,5},{5,4},{6,7},{7,6},{8,9},{9,8},{10,11... | collective-permute-start | bytes 3145736 | tf_op jit(solution)/shard_map/ppermute | solution.py:309
  98.4 10.7 %collective-permute-start.14 = (f32[32,64,128]{2,1,0:T(8,128)S(1)}, f32[32,64,128]{2,1,0:T(8,128)S(1)}, u32[]{:S(2)}, u32[]{:S(2)}) collective-permute-start(f32[32,64,128]{2,1,0:T(8,128)S(1)} %collective-permute-done.13.refs_2_), channel_id=1, source_target_pairs={{0,1},{1,0},{2,3},{3,2},{4,5},{5,4},{6,7},{7,6},{8,9},{9,8},{10,11... | collective-permute-start | bytes 3145736 | tf_op jit(solution)/shard_map/ppermute | solution.py:309
  136.6 5.5 %collective-permute-start.23 = (f32[56,128]{1,0:T(8,128)S(1)}, f32[56,128]{1,0:T(8,128)S(1)}, u32[]{:S(2)}, u32[]{:S(2)}) collective-permute-start(f32[56,128]{1,0:T(8,128)S(1)} %get-tuple-element.62), channel_id=1, source_target_pairs={{0,128},{1,5},{2,130},{3,7},{4,132},{5,1},{6,134},{7,3},{64,192},{... | collective-permute-start | bytes 86024 | tf_op jit(solution)/shard_map/ppermute | solution.py:305
  136.7 5.4 %collective-permute-start.22 = (f32[56,128]{1,0:T(8,128)S(1)}, f32[56,128]{1,0:T(8,128)S(1)}, u32[]{:S(2)}, u32[]{:S(2)}) collective-permute-start(f32[56,128]{1,0:T(8,128)S(1)} %get-tuple-element.62), channel_id=1, source_target_pairs={{0,192},{1,7},{2,194},{3,1},{4,196},{5,3},{6,198},{7,5},{64,0},{65... | collective-permute-start | bytes 86024 | tf_op jit(solution)/shard_map/ppermute | solution.py:305
  137.1 5.5 %collective-permute-start.21 = (f32[56,128]{1,0:T(8,128)S(1)}, f32[56,128]{1,0:T(8,128)S(1)}, u32[]{:S(2)}, u32[]{:S(2)}) collective-permute-start(f32[56,128]{1,0:T(8,128)S(1)} %get-tuple-element.62), channel_id=1, source_target_pairs={{0,64},{1,3},{2,66},{3,5},{4,68},{5,7},{6,70},{7,1},{64,128},{65,6... | collective-permute-start | bytes 86024 | tf_op jit(solution)/shard_map/ppermute | solution.py:305
  142.6 6.1 %collective-permute-start.24 = (f32[4,56,128]{2,1,0:T(8,128)S(1)}, f32[4,56,128]{2,1,0:T(8,128)S(1)}, u32[]{:S(2)}, u32[]{:S(2)}) collective-permute-start(f32[4,56,128]{2,1,0:T(8,128)S(1)} %pad_maximum_fusion.wide_ref), channel_id=1, source_target_pairs={{0,2},{1,65},{2,4},{3,67},{4,6},{5,69},{6,0},{7,71},{64,66},{65,12... | collective-permute-start | bytes 344072 | tf_op jit(solution)/shard_map/ppermute | solution.py:305
  143.4 9.4 %collective-permute-start.26 = (f32[4,56,128]{2,1,0:T(8,128)S(1)}, f32[4,56,128]{2,1,0:T(8,128)S(1)}, u32[]{:S(2)}, u32[]{:S(2)}) collective-permute-start(f32[4,56,128]{2,1,0:T(8,128)S(1)} %pad_maximum_fusion.wide_ref), channel_id=1, source_target_pairs={{0,4},{1,129},{2,6},{3,131},{4,0},{5,133},{6,2},{7,135},{64,68},{6... | collective-permute-start | bytes 344072 | tf_op jit(solution)/shard_map/ppermute | solution.py:305
  148.0 4.8 %collective-permute-start.25 = (f32[4,56,128]{2,1,0:T(8,128)S(1)}, f32[4,56,128]{2,1,0:T(8,128)S(1)}, u32[]{:S(2)}, u32[]{:S(2)}) collective-permute-start(f32[4,56,128]{2,1,0:T(8,128)S(1)} %pad_maximum_fusion.wide_ref), channel_id=1, source_target_pairs={{0,6},{1,193},{2,0},{3,195},{4,2},{5,197},{6,4},{7,199},{64,70},{6... | collective-permute-start | bytes 344072 | tf_op jit(solution)/shard_map/ppermute | solution.py:305
  (8 other events, 24.8 us)
